TPU v7x, 32 devices: a whole 2x2x4 slice. The times are simulated.
32 devices in a mesh: slab: 8 (over z, core), cross: 4 (over y, x).
Axes of the slice: x: 2, y: 2, z: 4, core: 2. Of those that a mesh axis runs over, the one named last changes fastest.
Arguments:
- forcing: float32 [2, 32, 256, 512], P(None, 'slab', 'cross'), may hold values from -6 to 6
- viscosity: float32 [32, 256, 512], P('slab', 'cross'), may hold values from 0.1 to 10
- owner_slot: int32 [512], replicated, may hold values from 0 to 511, each once
Outputs:
- velocity: float32 [2, 32, 256, 512], P(None, 'slab', 'cross')
- pressure: float32 [32, 512], P('slab', 'cross')
All inputs are finite; a program needn't handle non-finite values.
Results may differ from a plain program's by a relative error of at most 0.00013.
Values sent between devices are 32-bit elements; how exact they have to be, the bound alone decides.
A program may use at most 64 MiB of HBM per device.

v0:
```python
import jax
import jax.numpy as jnp
from jax import lax
from jax.sharding import PartitionSpec as P

OUTER = 2
DEGREE = 3


cheb_theta = 1.025
cheb_delta = 0.975


def with_halo(cells, sides, width):
    for axis, dim in sides:
        count = lax.axis_size(axis)
        ends = count - 1
        head = lax.slice_in_dim(cells, 0, width, axis=dim)
        tail = lax.slice_in_dim(cells, cells.shape[dim] - width, cells.shape[dim], axis=dim)
        cells = jnp.concatenate(
            [
                lax.ppermute(tail, axis, [(i, (i + 1) % count) for i in range(ends)]),
                cells,
                lax.ppermute(head, axis, [((i + 1) % count, i) for i in range(ends)]),
            ],
            axis=dim,
        )
    return cells


def passed_along(block, axis, distance):
    devices = range(lax.axis_size(axis))
    route = [(i - distance, i) for i in devices if i - distance in devices]
    return lax.ppermute(block, axis, route)


def face_parts(viscosity):
    rim = with_halo(viscosity, (("slab", 0), ("cross", 1)), 1)
    rim = jnp.pad(rim, ((0, 0), (0, 0), (1, 1)))
    centre = rim[1:-1, 1:-1, 1:-1]
    neighbours = [
        rim[2:, 1:-1, 1:-1],
        rim[:-2, 1:-1, 1:-1],
        rim[1:-1, 2:, 1:-1],
        rim[1:-1, :-2, 1:-1],
        rim[1:-1, 1:-1, 2:],
        rim[1:-1, 1:-1, :-2],
    ]
    faces = [0.5 * (centre + nb) for nb in neighbours]
    diag = faces[0] + faces[1] + faces[2] + faces[3] + faces[4] + faces[5]
    return (faces, diag)


def apply_op(field, faces):
    padded = with_halo(field, (("slab", 1), ("cross", 2)), 1)
    padded = jnp.pad(padded, ((0, 0), (0, 0), (0, 0), (1, 1)))
    neighbours = [
        padded[:, 2:, 1:-1, 1:-1],
        padded[:, :-2, 1:-1, 1:-1],
        padded[:, 1:-1, 2:, 1:-1],
        padded[:, 1:-1, :-2, 1:-1],
        padded[:, 1:-1, 1:-1, 2:],
        padded[:, 1:-1, 1:-1, :-2],
    ]
    result = jnp.zeros_like(field)
    for face, nb in zip(faces, neighbours):
        result = result + face[None] * (field - nb)
    return result


def velocity_solve(rhs, faces, diag):
    sigma = cheb_theta / cheb_delta
    solved = rhs / (cheb_theta * diag[None])
    change = solved
    rho_prev = 1.0 / sigma
    for step in range(DEGREE - 1):
        resid = rhs - apply_op(solved, faces)
        rho = 1.0 / (2.0 * sigma - rho_prev)
        change = rho * rho_prev * change + 2.0 * rho / cheb_delta * resid / diag[None]
        solved = solved + change
        rho_prev = rho
    return solved


def diverge(field, onehot):
    col_x = jnp.sum(field[0], axis=1)
    col_z = jnp.sum(field[1], axis=1)
    prior = passed_along(col_x[-1:], "slab", 1)
    below = jnp.concatenate([prior, col_x[:-1]], 0)
    behind = jnp.pad(col_z[:, :-1], ((0, 0), (1, 0)))
    local = col_x - below + col_z - behind
    ordered = jnp.dot(local, onehot, precision=lax.Precision.HIGHEST)
    return lax.psum(ordered, "cross")


def gradient(press, onehot, ny):
    column = jnp.dot(press, onehot.T, precision=lax.Precision.HIGHEST)
    after = passed_along(column[:1], "slab", -1)
    grad_x = column - jnp.concatenate([column[1:], after], 0)
    grad_z = column - jnp.pad(column[:, 1:], ((0, 0), (0, 1)))
    both = jnp.stack([grad_x, grad_z])[:, :, None, :]
    return jnp.broadcast_to(both, (2, column.shape[0], ny, column.shape[1]))


def total(value):
    return lax.psum(value, "slab")


def shards(forcing, viscosity, owner_slot):
    faces, diag = face_parts(viscosity)
    ny = viscosity.shape[1]
    depth = owner_slot.shape[0]
    onehot = (owner_slot[:, None] == jnp.arange(depth, dtype=jnp.int32)[None, :]).astype(
        jnp.float32
    )
    target = diverge(velocity_solve(forcing, faces, diag), onehot)
    pressure = jnp.zeros_like(target)
    resid = target
    dirn = target
    rr = total(jnp.sum(resid * resid))
    for step in range(OUTER):
        image = diverge(velocity_solve(gradient(dirn, onehot, ny), faces, diag), onehot)
        alpha = rr / total(jnp.sum(dirn * image))
        pressure = pressure + alpha * dirn
        if step + 1 < OUTER:
            resid = resid - alpha * image
            fresh = total(jnp.sum(resid * resid))
            dirn = resid + fresh / rr * dirn
            rr = fresh
    velocity = velocity_solve(forcing - gradient(pressure, onehot, ny), faces, diag)
    width = depth // lax.axis_size("cross")
    owned_cols = lax.dynamic_slice_in_dim(pressure, lax.axis_index("cross") * width, width, 1)
    return (velocity, owned_cols)


def solution(mesh):
    in_specs = (P(None, "slab", "cross", None), P("slab", "cross", None), P())
    out_specs = (P(None, "slab", "cross", None), P("slab", "cross"))
    return jax.shard_map(shards, mesh=mesh, in_specs=in_specs, out_specs=out_specs, check_vma=False)
```

profile of v0, /device:TPU:12, one launch (start us, length us, event | category | flops | bytes accessed | tf_op | source)
XLA Modules:
  0.0 310.1 jit_solution(14923868998203583419)
XLA Ops:
  1.7 1.9 collective-permute-start.1
  3.6 3.6 %collective-permute-start = (f32[1,64,512]{2,1,0:T(8,128)S(1)}, f32[1,64,512]{2,1,0:T(8,128)S(1)}, u32[]{:S(2)}, u32[]{:S(2)}) collective-permute-start(f32[1,64,512]{2,1,0:T(8,128)S(1)} %get-tuple-element.62), channel_id=1, source_target_pairs={{4,0},{8,4},{12,8},{16,12},{20,16},{24,20},{28,24},{5,1},{9,5},{13... | collective-permute-start | bytes 393224 | tf_op jit(solution)/shard_map/ppermute | solution.py:24
  9.8 3.3 %collective-permute-start.2 = (f32[6,1,512]{2,1,0:T(1,128)S(1)}, f32[6,1,512]{2,1,0:T(1,128)S(1)}, u32[]{:S(2)}, u32[]{:S(2)}) collective-permute-start(f32[6,1,512]{2,1,0:T(1,128)S(1)} %get-tuple-element.61), channel_id=1, source_target_pairs={{1,0},{2,1},{3,2},{5,4},{6,5},{7,6},{9,8},{10,9},{11,10},{13,12},{... | collective-permute-start | bytes 36872 | tf_op jit(solution)/shard_map/ppermute | solution.py:24
  13.2 2.5 collective-permute-start.3
  15.7 4.0 %collective-permute-done.3 = f32[6,1,512]{2,1,0:T(1,128)S(1)} collective-permute-done((f32[6,1,512]{2,1,0:T(1,128)S(1)}, f32[6,1,512]{2,1,0:T(1,128)S(1)}, u32[]{:S(2)}, u32[]{:S(2)}) %collective-permute-start.3) | collective-permute-done | bytes 12320 | tf_op jit(solution)/shard_map/ppermute | solution.py:22
  22.4 2.4 collective-permute-start.4
  24.8 2.0 collective-permute-start.5
  28.7 3.8 %collective-permute-done.5 = f32[2,1,64,512]{3,2,1,0:T(8,128)S(1)} collective-permute-done((f32[2,1,64,512]{3,2,1,0:T(8,128)S(1)}, f32[2,1,64,512]{3,2,1,0:T(8,128)S(1)}, u32[]{:S(2)}, u32[]{:S(2)}) %collective-permute-start.5) | collective-permute-done | bytes 262176 | tf_op jit(solution)/shard_map/ppermute | solution.py:22
  32.5 1.9 collective-permute-start.6
  34.5 3.9 %collective-permute-start.7 = (f32[2,6,1,512]{3,2,1,0:T(1,128)S(1)}, f32[2,6,1,512]{3,2,1,0:T(1,128)S(1)}, u32[]{:S(2)}, u32[]{:S(2)}) collective-permute-start(f32[2,6,1,512]{3,2,1,0:T(1,128)S(1)} %get-tuple-element.42), channel_id=1, source_target_pairs={{0,1},{1,2},{2,3},{4,5},{5,6},{6,7},{8,9},{9,10},{10,11},{12,13},{... | collective-permute-start | bytes 73736 | tf_op jit(solution)/shard_map/ppermute | solution.py:22
  38.4 2.7 collective-permute-done.7
  45.5 2.4 collective-permute-start.9
  49.4 3.8 %collective-permute-done.9 = f32[2,1,64,512]{3,2,1,0:T(8,128)S(1)} collective-permute-done((f32[2,1,64,512]{3,2,1,0:T(8,128)S(1)}, f32[2,1,64,512]{3,2,1,0:T(8,128)S(1)}, u32[]{:S(2)}, u32[]{:S(2)}) %collective-permute-start.9) | collective-permute-done | bytes 262176 | tf_op jit(solution)/shard_map/ppermute | solution.py:22
  55.2 3.9 %collective-permute-start.11 = (f32[2,6,1,512]{3,2,1,0:T(1,128)S(1)}, f32[2,6,1,512]{3,2,1,0:T(1,128)S(1)}, u32[]{:S(2)}, u32[]{:S(2)}) collective-permute-start(f32[2,6,1,512]{3,2,1,0:T(1,128)S(1)} %get-tuple-element.40), channel_id=1, source_target_pairs={{0,1},{1,2},{2,3},{4,5},{5,6},{6,7},{8,9},{9,10},{10,11},{12,13},{... | collective-permute-start | bytes 73736 | tf_op jit(solution)/shard_map/ppermute | solution.py:22
  59.1 2.7 collective-permute-done.11
  64.6 1.9 collective-permute-start.12
  66.5 3.0 collective-permute-done.12
  70.0 8.7 %psum.49 = f32[4,512]{1,0:T(4,128)S(1)} all-reduce(f32[4,512]{1,0:T(4,128)S(1)} %fusion.163), channel_id=1, replica_groups=mesh['slab'=8,'cross'=4] {'cross'}, use_global_device_ids=true, to_apply=%region_2.3 | all-reduce | flops 2048 | bytes 16384 | tf_op jit(solution)/shard_map/psum | solution.py:93
  79.3 1.9 collective-permute-start.13
  83.8 3.6 %collective-permute-start.14 = (f32[2,1,64,512]{3,2,1,0:T(8,128)S(1)}, f32[2,1,64,512]{3,2,1,0:T(8,128)S(1)}, u32[]{:S(2)}, u32[]{:S(2)}) collective-permute-start(f32[2,1,64,512]{3,2,1,0:T(8,128)S(1)} %get-tuple-element.55), channel_id=1, source_target_pairs={{4,0},{8,4},{12,8},{16,12},{20,16},{24,20},{28,24},{5,1},{9,5},{13... | collective-permute-start | bytes 786440 | tf_op jit(solution)/shard_map/ppermute | solution.py:24
  89.3 1.9 collective-permute-done.14
  91.3 3.8 %collective-permute-done.15 = f32[2,1,64,512]{3,2,1,0:T(8,128)S(1)} collective-permute-done((f32[2,1,64,512]{3,2,1,0:T(8,128)S(1)}, f32[2,1,64,512]{3,2,1,0:T(8,128)S(1)}, u32[]{:S(2)}, u32[]{:S(2)}) %collective-permute-start.15) | collective-permute-done | bytes 262176 | tf_op jit(solution)/shard_map/ppermute | solution.py:22
  95.2 3.0 collective-permute-start.16
  98.1 3.0 collective-permute-start.17
  101.2 3.6 %collective-permute-done.17 = f32[2,6,1,512]{3,2,1,0:T(1,128)S(1)} collective-permute-done((f32[2,6,1,512]{3,2,1,0:T(1,128)S(1)}, f32[2,6,1,512]{3,2,1,0:T(1,128)S(1)}, u32[]{:S(2)}, u32[]{:S(2)}) %collective-permute-start.17) | collective-permute-done | bytes 24608 | tf_op jit(solution)/shard_map/ppermute | solution.py:22
  107.2 1.9 collective-permute-start.18
  109.2 2.4 collective-permute-start.19
  113.0 3.8 %collective-permute-done.19 = f32[2,1,64,512]{3,2,1,0:T(8,128)S(1)} collective-permute-done((f32[2,1,64,512]{3,2,1,0:T(8,128)S(1)}, f32[2,1,64,512]{3,2,1,0:T(8,128)S(1)}, u32[]{:S(2)}, u32[]{:S(2)}) %collective-permute-start.19) | collective-permute-done | bytes 262176 | tf_op jit(solution)/shard_map/ppermute | solution.py:22
  116.9 3.0 collective-permute-start.20
  119.9 2.8 collective-permute-start.21
  122.8 3.8 %collective-permute-done.21 = f32[2,6,1,512]{3,2,1,0:T(1,128)S(1)} collective-permute-done((f32[2,6,1,512]{3,2,1,0:T(1,128)S(1)}, f32[2,6,1,512]{3,2,1,0:T(1,128)S(1)}, u32[]{:S(2)}, u32[]{:S(2)}) %collective-permute-start.21) | collective-permute-done | bytes 24608 | tf_op jit(solution)/shard_map/ppermute | solution.py:22
  131.1 3.0 collective-permute-done.22
  134.6 7.7 %psum.51 = f32[4,512]{1,0:T(4,128)S(1)} all-reduce(f32[4,512]{1,0:T(4,128)S(1)} %fusion.161), channel_id=1, replica_groups=mesh['slab'=8,'cross'=4] {'cross'}, use_global_device_ids=true, to_apply=%region_7.8 | all-reduce | flops 2048 | bytes 16384 | tf_op jit(solution)/shard_map/psum | solution.py:93
  143.0 10.6 %all-reduce.15 = (f32[]{:T(128)}, f32[]{:T(128)}) all-reduce(f32[]{:T(128)} %get-tuple-element.9, f32[]{:T(128)} %get-tuple-element.8), channel_id=1, replica_groups=mesh['slab'=8,'cross'=4] {'slab'}, use_global_device_ids=true, to_apply=%region_4.5 | all-reduce | flops 2 | bytes 16 | tf_op jit(solution)/shard_map/psum | solution.py:106
  155.5 14.3 %psum.53 = f32[]{:T(128)} all-reduce(f32[]{:T(128)} %multiply_reduce_fusion.1), channel_id=1, replica_groups=mesh['slab'=8,'cross'=4] {'slab'}, use_global_device_ids=true, to_apply=%region_11.12 | all-reduce | flops 1 | bytes 8 | tf_op jit(solution)/shard_map/psum | solution.py:106
  171.7 5.0 %collective-permute-start.23 = (f32[1,512]{1,0:T(1,128)S(1)}, f32[1,512]{1,0:T(1,128)S(1)}, u32[]{:S(2)}, u32[]{:S(2)}) collective-permute-start(f32[1,512]{1,0:T(1,128)S(1)} %slice.583), channel_id=1, source_target_pairs={{4,0},{8,4},{12,8},{16,12},{20,16},{24,20},{28,24},{5,1},{9,5},{13... | collective-permute-start | bytes 6152 | tf_op jit(solution)/shard_map/ppermute | solution.py:34
  179.2 3.6 %collective-permute-start.24 = (f32[2,1,64,512]{3,2,1,0:T(8,128)S(1)}, f32[2,1,64,512]{3,2,1,0:T(8,128)S(1)}, u32[]{:S(2)}, u32[]{:S(2)}) collective-permute-start(f32[2,1,64,512]{3,2,1,0:T(8,128)S(1)} %get-tuple-element.51), channel_id=1, source_target_pairs={{4,0},{8,4},{12,8},{16,12},{20,16},{24,20},{28,24},{5,1},{9,5},{13... | collective-permute-start | bytes 786440 | tf_op jit(solution)/shard_map/ppermute | solution.py:24
  184.8 1.9 collective-permute-done.24
  186.7 3.8 %collective-permute-done.25 = f32[2,1,64,512]{3,2,1,0:T(8,128)S(1)} collective-permute-done((f32[2,1,64,512]{3,2,1,0:T(8,128)S(1)}, f32[2,1,64,512]{3,2,1,0:T(8,128)S(1)}, u32[]{:S(2)}, u32[]{:S(2)}) %collective-permute-start.25) | collective-permute-done | bytes 262176 | tf_op jit(solution)/shard_map/ppermute | solution.py:22
  190.6 4.1 %collective-permute-start.26 = (f32[2,6,1,512]{3,2,1,0:T(1,128)S(1)}, f32[2,6,1,512]{3,2,1,0:T(1,128)S(1)}, u32[]{:S(2)}, u32[]{:S(2)}) collective-permute-start(f32[2,6,1,512]{3,2,1,0:T(1,128)S(1)} %get-tuple-element.35), channel_id=1, source_target_pairs={{1,0},{2,1},{3,2},{5,4},{6,5},{7,6},{9,8},{10,9},{11,10},{13,12},{... | collective-permute-start | bytes 73736 | tf_op jit(solution)/shard_map/ppermute | solution.py:24
  196.6 4.7 %collective-permute-done.27 = f32[2,6,1,512]{3,2,1,0:T(1,128)S(1)} collective-permute-done((f32[2,6,1,512]{3,2,1,0:T(1,128)S(1)}, f32[2,6,1,512]{3,2,1,0:T(1,128)S(1)}, u32[]{:S(2)}, u32[]{:S(2)}) %collective-permute-start.27) | collective-permute-done | bytes 24608 | tf_op jit(solution)/shard_map/ppermute | solution.py:22
  203.8 1.9 collective-permute-start.28
  205.7 2.4 collective-permute-start.29
  209.6 3.8 %collective-permute-done.29 = f32[2,1,64,512]{3,2,1,0:T(8,128)S(1)} collective-permute-done((f32[2,1,64,512]{3,2,1,0:T(8,128)S(1)}, f32[2,1,64,512]{3,2,1,0:T(8,128)S(1)}, u32[]{:S(2)}, u32[]{:S(2)}) %collective-permute-start.29) | collective-permute-done | bytes 262176 | tf_op jit(solution)/shard_map/ppermute | solution.py:22
  213.4 2.0 collective-permute-start.30
  215.5 3.8 %collective-permute-start.31 = (f32[2,6,1,512]{3,2,1,0:T(1,128)S(1)}, f32[2,6,1,512]{3,2,1,0:T(1,128)S(1)}, u32[]{:S(2)}, u32[]{:S(2)}) collective-permute-start(f32[2,6,1,512]{3,2,1,0:T(1,128)S(1)} %get-tuple-element.32), channel_id=1, source_target_pairs={{0,1},{1,2},{2,3},{4,5},{5,6},{6,7},{8,9},{9,10},{10,11},{12,13},{... | collective-permute-start | bytes 73736 | tf_op jit(solution)/shard_map/ppermute | solution.py:22
  219.3 2.8 collective-permute-done.31
  226.7 3.0 collective-permute-done.32
  230.1 8.6 %psum.54 = f32[4,512]{1,0:T(4,128)S(1)} all-reduce(f32[4,512]{1,0:T(4,128)S(1)} %fusion.159), channel_id=1, replica_groups=mesh['slab'=8,'cross'=4] {'cross'}, use_global_device_ids=true, to_apply=%region_14.15 | all-reduce | flops 2048 | bytes 16384 | tf_op jit(solution)/shard_map/psum | solution.py:93
  239.4 11.2 %psum.55 = f32[]{:T(128)} all-reduce(f32[]{:T(128)} %multiply_reduce_fusion), channel_id=1, replica_groups=mesh['slab'=8,'cross'=4] {'slab'}, use_global_device_ids=true, to_apply=%region_16.17 | all-reduce | flops 1 | bytes 8 | tf_op jit(solution)/shard_map/psum | solution.py:106
  252.6 2.4 collective-permute-start.33
  257.9 3.6 %collective-permute-start.34 = (f32[2,1,64,512]{3,2,1,0:T(8,128)S(1)}, f32[2,1,64,512]{3,2,1,0:T(8,128)S(1)}, u32[]{:S(2)}, u32[]{:S(2)}) collective-permute-start(f32[2,1,64,512]{3,2,1,0:T(8,128)S(1)} %get-tuple-element.47), channel_id=1, source_target_pairs={{4,0},{8,4},{12,8},{16,12},{20,16},{24,20},{28,24},{5,1},{9,5},{13... | collective-permute-start | bytes 786440 | tf_op jit(solution)/shard_map/ppermute | solution.py:24
  263.5 1.9 collective-permute-done.34
  265.4 3.8 %collective-permute-done.35 = f32[2,1,64,512]{3,2,1,0:T(8,128)S(1)} collective-permute-done((f32[2,1,64,512]{3,2,1,0:T(8,128)S(1)}, f32[2,1,64,512]{3,2,1,0:T(8,128)S(1)}, u32[]{:S(2)}, u32[]{:S(2)}) %collective-permute-start.35) | collective-permute-done | bytes 262176 | tf_op jit(solution)/shard_map/ppermute | solution.py:22
  269.3 3.0 collective-permute-start.36
  272.3 2.9 collective-permute-start.37
  275.3 3.7 %collective-permute-done.37 = f32[2,6,1,512]{3,2,1,0:T(1,128)S(1)} collective-permute-done((f32[2,6,1,512]{3,2,1,0:T(1,128)S(1)}, f32[2,6,1,512]{3,2,1,0:T(1,128)S(1)}, u32[]{:S(2)}, u32[]{:S(2)}) %collective-permute-start.37) | collective-permute-done | bytes 24608 | tf_op jit(solution)/shard_map/ppermute | solution.py:22
  279.8 2.5 fusion.210
  286.0 2.4 collective-permute-start.39
  290.2 3.8 %collective-permute-done.39 = f32[2,1,64,512]{3,2,1,0:T(8,128)} collective-permute-done((f32[2,1,64,512]{3,2,1,0:T(8,128)}, f32[2,1,64,512]{3,2,1,0:T(8,128)}, u32[]{:S(2)}, u32[]{:S(2)}) %collective-permute-start.39) | collective-permute-done | bytes 262176 | tf_op jit(solution)/shard_map/ppermute | solution.py:22
  295.1 3.1 collective-permute-start.40
  298.1 2.9 collective-permute-start.41
  301.7 3.1 %collective-permute-done.41 = f32[2,6,1,512]{3,2,1,0:T(1,128)S(1)} collective-permute-done((f32[2,6,1,512]{3,2,1,0:T(1,128)S(1)}, f32[2,6,1,512]{3,2,1,0:T(1,128)S(1)}, u32[]{:S(2)}, u32[]{:S(2)}) %collective-permute-start.41) | collective-permute-done | bytes 24608 | tf_op jit(solution)/shard_map/ppermute | solution.py:22
  306.6 3.5 %fusion.8 = f32[2,4,64,512]{3,2,1,0:T(8,128)} fusion(f32[2,4,64,512]{3,2,1,0:T(8,128)S(1)} %copy-done.12, f32[2,6,66,514]{3,2,1,0:T(8,128)S(1)} %select_maximum_fusion, f32[2,6,1,512]{3,2,1,0:T(1,128)S(1)} %collective-permute-done.41, f32[2,1,64,512]{3,2,1,0:T(8,128)S(1)} %collective-permute-done.38, f32[2,1,64,512]{3,2,1,0:T(8,128)} %collective-permute-done.39, ...), kind=kLoop, calls=%fused_computation.47 | loop fusion | flops 8388608 | bytes 10551296 | tf_op jit(solution)/shard_map/add | solution.py:80
  (134 shorter events, 66.5 us)
Async XLA Ops:
  0.6 19.5 %copy-start.14 = (f32[4,64,512]{2,1,0:T(8,128)S(1)}, f32[4,64,512]{2,1,0:T(8,128)}, u32[]{:S(2)}) copy-start(f32[4,64,512]{2,1,0:T(8,128)} %param.4) | copy-start | bytes 1572868
  1.7 6.3 %collective-permute-start.1 = (f32[1,64,512]{2,1,0:T(8,128)S(1)}, f32[1,64,512]{2,1,0:T(8,128)S(1)}, u32[]{:S(2)}, u32[]{:S(2)}) collective-permute-start(f32[1,64,512]{2,1,0:T(8,128)S(1)} %get-tuple-element.63), channel_id=1, source_target_pairs={{0,4},{4,8},{8,12},{12,16},{16,20},{20,24},{24,28},{1,5},{5,9},{9,... | collective-permute-start | bytes 393224 | tf_op jit(solution)/shard_map/ppermute | solution.py:22
  3.6 6.1 %collective-permute-start = (f32[1,64,512]{2,1,0:T(8,128)S(1)}, f32[1,64,512]{2,1,0:T(8,128)S(1)}, u32[]{:S(2)}, u32[]{:S(2)}) collective-permute-start(f32[1,64,512]{2,1,0:T(8,128)S(1)} %get-tuple-element.62), channel_id=1, source_target_pairs={{4,0},{8,4},{12,8},{16,12},{20,16},{24,20},{28,24},{5,1},{9,5},{13... | collective-permute-start | bytes 393224 | tf_op jit(solution)/shard_map/ppermute | solution.py:24
  9.8 5.9 %collective-permute-start.2 = (f32[6,1,512]{2,1,0:T(1,128)S(1)}, f32[6,1,512]{2,1,0:T(1,128)S(1)}, u32[]{:S(2)}, u32[]{:S(2)}) collective-permute-start(f32[6,1,512]{2,1,0:T(1,128)S(1)} %get-tuple-element.61), channel_id=1, source_target_pairs={{1,0},{2,1},{3,2},{5,4},{6,5},{7,6},{9,8},{10,9},{11,10},{13,12},{... | collective-permute-start | bytes 36872 | tf_op jit(solution)/shard_map/ppermute | solution.py:24
  13.2 6.5 %collective-permute-start.3 = (f32[6,1,512]{2,1,0:T(1,128)S(1)}, f32[6,1,512]{2,1,0:T(1,128)S(1)}, u32[]{:S(2)}, u32[]{:S(2)}) collective-permute-start(f32[6,1,512]{2,1,0:T(1,128)S(1)} %get-tuple-element.60), channel_id=1, source_target_pairs={{0,1},{1,2},{2,3},{4,5},{5,6},{6,7},{8,9},{9,10},{10,11},{12,13},{... | collective-permute-start | bytes 36872 | tf_op jit(solution)/shard_map/ppermute | solution.py:22
  20.8 41.9 %copy-start = (f32[4,64,512]{2,1,0:T(8,128)}, f32[4,64,512]{2,1,0:T(8,128)S(1)}, u32[]{:S(2)}) copy-start(f32[4,64,512]{2,1,0:T(8,128)S(1)} %get-tuple-element.26) | copy-start | bytes 1572868
  20.8 1.4 copy-start.5
  22.2 10.3 %copy-start.8 = (f32[4,64,512]{2,1,0:T(8,128)}, f32[4,64,512]{2,1,0:T(8,128)S(1)}, u32[]{:S(2)}) copy-start(f32[4,64,512]{2,1,0:T(8,128)S(1)} %fusion.180) | copy-start | bytes 1572868
  22.4 6.2 %collective-permute-start.4 = (f32[2,1,64,512]{3,2,1,0:T(8,128)S(1)}, f32[2,1,64,512]{3,2,1,0:T(8,128)S(1)}, u32[]{:S(2)}, u32[]{:S(2)}) collective-permute-start(f32[2,1,64,512]{3,2,1,0:T(8,128)S(1)} %get-tuple-element.59), channel_id=1, source_target_pairs={{4,0},{8,4},{12,8},{16,12},{20,16},{24,20},{28,24},{5,1},{9,5},{13... | collective-permute-start | bytes 786440 | tf_op jit(solution)/shard_map/ppermute | solution.py:24
  24.8 7.7 %collective-permute-start.5 = (f32[2,1,64,512]{3,2,1,0:T(8,128)S(1)}, f32[2,1,64,512]{3,2,1,0:T(8,128)S(1)}, u32[]{:S(2)}, u32[]{:S(2)}) collective-permute-start(f32[2,1,64,512]{3,2,1,0:T(8,128)S(1)} %get-tuple-element.58), channel_id=1, source_target_pairs={{0,4},{4,8},{8,12},{12,16},{16,20},{20,24},{24,28},{1,5},{5,9},{9,... | collective-permute-start | bytes 786440 | tf_op jit(solution)/shard_map/ppermute | solution.py:22
  32.5 5.9 %collective-permute-start.6 = (f32[2,6,1,512]{3,2,1,0:T(1,128)S(1)}, f32[2,6,1,512]{3,2,1,0:T(1,128)S(1)}, u32[]{:S(2)}, u32[]{:S(2)}) collective-permute-start(f32[2,6,1,512]{3,2,1,0:T(1,128)S(1)} %get-tuple-element.43), channel_id=1, source_target_pairs={{1,0},{2,1},{3,2},{5,4},{6,5},{7,6},{9,8},{10,9},{11,10},{13,12},{... | collective-permute-start | bytes 73736 | tf_op jit(solution)/shard_map/ppermute | solution.py:24
  34.5 6.6 %collective-permute-start.7 = (f32[2,6,1,512]{3,2,1,0:T(1,128)S(1)}, f32[2,6,1,512]{3,2,1,0:T(1,128)S(1)}, u32[]{:S(2)}, u32[]{:S(2)}) collective-permute-start(f32[2,6,1,512]{3,2,1,0:T(1,128)S(1)} %get-tuple-element.42), channel_id=1, source_target_pairs={{0,1},{1,2},{2,3},{4,5},{5,6},{6,7},{8,9},{9,10},{10,11},{12,13},{... | collective-permute-start | bytes 73736 | tf_op jit(solution)/shard_map/ppermute | solution.py:22
  43.6 5.8 %collective-permute-start.8 = (f32[2,1,64,512]{3,2,1,0:T(8,128)S(1)}, f32[2,1,64,512]{3,2,1,0:T(8,128)S(1)}, u32[]{:S(2)}, u32[]{:S(2)}) collective-permute-start(f32[2,1,64,512]{3,2,1,0:T(8,128)S(1)} %get-tuple-element.57), channel_id=1, source_target_pairs={{4,0},{8,4},{12,8},{16,12},{20,16},{24,20},{28,24},{5,1},{9,5},{13... | collective-permute-start | bytes 786440 | tf_op jit(solution)/shard_map/ppermute | solution.py:24
  45.5 7.7 %collective-permute-start.9 = (f32[2,1,64,512]{3,2,1,0:T(8,128)S(1)}, f32[2,1,64,512]{3,2,1,0:T(8,128)S(1)}, u32[]{:S(2)}, u32[]{:S(2)}) collective-permute-start(f32[2,1,64,512]{3,2,1,0:T(8,128)S(1)} %get-tuple-element.56), channel_id=1, source_target_pairs={{0,4},{4,8},{8,12},{12,16},{16,20},{20,24},{24,28},{1,5},{5,9},{9,... | collective-permute-start | bytes 786440 | tf_op jit(solution)/shard_map/ppermute | solution.py:22
  53.3 5.9 %collective-permute-start.10 = (f32[2,6,1,512]{3,2,1,0:T(1,128)S(1)}, f32[2,6,1,512]{3,2,1,0:T(1,128)S(1)}, u32[]{:S(2)}, u32[]{:S(2)}) collective-permute-start(f32[2,6,1,512]{3,2,1,0:T(1,128)S(1)} %get-tuple-element.41), channel_id=1, source_target_pairs={{1,0},{2,1},{3,2},{5,4},{6,5},{7,6},{9,8},{10,9},{11,10},{13,12},{... | collective-permute-start | bytes 73736 | tf_op jit(solution)/shard_map/ppermute | solution.py:24
  55.2 6.6 %collective-permute-start.11 = (f32[2,6,1,512]{3,2,1,0:T(1,128)S(1)}, f32[2,6,1,512]{3,2,1,0:T(1,128)S(1)}, u32[]{:S(2)}, u32[]{:S(2)}) collective-permute-start(f32[2,6,1,512]{3,2,1,0:T(1,128)S(1)} %get-tuple-element.40), channel_id=1, source_target_pairs={{0,1},{1,2},{2,3},{4,5},{5,6},{6,7},{8,9},{9,10},{10,11},{12,13},{... | collective-permute-start | bytes 73736 | tf_op jit(solution)/shard_map/ppermute | solution.py:22
  62.7 6.8 %copy-start.15 = (s32[512]{0:T(512)S(1)}, s32[512]{0:T(512)}, u32[]{:S(2)}) copy-start(s32[512]{0:T(512)} %param.5) | copy-start | bytes 6148
  64.6 4.9 %collective-permute-start.12 = (f32[1,512]{1,0:T(1,128)S(1)}, f32[1,512]{1,0:T(1,128)S(1)}, u32[]{:S(2)}, u32[]{:S(2)}) collective-permute-start(f32[1,512]{1,0:T(1,128)S(1)} %slice.562), channel_id=1, source_target_pairs={{0,4},{4,8},{8,12},{12,16},{16,20},{20,24},{24,28},{1,5},{5,9},{9,... | collective-permute-start | bytes 6152 | tf_op jit(solution)/shard_map/ppermute | solution.py:34
  79.3 3.2 %collective-permute-start.13 = (f32[1,512]{1,0:T(1,128)S(1)}, f32[1,512]{1,0:T(1,128)S(1)}, u32[]{:S(2)}, u32[]{:S(2)}) collective-permute-start(f32[1,512]{1,0:T(1,128)S(1)} %slice.567), channel_id=1, source_target_pairs={{4,0},{8,4},{12,8},{16,12},{20,16},{24,20},{28,24},{5,1},{9,5},{13... | collective-permute-start | bytes 6152 | tf_op jit(solution)/shard_map/ppermute | solution.py:34
  83.8 7.5 %collective-permute-start.14 = (f32[2,1,64,512]{3,2,1,0:T(8,128)S(1)}, f32[2,1,64,512]{3,2,1,0:T(8,128)S(1)}, u32[]{:S(2)}, u32[]{:S(2)}) collective-permute-start(f32[2,1,64,512]{3,2,1,0:T(8,128)S(1)} %get-tuple-element.55), channel_id=1, source_target_pairs={{4,0},{8,4},{12,8},{16,12},{20,16},{24,20},{28,24},{5,1},{9,5},{13... | collective-permute-start | bytes 786440 | tf_op jit(solution)/shard_map/ppermute | solution.py:24
  87.4 7.7 %collective-permute-start.15 = (f32[2,1,64,512]{3,2,1,0:T(8,128)S(1)}, f32[2,1,64,512]{3,2,1,0:T(8,128)S(1)}, u32[]{:S(2)}, u32[]{:S(2)}) collective-permute-start(f32[2,1,64,512]{3,2,1,0:T(8,128)S(1)} %get-tuple-element.54), channel_id=1, source_target_pairs={{0,4},{4,8},{8,12},{12,16},{16,20},{20,24},{24,28},{1,5},{5,9},{9,... | collective-permute-start | bytes 786440 | tf_op jit(solution)/shard_map/ppermute | solution.py:22
  95.1 10.5 %copy-start.1 = (f32[4,64,512]{2,1,0:T(8,128)S(1)}, f32[4,64,512]{2,1,0:T(8,128)}, u32[]{:S(2)}) copy-start(f32[4,64,512]{2,1,0:T(8,128)} %copy-done) | copy-start | bytes 1572868
  95.2 10.5 %copy-start.9 = (f32[4,64,512]{2,1,0:T(8,128)S(1)}, f32[4,64,512]{2,1,0:T(8,128)}, u32[]{:S(2)}) copy-start(f32[4,64,512]{2,1,0:T(8,128)} %copy-done.8) | copy-start | bytes 1572868
  95.2 6.0 %collective-permute-start.16 = (f32[2,6,1,512]{3,2,1,0:T(1,128)S(1)}, f32[2,6,1,512]{3,2,1,0:T(1,128)S(1)}, u32[]{:S(2)}, u32[]{:S(2)}) collective-permute-start(f32[2,6,1,512]{3,2,1,0:T(1,128)S(1)} %get-tuple-element.39), channel_id=1, source_target_pairs={{1,0},{2,1},{3,2},{5,4},{6,5},{7,6},{9,8},{10,9},{11,10},{13,12},{... | collective-permute-start | bytes 73736 | tf_op jit(solution)/shard_map/ppermute | solution.py:24
  98.1 6.6 %collective-permute-start.17 = (f32[2,6,1,512]{3,2,1,0:T(1,128)S(1)}, f32[2,6,1,512]{3,2,1,0:T(1,128)S(1)}, u32[]{:S(2)}, u32[]{:S(2)}) collective-permute-start(f32[2,6,1,512]{3,2,1,0:T(1,128)S(1)} %get-tuple-element.38), channel_id=1, source_target_pairs={{0,1},{1,2},{2,3},{4,5},{5,6},{6,7},{8,9},{9,10},{10,11},{12,13},{... | collective-permute-start | bytes 73736 | tf_op jit(solution)/shard_map/ppermute | solution.py:22
  107.2 5.8 %collective-permute-start.18 = (f32[2,1,64,512]{3,2,1,0:T(8,128)S(1)}, f32[2,1,64,512]{3,2,1,0:T(8,128)S(1)}, u32[]{:S(2)}, u32[]{:S(2)}) collective-permute-start(f32[2,1,64,512]{3,2,1,0:T(8,128)S(1)} %get-tuple-element.53), channel_id=1, source_target_pairs={{4,0},{8,4},{12,8},{16,12},{20,16},{24,20},{28,24},{5,1},{9,5},{13... | collective-permute-start | bytes 786440 | tf_op jit(solution)/shard_map/ppermute | solution.py:24
  109.2 7.7 %collective-permute-start.19 = (f32[2,1,64,512]{3,2,1,0:T(8,128)S(1)}, f32[2,1,64,512]{3,2,1,0:T(8,128)S(1)}, u32[]{:S(2)}, u32[]{:S(2)}) collective-permute-start(f32[2,1,64,512]{3,2,1,0:T(8,128)S(1)} %get-tuple-element.52), channel_id=1, source_target_pairs={{0,4},{4,8},{8,12},{12,16},{16,20},{20,24},{24,28},{1,5},{5,9},{9,... | collective-permute-start | bytes 786440 | tf_op jit(solution)/shard_map/ppermute | solution.py:22
  116.9 5.9 %collective-permute-start.20 = (f32[2,6,1,512]{3,2,1,0:T(1,128)S(1)}, f32[2,6,1,512]{3,2,1,0:T(1,128)S(1)}, u32[]{:S(2)}, u32[]{:S(2)}) collective-permute-start(f32[2,6,1,512]{3,2,1,0:T(1,128)S(1)} %get-tuple-element.37), channel_id=1, source_target_pairs={{1,0},{2,1},{3,2},{5,4},{6,5},{7,6},{9,8},{10,9},{11,10},{13,12},{... | collective-permute-start | bytes 73736 | tf_op jit(solution)/shard_map/ppermute | solution.py:24
  119.9 6.6 %collective-permute-start.21 = (f32[2,6,1,512]{3,2,1,0:T(1,128)S(1)}, f32[2,6,1,512]{3,2,1,0:T(1,128)S(1)}, u32[]{:S(2)}, u32[]{:S(2)}) collective-permute-start(f32[2,6,1,512]{3,2,1,0:T(1,128)S(1)} %get-tuple-element.36), channel_id=1, source_target_pairs={{0,1},{1,2},{2,3},{4,5},{5,6},{6,7},{8,9},{9,10},{10,11},{12,13},{... | collective-permute-start | bytes 73736 | tf_op jit(solution)/shard_map/ppermute | solution.py:22
  129.2 4.9 %collective-permute-start.22 = (f32[1,512]{1,0:T(1,128)S(1)}, f32[1,512]{1,0:T(1,128)S(1)}, u32[]{:S(2)}, u32[]{:S(2)}) collective-permute-start(f32[1,512]{1,0:T(1,128)S(1)} %slice.578), channel_id=1, source_target_pairs={{0,4},{4,8},{8,12},{12,16},{16,20},{20,24},{24,28},{1,5},{5,9},{9,... | collective-permute-start | bytes 6152 | tf_op jit(solution)/shard_map/ppermute | solution.py:34
  171.7 6.3 %collective-permute-start.23 = (f32[1,512]{1,0:T(1,128)S(1)}, f32[1,512]{1,0:T(1,128)S(1)}, u32[]{:S(2)}, u32[]{:S(2)}) collective-permute-start(f32[1,512]{1,0:T(1,128)S(1)} %slice.583), channel_id=1, source_target_pairs={{4,0},{8,4},{12,8},{16,12},{20,16},{24,20},{28,24},{5,1},{9,5},{13... | collective-permute-start | bytes 6152 | tf_op jit(solution)/shard_map/ppermute | solution.py:34
  179.2 7.5 %collective-permute-start.24 = (f32[2,1,64,512]{3,2,1,0:T(8,128)S(1)}, f32[2,1,64,512]{3,2,1,0:T(8,128)S(1)}, u32[]{:S(2)}, u32[]{:S(2)}) collective-permute-start(f32[2,1,64,512]{3,2,1,0:T(8,128)S(1)} %get-tuple-element.51), channel_id=1, source_target_pairs={{4,0},{8,4},{12,8},{16,12},{20,16},{24,20},{28,24},{5,1},{9,5},{13... | collective-permute-start | bytes 786440 | tf_op jit(solution)/shard_map/ppermute | solution.py:24
  182.9 7.7 %collective-permute-start.25 = (f32[2,1,64,512]{3,2,1,0:T(8,128)S(1)}, f32[2,1,64,512]{3,2,1,0:T(8,128)S(1)}, u32[]{:S(2)}, u32[]{:S(2)}) collective-permute-start(f32[2,1,64,512]{3,2,1,0:T(8,128)S(1)} %get-tuple-element.50), channel_id=1, source_target_pairs={{0,4},{4,8},{8,12},{12,16},{16,20},{20,24},{24,28},{1,5},{5,9},{9,... | collective-permute-start | bytes 786440 | tf_op jit(solution)/shard_map/ppermute | solution.py:22
  190.6 11.6 %copy-start.2 = (f32[4,64,512]{2,1,0:T(8,128)S(1)}, f32[4,64,512]{2,1,0:T(8,128)}, u32[]{:S(2)}) copy-start(f32[4,64,512]{2,1,0:T(8,128)} %copy-done) | copy-start | bytes 1572868
  190.6 11.6 %copy-start.10 = (f32[4,64,512]{2,1,0:T(8,128)S(1)}, f32[4,64,512]{2,1,0:T(8,128)}, u32[]{:S(2)}) copy-start(f32[4,64,512]{2,1,0:T(8,128)} %copy-done.8) | copy-start | bytes 1572868
  190.6 6.0 %collective-permute-start.26 = (f32[2,6,1,512]{3,2,1,0:T(1,128)S(1)}, f32[2,6,1,512]{3,2,1,0:T(1,128)S(1)}, u32[]{:S(2)}, u32[]{:S(2)}) collective-permute-start(f32[2,6,1,512]{3,2,1,0:T(1,128)S(1)} %get-tuple-element.35), channel_id=1, source_target_pairs={{1,0},{2,1},{3,2},{5,4},{6,5},{7,6},{9,8},{10,9},{11,10},{13,12},{... | collective-permute-start | bytes 73736 | tf_op jit(solution)/shard_map/ppermute | solution.py:24
  194.7 6.6 %collective-permute-start.27 = (f32[2,6,1,512]{3,2,1,0:T(1,128)S(1)}, f32[2,6,1,512]{3,2,1,0:T(1,128)S(1)}, u32[]{:S(2)}, u32[]{:S(2)}) collective-permute-start(f32[2,6,1,512]{3,2,1,0:T(1,128)S(1)} %get-tuple-element.34), channel_id=1, source_target_pairs={{0,1},{1,2},{2,3},{4,5},{5,6},{6,7},{8,9},{9,10},{10,11},{12,13},{... | collective-permute-start | bytes 73736 | tf_op jit(solution)/shard_map/ppermute | solution.py:22
  203.8 5.8 %collective-permute-start.28 = (f32[2,1,64,512]{3,2,1,0:T(8,128)S(1)}, f32[2,1,64,512]{3,2,1,0:T(8,128)S(1)}, u32[]{:S(2)}, u32[]{:S(2)}) collective-permute-start(f32[2,1,64,512]{3,2,1,0:T(8,128)S(1)} %get-tuple-element.49), channel_id=1, source_target_pairs={{4,0},{8,4},{12,8},{16,12},{20,16},{24,20},{28,24},{5,1},{9,5},{13... | collective-permute-start | bytes 786440 | tf_op jit(solution)/shard_map/ppermute | solution.py:24
  205.7 7.7 %collective-permute-start.29 = (f32[2,1,64,512]{3,2,1,0:T(8,128)S(1)}, f32[2,1,64,512]{3,2,1,0:T(8,128)S(1)}, u32[]{:S(2)}, u32[]{:S(2)}) collective-permute-start(f32[2,1,64,512]{3,2,1,0:T(8,128)S(1)} %get-tuple-element.48), channel_id=1, source_target_pairs={{0,4},{4,8},{8,12},{12,16},{16,20},{20,24},{24,28},{1,5},{5,9},{9,... | collective-permute-start | bytes 786440 | tf_op jit(solution)/shard_map/ppermute | solution.py:22
  213.4 5.9 %collective-permute-start.30 = (f32[2,6,1,512]{3,2,1,0:T(1,128)S(1)}, f32[2,6,1,512]{3,2,1,0:T(1,128)S(1)}, u32[]{:S(2)}, u32[]{:S(2)}) collective-permute-start(f32[2,6,1,512]{3,2,1,0:T(1,128)S(1)} %get-tuple-element.33), channel_id=1, source_target_pairs={{1,0},{2,1},{3,2},{5,4},{6,5},{7,6},{9,8},{10,9},{11,10},{13,12},{... | collective-permute-start | bytes 73736 | tf_op jit(solution)/shard_map/ppermute | solution.py:24
  215.5 6.6 %collective-permute-start.31 = (f32[2,6,1,512]{3,2,1,0:T(1,128)S(1)}, f32[2,6,1,512]{3,2,1,0:T(1,128)S(1)}, u32[]{:S(2)}, u32[]{:S(2)}) collective-permute-start(f32[2,6,1,512]{3,2,1,0:T(1,128)S(1)} %get-tuple-element.32), channel_id=1, source_target_pairs={{0,1},{1,2},{2,3},{4,5},{5,6},{6,7},{8,9},{9,10},{10,11},{12,13},{... | collective-permute-start | bytes 73736 | tf_op jit(solution)/shard_map/ppermute | solution.py:22
  224.7 4.9 %collective-permute-start.32 = (f32[1,512]{1,0:T(1,128)S(1)}, f32[1,512]{1,0:T(1,128)S(1)}, u32[]{:S(2)}, u32[]{:S(2)}) collective-permute-start(f32[1,512]{1,0:T(1,128)S(1)} %slice.594), channel_id=1, source_target_pairs={{0,4},{4,8},{8,12},{12,16},{16,20},{20,24},{24,28},{1,5},{5,9},{9,... | collective-permute-start | bytes 6152 | tf_op jit(solution)/shard_map/ppermute | solution.py:34
  252.6 3.7 %collective-permute-start.33 = (f32[1,512]{1,0:T(1,128)S(1)}, f32[1,512]{1,0:T(1,128)S(1)}, u32[]{:S(2)}, u32[]{:S(2)}) collective-permute-start(f32[1,512]{1,0:T(1,128)S(1)} %slice.599), channel_id=1, source_target_pairs={{4,0},{8,4},{12,8},{16,12},{20,16},{24,20},{28,24},{5,1},{9,5},{13... | collective-permute-start | bytes 6152 | tf_op jit(solution)/shard_map/ppermute | solution.py:34
  257.9 7.5 %collective-permute-start.34 = (f32[2,1,64,512]{3,2,1,0:T(8,128)S(1)}, f32[2,1,64,512]{3,2,1,0:T(8,128)S(1)}, u32[]{:S(2)}, u32[]{:S(2)}) collective-permute-start(f32[2,1,64,512]{3,2,1,0:T(8,128)S(1)} %get-tuple-element.47), channel_id=1, source_target_pairs={{4,0},{8,4},{12,8},{16,12},{20,16},{24,20},{28,24},{5,1},{9,5},{13... | collective-permute-start | bytes 786440 | tf_op jit(solution)/shard_map/ppermute | solution.py:24
  261.5 7.7 %collective-permute-start.35 = (f32[2,1,64,512]{3,2,1,0:T(8,128)S(1)}, f32[2,1,64,512]{3,2,1,0:T(8,128)S(1)}, u32[]{:S(2)}, u32[]{:S(2)}) collective-permute-start(f32[2,1,64,512]{3,2,1,0:T(8,128)S(1)} %get-tuple-element.46), channel_id=1, source_target_pairs={{0,4},{4,8},{8,12},{12,16},{16,20},{20,24},{24,28},{1,5},{5,9},{9,... | collective-permute-start | bytes 786440 | tf_op jit(solution)/shard_map/ppermute | solution.py:22
  269.3 10.5 %copy-start.3 = (f32[4,64,512]{2,1,0:T(8,128)S(1)}, f32[4,64,512]{2,1,0:T(8,128)}, u32[]{:S(2)}) copy-start(f32[4,64,512]{2,1,0:T(8,128)} %copy-done) | copy-start | bytes 1572868
  269.3 10.5 %copy-start.6 = (f32[2,4,64,512]{3,2,1,0:T(8,128)S(1)}, f32[2,4,64,512]{3,2,1,0:T(8,128)}, u32[]{:S(2)}) copy-start(f32[2,4,64,512]{3,2,1,0:T(8,128)} %param.3) | copy-start | bytes 3145732
  269.3 6.0 %collective-permute-start.36 = (f32[2,6,1,512]{3,2,1,0:T(1,128)S(1)}, f32[2,6,1,512]{3,2,1,0:T(1,128)S(1)}, u32[]{:S(2)}, u32[]{:S(2)}) collective-permute-start(f32[2,6,1,512]{3,2,1,0:T(1,128)S(1)} %get-tuple-element.31), channel_id=1, source_target_pairs={{1,0},{2,1},{3,2},{5,4},{6,5},{7,6},{9,8},{10,9},{11,10},{13,12},{... | collective-permute-start | bytes 73736 | tf_op jit(solution)/shard_map/ppermute | solution.py:24
  272.3 6.6 %collective-permute-start.37 = (f32[2,6,1,512]{3,2,1,0:T(1,128)S(1)}, f32[2,6,1,512]{3,2,1,0:T(1,128)S(1)}, u32[]{:S(2)}, u32[]{:S(2)}) collective-permute-start(f32[2,6,1,512]{3,2,1,0:T(1,128)S(1)} %get-tuple-element.30), channel_id=1, source_target_pairs={{0,1},{1,2},{2,3},{4,5},{5,6},{6,7},{8,9},{9,10},{10,11},{12,13},{... | collective-permute-start | bytes 73736 | tf_op jit(solution)/shard_map/ppermute | solution.py:22
  282.3 1.0 copy-start.11
  284.1 6.1 %collective-permute-start.38 = (f32[2,1,64,512]{3,2,1,0:T(8,128)}, f32[2,1,64,512]{3,2,1,0:T(8,128)S(1)}, u32[]{:S(2)}, u32[]{:S(2)}) collective-permute-start(f32[2,1,64,512]{3,2,1,0:T(8,128)} %get-tuple-element.45), channel_id=1, source_target_pairs={{4,0},{8,4},{12,8},{16,12},{20,16},{24,20},{28,24},{5,1},{9,5},{13... | collective-permute-start | bytes 786440 | tf_op jit(solution)/shard_map/ppermute | solution.py:24
  286.0 8.0 %collective-permute-start.39 = (f32[2,1,64,512]{3,2,1,0:T(8,128)}, f32[2,1,64,512]{3,2,1,0:T(8,128)}, u32[]{:S(2)}, u32[]{:S(2)}) collective-permute-start(f32[2,1,64,512]{3,2,1,0:T(8,128)} %get-tuple-element.44), channel_id=1, source_target_pairs={{0,4},{4,8},{8,12},{12,16},{16,20},{20,24},{24,28},{1,5},{5,9},{9,... | collective-permute-start | bytes 786440 | tf_op jit(solution)/shard_map/ppermute | solution.py:22
  288.4 16.3 %copy-start.12 = (f32[2,4,64,512]{3,2,1,0:T(8,128)S(1)}, f32[2,4,64,512]{3,2,1,0:T(8,128)}, u32[]{:S(2)}) copy-start(f32[2,4,64,512]{3,2,1,0:T(8,128)} %copy-done.11) | copy-start | bytes 3145732
  295.0 11.5 %copy-start.4 = (f32[4,64,512]{2,1,0:T(8,128)S(1)}, f32[4,64,512]{2,1,0:T(8,128)}, u32[]{:S(2)}) copy-start(f32[4,64,512]{2,1,0:T(8,128)} %copy-done) | copy-start | bytes 1572868
  295.1 11.5 %copy-start.7 = (f32[2,4,64,512]{3,2,1,0:T(8,128)S(1)}, f32[2,4,64,512]{3,2,1,0:T(8,128)}, u32[]{:S(2)}) copy-start(f32[2,4,64,512]{3,2,1,0:T(8,128)} %param.3) | copy-start | bytes 3145732
  295.1 11.5 %copy-start.13 = (f32[2,4,64,512]{3,2,1,0:T(8,128)S(1)}, f32[2,4,64,512]{3,2,1,0:T(8,128)}, u32[]{:S(2)}) copy-start(f32[2,4,64,512]{3,2,1,0:T(8,128)} %get-tuple-element.13) | copy-start | bytes 3145732
  295.1 6.6 %collective-permute-start.40 = (f32[2,6,1,512]{3,2,1,0:T(1,128)S(1)}, f32[2,6,1,512]{3,2,1,0:T(1,128)S(1)}, u32[]{:S(2)}, u32[]{:S(2)}) collective-permute-start(f32[2,6,1,512]{3,2,1,0:T(1,128)S(1)} %get-tuple-element.29), channel_id=1, source_target_pairs={{1,0},{2,1},{3,2},{5,4},{6,5},{7,6},{9,8},{10,9},{11,10},{13,12},{... | collective-permute-start | bytes 73736 | tf_op jit(solution)/shard_map/ppermute | solution.py:24
  298.1 6.6 %collective-permute-start.41 = (f32[2,6,1,512]{3,2,1,0:T(1,128)S(1)}, f32[2,6,1,512]{3,2,1,0:T(1,128)S(1)}, u32[]{:S(2)}, u32[]{:S(2)}) collective-permute-start(f32[2,6,1,512]{3,2,1,0:T(1,128)S(1)} %get-tuple-element.28), channel_id=1, source_target_pairs={{0,1},{1,2},{2,3},{4,5},{5,6},{6,7},{8,9},{9,10},{10,11},{12,13},{... | collective-permute-start | bytes 73736 | tf_op jit(solution)/shard_map/ppermute | solution.py:22
where the time goes:
time: 312 us; the launch traced here: 310 us
  starting transfers between devices  112 us (36%)
  waiting for transfers between devices  89.3 us (29%)
  blocking collectives  61.2 us (20%)
  other arithmetic  32.4 us (10%)
  local copies, waits for them, and re-layouts  6.4 us (2%)
  between operations  5.48 us (2%)
  matrix products  3.36 us (1%)
    ppermute x18, waiting for transfers between devices, with_halo(): lax.ppermute(tail, axis, [(i, (i + 1) % count) for i in range(ends)])  62.2 us
    ppermute x18, starting transfers between devices, with_halo(): lax.ppermute(head, axis, [((i + 1) % count, i) for i in range(ends)])  49.8 us
    ppermute x18, starting transfers between devices, with_halo(): lax.ppermute(tail, axis, [(i, (i + 1) % count) for i in range(ends)])  47 us
    psum x3, blocking collectives, total(): return lax.psum(value, 'slab')  36.2 us
    psum x3, blocking collectives, diverge(): return lax.psum(ordered, 'cross')  25.1 us
    add x8, other arithmetic, velocity_solve(): solved = solved + change  15.6 us
    ppermute x6, starting transfers between devices, passed_along(): return lax.ppermute(block, axis, route)  15.1 us
    ppermute x18, waiting for transfers between devices, with_halo(): lax.ppermute(head, axis, [((i + 1) % count, i) for i in range(ends)])  14.5 us
  transfers between devices with their start and end apart: 42, of which 33 were waited for; matrix products, arithmetic and copies ran while one was open for 1% of the time, Pallas kernels for 0%

commit v1 on v0

v1 whole, which is shorter than its diff:
```python
import jax
import jax.numpy as jnp
from jax import lax
from jax.sharding import PartitionSpec as P

OUTER = 2
DEGREE = 3


cheb_theta = 1.025
cheb_delta = 0.975


def cheb_weights():
    sigma = cheb_theta / cheb_delta
    solved = [1.0 / cheb_theta] + [0.0] * (DEGREE - 1)
    change = list(solved)
    rho_prev = 1.0 / sigma
    for step in range(DEGREE - 1):
        resid = [(1.0 if k == 0 else solved[k - 1]) - solved[k] for k in range(DEGREE)]
        resid[0] = 1.0 - solved[0]
        rho = 1.0 / (2.0 * sigma - rho_prev)
        change = [rho * rho_prev * c + 2.0 * rho / cheb_delta * r for c, r in zip(change, resid)]
        solved = [s + c for s, c in zip(solved, change)]
        rho_prev = rho
    return solved


OFFSETS = [(0, 0), (1, 0), (0, 1), (2, 0), (0, 2), (1, 1), (1, -1)]


def with_halo(cells, axis, dim, width):
    count = lax.axis_size(axis)
    ends = count - 1
    head = lax.slice_in_dim(cells, 0, width, axis=dim)
    tail = lax.slice_in_dim(cells, cells.shape[dim] - width, cells.shape[dim], axis=dim)
    return jnp.concatenate(
        [
            lax.ppermute(tail, axis, [(i, i + 1) for i in range(ends)]),
            cells,
            lax.ppermute(head, axis, [(i + 1, i) for i in range(ends)]),
        ],
        axis=dim,
    )


def zs(a, s):
    if s > 0:
        return jnp.pad(a[..., s:], [(0, 0)] * (a.ndim - 1) + [(0, s)])
    return jnp.pad(a[..., :s], [(0, 0)] * (a.ndim - 1) + [(-s, 0)])


def rows(a, s):
    if s == 0:
        return a
    if s > 0:
        return jnp.pad(a[s:], ((0, s), (0, 0)))
    return jnp.pad(a[:s], ((-s, 0), (0, 0)))


def at(a, dx, dz):
    a = rows(a, dx)
    return zs(a, dz) if dz else a


def shards(forcing, viscosity, owner_slot):
    w0, w1, w2 = cheb_weights()
    slab_n, cross_n = lax.axis_size("slab"), lax.axis_size("cross")
    slab, cross = lax.axis_index("slab"), lax.axis_index("cross")
    nx, ny, nz = viscosity.shape
    v = with_halo(with_halo(viscosity, "cross", 1, 3), "slab", 0, 3)
    f = with_halo(with_halo(forcing, "cross", 2, 2), "slab", 1, 2)
    c = v[1:-1, 1:-1]
    fxp, fxm = 0.5 * (c + v[2:, 1:-1]), 0.5 * (c + v[:-2, 1:-1])
    fyp, fym = 0.5 * (c + v[1:-1, 2:]), 0.5 * (c + v[1:-1, :-2])
    fzp, fzm = 0.5 * (c + zs(c, 1)), 0.5 * (c + zs(c, -1))
    diag = fxp + fxm + fyp + fym + fzp + fzm
    xi = lax.broadcasted_iota(jnp.int32, c.shape, 0) + slab * nx - 2
    yi = lax.broadcasted_iota(jnp.int32, c.shape, 1) + cross * ny - 2
    inside = (xi >= 0) & (xi < nx * slab_n) & (yi >= 0) & (yi < ny * cross_n)
    dinv = jnp.where(inside, 1.0 / jnp.where(inside, diag, 1.0), 0.0)

    def inner(a):
        return a[..., 1:-1, 1:-1, :]

    def nbr(a, dx, dy):
        n1, n2 = a.shape[-3], a.shape[-2]
        return a[..., 1 + dx : n1 - 1 + dx, 1 + dy : n2 - 1 + dy, :]

    faces2 = (fxp, fxm, fyp, fym, fzp, fzm)
    faces1 = tuple(inner(a) for a in faces2)
    faces0 = tuple(inner(a) for a in faces1)
    d1, d0 = inner(dinv), inner(inner(dinv))

    def tapply(y, fc, di):
        fxp, fxm, fyp, fym, fzp, fzm = fc
        yc = inner(y)
        return di * (
            fxp * nbr(y, 1, 0) + fxm * nbr(y, -1, 0) + fyp * nbr(y, 0, 1)
            + fym * nbr(y, 0, -1) + fzp * zs(yc, 1) + fzm * zs(yc, -1)
        )

    y0 = dinv * f
    t1 = tapply(y0, faces1, d1)
    free = w0 * inner(inner(y0)) + tapply(w1 * inner(y0) + w2 * t1, faces0, d0)

    xp, xm, yp, ym, zp, zm = faces1
    W = {
        (0, 0): d1 * (yp * nbr(dinv, 0, 1) + ym * nbr(dinv, 0, -1)),
        (1, 0): d1 * xp * nbr(dinv, 1, 0),
        (-1, 0): d1 * xm * nbr(dinv, -1, 0),
        (0, 1): d1 * zp * zs(d1, 1),
        (0, -1): d1 * zm * zs(d1, -1),
    }
    U = {o: w2 * a for o, a in W.items()}
    U[(0, 0)] = U[(0, 0)] + w1 * d1
    xp, xm, yp, ym, zp, zm = faces0
    acc = {}

    def add(o, a):
        acc[o] = acc[o] + a if o in acc else a

    for o, a in U.items():
        ac = inner(a)
        add(o, yp * nbr(a, 0, 1) + ym * nbr(a, 0, -1))
        add((o[0] + 1, o[1]), xp * nbr(a, 1, 0))
        add((o[0] - 1, o[1]), xm * nbr(a, -1, 0))
        add((o[0], o[1] + 1), zp * zs(ac, 1))
        add((o[0], o[1] - 1), zm * zs(ac, -1))
    m = {o: d0 * a for o, a in acc.items()}
    m[(0, 0)] = m[(0, 0)] + w0 * d0

    part = jnp.stack([jnp.sum(m[o], axis=1) for o in OFFSETS] + [jnp.sum(free[0], 1), jnp.sum(free[1], 1)], 1)
    whole = lax.psum(part, "cross")
    whole = lax.all_gather(whole, "slab", axis=0, tiled=True)
    K = {o: whole[:, n] for n, o in enumerate(OFFSETS)}
    cx, cz = whole[:, 7], whole[:, 8]

    def diverge(cx, cz):
        return cx - rows(cx, -1) + cz - zs(cz, -1)

    def grad(q):
        return q - rows(q, 1), q - zs(q, 1)

    back = {o: at(a, -o[0], -o[1]) for o, a in K.items()}

    def kapply(q):
        out = K[(0, 0)] * q
        for o in OFFSETS[1:]:
            out = out + K[o] * at(q, o[0], o[1]) + back[o] * at(q, -o[0], -o[1])
        return out

    target = diverge(cx, cz)
    pressure = jnp.zeros_like(target)
    resid = dirn = target
    rr = jnp.sum(resid * resid)
    for step in range(OUTER):
        gx, gz = grad(dirn)
        image = diverge(kapply(gx), kapply(gz))
        alpha = rr / jnp.sum(dirn * image)
        pressure = pressure + alpha * dirn
        if step + 1 < OUTER:
            resid = resid - alpha * image
            fresh = jnp.sum(resid * resid)
            dirn = resid + (fresh / rr) * dirn
            rr = fresh
    g = jnp.pad(jnp.stack(grad(pressure)), ((0, 0), (2, 2), (0, 0)))
    g = lax.dynamic_slice_in_dim(g, slab * nx, nx + 4, 1)
    velocity = free
    for o, a in m.items():
        s = g[:, 2 + o[0] : 2 + o[0] + nx]
        s = zs(s, o[1]) if o[1] else s
        velocity = velocity - a[None] * s[:, :, None, :]
    mine = lax.dynamic_slice_in_dim(pressure, slab * nx, nx, 0)
    width = nz // cross_n
    cols = cross * width + jnp.arange(width, dtype=jnp.int32)
    onehot = (owner_slot[:, None] == cols[None, :]).astype(jnp.float32)
    return velocity, jnp.dot(mine, onehot, precision=lax.Precision.HIGHEST)


def solution(mesh):
    in_specs = (P(None, "slab", "cross", None), P("slab", "cross", None), P())
    out_specs = (P(None, "slab", "cross", None), P("slab", "cross"))
    return jax.shard_map(shards, mesh=mesh, in_specs=in_specs, out_specs=out_specs, check_vma=False)
```

time: 312 us -> 146 us (0.47)
  the two profiles are of different devices: /device:TPU:12 before, /device:TPU:9 now
where the time goes in v1:
time: 146 us; the launch traced here: 145 us
  waiting for transfers between devices  45 us (31%)
  other arithmetic  26.1 us (18%)
  starting transfers between devices  21.9 us (15%)
  between operations  18.8 us (13%)
  blocking collectives  17.5 us (12%)
  local copies, waits for them, and re-layouts  14.5 us (10%)
    psum x1, waiting for transfers between devices, shards(): whole = lax.psum(part, 'cross')  43.9 us
    all_gather x1, blocking collectives, shards(): whole = lax.all_gather(whole, 'slab', axis=0, tiled=True)  17.5 us
    ppermute x4, starting transfers between devices, with_halo(): lax.ppermute(tail, axis, [(i, i + 1) for i in range(ends)])  15.5 us
    reduce_sum x4, other arithmetic, shards(): jnp.sum(m[o], axis=1)  7.7 us
    ppermute x4, starting transfers between devices, with_halo(): lax.ppermute(head, axis, [(i + 1, i) for i in range(ends)])  6.43 us
    sub x1, other arithmetic, shards(): velocity = velocity - a[None] * s[:, :, None, :]  4.24 us
    slice x4, local copies, waits for them, and re-layouts, with_halo(): lax.slice_in_dim(cells, cells.shape[dim] - width, cells.shape[dim], axis=...  3.76 us
    slice x23, local copies, waits for them, and re-layouts, zs(): return jnp.pad(a[..., s:], [(0, 0)] * (a.ndim - 1) + [(0, s)])  3.62 us
  transfers between devices with their start and end apart: 9, of which 2 were waited for; matrix products, arithmetic and copies ran while one was open for 14% of the time, Pallas kernels for 0%

profile of v1, /device:TPU:9, one launch (start us, length us, event | category | flops | bytes accessed | tf_op | source)
XLA Modules:
  0.0 144.8 jit_solution(8039660950625776331)
XLA Ops:
  7.2 0.9 fusion.102
  8.1 3.1 %collective-permute-start = (f32[4,3,512]{2,1,0:T(4,128)S(1)}, f32[4,3,512]{2,1,0:T(4,128)S(1)}, u32[]{:S(2)}, u32[]{:S(2)}) collective-permute-start(f32[4,3,512]{2,1,0:T(4,128)S(1)} %get-tuple-element.92), channel_id=1, source_target_pairs={{0,1},{1,2},{2,3},{4,5},{5,6},{6,7},{8,9},{9,10},{10,11},{12,13},{... | collective-permute-start | bytes 73736 | tf_op jit(solution)/shard_map/ppermute | solution.py:39
  11.2 1.3 collective-permute-start.1
  12.5 1.6 %fusion.95 = (f32[2,4,2,512]{3,2,1,0:T(2,128)}, f32[2,4,2,512]{3,2,1,0:T(2,128)}) fusion(f32[2,4,64,512]{3,2,1,0:T(8,128)} %param.3), kind=kLoop, calls=%fused_computation.193 | loop fusion | bytes 131072 | tf_op jit(solution)/shard_map/slice | solution.py:36
  14.1 4.0 %collective-permute-start.4 = (f32[2,4,2,512]{3,2,1,0:T(2,128)}, f32[2,4,2,512]{3,2,1,0:T(2,128)S(1)}, u32[]{:S(2)}, u32[]{:S(2)}) collective-permute-start(f32[2,4,2,512]{3,2,1,0:T(2,128)} %get-tuple-element.78), channel_id=1, source_target_pairs={{0,1},{1,2},{2,3},{4,5},{5,6},{6,7},{8,9},{9,10},{10,11},{12,13},{... | collective-permute-start | bytes 98312 | tf_op jit(solution)/shard_map/ppermute | solution.py:39
  18.1 1.3 collective-permute-start.5
  19.5 1.1 pad_maximum_fusion.2
  20.6 0.1 fusion.101
  20.7 4.7 %collective-permute-start.2 = (f32[3,70,512]{2,1,0:T(8,128)S(1)}, f32[3,70,512]{2,1,0:T(8,128)S(1)}, u32[]{:S(2)}, u32[]{:S(2)}) collective-permute-start(f32[3,70,512]{2,1,0:T(8,128)S(1)} %get-tuple-element.90), channel_id=1, source_target_pairs={{0,4},{4,8},{8,12},{12,16},{16,20},{20,24},{24,28},{1,5},{5,9},{9,... | collective-permute-start | bytes 1290248 | tf_op jit(solution)/shard_map/ppermute | solution.py:39
  25.5 1.9 %collective-permute-start.3 = (f32[3,70,512]{2,1,0:T(8,128)S(1)}, f32[3,70,512]{2,1,0:T(8,128)S(1)}, u32[]{:S(2)}, u32[]{:S(2)}) collective-permute-start(f32[3,70,512]{2,1,0:T(8,128)S(1)} %get-tuple-element.91), channel_id=1, source_target_pairs={{4,0},{8,4},{12,8},{16,12},{20,16},{24,20},{28,24},{5,1},{9,5},{13... | collective-permute-start | bytes 1290248 | tf_op jit(solution)/shard_map/ppermute | solution.py:41
  27.5 0.2 pad_maximum_fusion.1
  27.7 1.2 fusion.92
  28.9 3.6 %collective-permute-start.6 = (f32[2,2,68,512]{3,2,1,0:T(8,128)}, f32[2,2,68,512]{3,2,1,0:T(8,128)}, u32[]{:S(2)}, u32[]{:S(2)}) collective-permute-start(f32[2,2,68,512]{3,2,1,0:T(8,128)} %get-tuple-element.63), channel_id=1, source_target_pairs={{0,4},{4,8},{8,12},{12,16},{16,20},{20,24},{24,28},{1,5},{5,9},{9,... | collective-permute-start | bytes 1671176 | tf_op jit(solution)/shard_map/ppermute | solution.py:39
  32.5 1.9 %collective-permute-start.7 = (f32[2,2,68,512]{3,2,1,0:T(8,128)}, f32[2,2,68,512]{3,2,1,0:T(8,128)}, u32[]{:S(2)}, u32[]{:S(2)}) collective-permute-start(f32[2,2,68,512]{3,2,1,0:T(8,128)} %get-tuple-element.64), channel_id=1, source_target_pairs={{4,0},{8,4},{12,8},{16,12},{20,16},{24,20},{28,24},{5,1},{9,5},{13... | collective-permute-start | bytes 1671176 | tf_op jit(solution)/shard_map/ppermute | solution.py:41
  34.4 1.1 collective-permute-done.3
  35.5 0.2 pad_maximum_fusion
  35.7 0.5 fusion.90
  36.2 1.4 divide_select_fusion
  37.6 0.4 fusion.91
  38.1 0.9 slice.809
  39.0 0.8 slice.811
  39.9 1.5 %fusion.24 = (f32[6,66,512]{2,1,0:T(8,128)S(1)}, f32[6,66,512]{2,1,0:T(8,128)S(1)}, f32[6,66,512]{2,1,0:T(8,128)S(1)}, f32[6,66,512]{2,1,0:T(8,128)S(1)}, f32[6,...) fusion(f32[8,68,512]{2,1,0:T(8,128)S(1)} %get-tuple-element.21,, ...), kind=kLoop, calls=%fused_computation.48 | loop fusion | flops 3244032 | bytes 16216992 | tf_op jit(solution)/shard_map/add | solution.py:116
  41.4 0.2 fusion.97
  41.6 0.3 fusion.20
  41.9 0.2 fusion.99
  42.2 0.2 fusion.98
  42.4 0.2 fusion.100
  42.6 1.7 %fusion.71 = (f32[4,512]{1,0:T(4,128)S(1)}, f32[4,64,512]{2,1,0:T(8,128)S(1)}, f32[4,64,512]{2,1,0:T(8,128)S(1)}, f32[4,512]{1,0:T(4,128)S(1)}, f32[4,64,512]{2,1,0:T(8,128)S(1)}, /*index=5*/f32[4,64,512]{2,1,0:T(8,128)}) fusion(f32[6,66,512]{2,1,0:T(8,128)S(1)} %get-tuple-element.52, f32[8,68,512]{2,1,0:T(8,128)S(1)} %get-tuple-element.23, ...), kind=kLoop, calls=%fused_computation.179 | loop fusion | flops 2093056 | bytes 8401920 | tf_op jit(solution)/shard_map/reduce_sum | solution.py:133
  44.4 0.2 fusion.96
  44.7 2.2 %fusion.82 = (f32[4,512]{1,0:T(4,128)S(1)}, f32[4,64,512]{2,1,0:T(8,128)}, f32[4,64,512]{2,1,0:T(8,128)}) fusion(f32[8,68,512]{2,1,0:T(8,128)S(1)} %get-tuple-element.21, f32[4,64,511]{2,1,0:T(8,128)S(1)} %get-tuple-element.85, f32[8,68,512]{2,1,0:T(8,128)S(1)} %get-tuple-element.26, f32[4,64,511]{2,1,0:T(8,128)S(1)} %get-tuple-element.89, ...), kind=kLoop, calls=%fused_computation.185 | loop fusion | flops 2357248 | bytes 8918016 | tf_op jit(solution)/shard_map/reduce_sum | solution.py:133
  46.8 1.9 %fusion.78 = (f32[4,512]{1,0:T(4,128)S(1)}, f32[4,64,512]{2,1,0:T(8,128)}, f32[4,64,512]{2,1,0:T(8,128)}, f32[4,512]{1,0:T(4,128)S(1)}, f32[4,64,512]{2,1,0:T(8,128)}, /*index=5*/f32[4,64,512]{2,1,0:T(8,128)S(1)}) fusion(f32[6,66,512]{2,1,0:T(8,128)S(1)} %get-tuple-element.54, f32[8,68,512]{2,1,0:T(8,128)S(1)} %get-tuple-element.25, ...), kind=kLoop, calls=%fused_computation.183 | loop fusion | flops 2093056 | bytes 8401920 | tf_op jit(solution)/shard_map/reduce_sum | solution.py:133
  48.8 1.9 %fusion.80 = (f32[4,512]{1,0:T(4,128)S(1)}, f32[4,64,512]{2,1,0:T(8,128)}, f32[4,64,512]{2,1,0:T(8,128)}, f32[4,512]{1,0:T(4,128)S(1)}, f32[4,64,512]{2,1,0:T(8,128)}, /*index=5*/f32[4,64,512]{2,1,0:T(8,128)S(1)}) fusion(f32[6,66,512]{2,1,0:T(8,128)S(1)} %get-tuple-element.58, f32[8,68,512]{2,1,0:T(8,128)S(1)} %get-tuple-element.25, ...), kind=kLoop, calls=%fused_computation.184 | loop fusion | flops 2093056 | bytes 8404992 | tf_op jit(solution)/shard_map/reduce_sum | solution.py:133
  50.7 1.0 multiply_multiply_fusion.2
  51.7 1.7 %maximum_multiply_fusion = f32[2,8,68,512]{3,2,1,0:T(8,128)S(1)} fusion(f32[2,2,68,512]{3,2,1,0:T(8,128)} %collective-permute-done.7, f32[2,4,2,512]{3,2,1,0:T(2,128)S(1)} %copy-done.15, f32[2,4,64,512]{3,2,1,0:T(8,128)S(1)} %copy-done, f32[2,4,2,512]{3,2,1,0:T(2,128)S(1)} %collective-permute-done.4, f32[2,2,68,512]{3,2,1,0:T(8,128)} %collective-permute-done.6, ...), kind=kLoop, calls=%fused_computation | loop fusion | flops 2785280 | bytes 5570560 | tf_op jit(solution)/shard_map/mul | solution.py:103
  53.5 0.8 fusion.88
  54.3 2.1 %fusion.5 = f32[2,6,66,512]{3,2,1,0:T(8,128)S(1)} fusion(f32[2,8,68,512]{3,2,1,0:T(8,128)S(1)} %maximum_multiply_fusion, f32[2,6,66,511]{3,2,1,0:T(8,128)S(1)} %get-tuple-element.40, f32[2,6,66,511]{3,2,1,0:T(8,128)S(1)} %get-tuple-element.39, f32[6,66,512]{2,1,0:T(8,128)S(1)} %get-tuple-element.53, f32[6,66,512]{2,1,0:T(8,128)S(1)} %get-tuple-element.55, ...), kind=kLoop, calls=%fused_computation.7 | loop fusion | flops 6082560 | bytes 18646848 | tf_op jit(solution)/shard_map/add | solution.py:105
  56.5 0.5 fusion.89
  56.9 0.5 copy-done.6
  57.5 0.2 copy-done.7
  57.7 1.1 fusion.16
  58.8 0.1 slice_reduce_fusion
  58.9 1.4 stack.48
  60.4 43.9 %all-reduce.97.cloned.1.call-done = f32[4,9,512]{2,1,0:T(8,128)} async-done(((f32[4,9,512]{2,1,0:T(8,128)}), f32[4,9,512]{2,1,0:T(8,128)}) %all-reduce.97.cloned.1.call-update) | async-done | bytes 73744 | tf_op jit(solution)/shard_map/psum | solution.py:134
  104.3 17.5 %all_gather.3 = f32[32,9,512]{2,1,0:T(8,128)S(1)} all-gather(f32[4,9,512]{2,1,0:T(8,128)} %all-reduce.97.cloned.1.call-done), channel_id=1, replica_groups=mesh['slab'=8,'cross'=4] {'slab'}, dimensions={0}, use_global_device_ids=true | all-gather | bytes 663552 | tf_op jit(solution)/shard_map/all_gather | solution.py:135
  121.8 0.4 fusion.94
  122.2 0.2 fusion.93
  122.5 0.1 fusion.60
  123.2 0.1 pad_slice_fusion.17
  123.5 0.1 pad_slice_fusion.13
  123.7 0.3 multiply_add_fusion.5
  124.0 0.1 copy-done.8
  124.1 0.3 multiply_add_fusion.4
  124.4 0.8 multiply_reduce_fusion.2
  126.5 0.6 multiply_reduce_fusion.1
  129.0 0.1 pad_slice_fusion.9
  129.1 0.1 pad_slice_fusion.5
  129.2 0.1 pad_slice_fusion.3
  129.3 0.2 copy-done.9
  129.6 0.3 multiply_add_fusion.2
  129.8 0.3 multiply_add_fusion.1
  130.1 0.7 multiply_reduce_fusion
  132.3 0.1 fusion.120
  132.9 0.9 fusion.54
  133.8 4.2 %multiply_subtract_fusion = f32[2,4,64,512]{3,2,1,0:T(8,128)} fusion(f32[2,4,64,512]{3,2,1,0:T(8,128)S(1)} %fusion.16, f32[2,4,512]{2,1,0:T(4,128)S(1)} %pad.418, f32[4,64,512]{2,1,0:T(8,128)} %get-tuple-element.47, f32[2,4,512]{2,1,0:T(4,128)S(1)} %pad.416, f32[4,64,512]{2,1,0:T(8,128)} %get-tuple-element.38, f32[2,4,512]{2,1,0:T(4,128)S(1)} %pad.415, ...), kind=kLoop, calls=%fused_computation.39 | loop fusion | flops 6815744 | bytes 9125888 | tf_op jit(solution)/shard_map/sub | solution.py:173
  (105 shorter events, 2.4 us)
Async XLA Ops:
  7.2 97.1 %all-reduce.97.cloned.1.call-start = ((), (), s32[]{:S(2)}) async-start(), calls=%async_computation | async-start | bytes 262144 | tf_op jit(solution)/shard_map/psum | solution.py:134
  8.1 11.4 %collective-permute-start = (f32[4,3,512]{2,1,0:T(4,128)S(1)}, f32[4,3,512]{2,1,0:T(4,128)S(1)}, u32[]{:S(2)}, u32[]{:S(2)}) collective-permute-start(f32[4,3,512]{2,1,0:T(4,128)S(1)} %get-tuple-element.92), channel_id=1, source_target_pairs={{0,1},{1,2},{2,3},{4,5},{5,6},{6,7},{8,9},{9,10},{10,11},{12,13},{... | collective-permute-start | bytes 73736 | tf_op jit(solution)/shard_map/ppermute | solution.py:39
  11.2 8.2 %collective-permute-start.1 = (f32[4,3,512]{2,1,0:T(4,128)S(1)}, f32[4,3,512]{2,1,0:T(4,128)S(1)}, u32[]{:S(2)}, u32[]{:S(2)}) collective-permute-start(f32[4,3,512]{2,1,0:T(4,128)S(1)} %get-tuple-element.93), channel_id=1, source_target_pairs={{1,0},{2,1},{3,2},{5,4},{6,5},{7,6},{9,8},{10,9},{11,10},{13,12},{... | collective-permute-start | bytes 73736 | tf_op jit(solution)/shard_map/ppermute | solution.py:41
  14.1 13.3 %collective-permute-start.4 = (f32[2,4,2,512]{3,2,1,0:T(2,128)}, f32[2,4,2,512]{3,2,1,0:T(2,128)S(1)}, u32[]{:S(2)}, u32[]{:S(2)}) collective-permute-start(f32[2,4,2,512]{3,2,1,0:T(2,128)} %get-tuple-element.78), channel_id=1, source_target_pairs={{0,1},{1,2},{2,3},{4,5},{5,6},{6,7},{8,9},{9,10},{10,11},{12,13},{... | collective-permute-start | bytes 98312 | tf_op jit(solution)/shard_map/ppermute | solution.py:39
  18.1 9.3 %collective-permute-start.5 = (f32[2,4,2,512]{3,2,1,0:T(2,128)}, f32[2,4,2,512]{3,2,1,0:T(2,128)S(1)}, u32[]{:S(2)}, u32[]{:S(2)}) collective-permute-start(f32[2,4,2,512]{3,2,1,0:T(2,128)} %get-tuple-element.79), channel_id=1, source_target_pairs={{1,0},{2,1},{3,2},{5,4},{6,5},{7,6},{9,8},{10,9},{11,10},{13,12},{... | collective-permute-start | bytes 98312 | tf_op jit(solution)/shard_map/ppermute | solution.py:41
  20.6 6.8 %copy-start = (f32[2,4,64,512]{3,2,1,0:T(8,128)S(1)}, f32[2,4,64,512]{3,2,1,0:T(8,128)}, u32[]{:S(2)}) copy-start(f32[2,4,64,512]{3,2,1,0:T(8,128)} %param.3) | copy-start | bytes 3145732
  20.7 13.7 %collective-permute-start.2 = (f32[3,70,512]{2,1,0:T(8,128)S(1)}, f32[3,70,512]{2,1,0:T(8,128)S(1)}, u32[]{:S(2)}, u32[]{:S(2)}) collective-permute-start(f32[3,70,512]{2,1,0:T(8,128)S(1)} %get-tuple-element.90), channel_id=1, source_target_pairs={{0,4},{4,8},{8,12},{12,16},{16,20},{20,24},{24,28},{1,5},{5,9},{9,... | collective-permute-start | bytes 1290248 | tf_op jit(solution)/shard_map/ppermute | solution.py:39
  25.5 10.0 %collective-permute-start.3 = (f32[3,70,512]{2,1,0:T(8,128)S(1)}, f32[3,70,512]{2,1,0:T(8,128)S(1)}, u32[]{:S(2)}, u32[]{:S(2)}) collective-permute-start(f32[3,70,512]{2,1,0:T(8,128)S(1)} %get-tuple-element.91), channel_id=1, source_target_pairs={{4,0},{8,4},{12,8},{16,12},{20,16},{24,20},{28,24},{5,1},{9,5},{13... | collective-permute-start | bytes 1290248 | tf_op jit(solution)/shard_map/ppermute | solution.py:41
  27.4 1.4 copy-start.14
  27.7 7.8 %copy-start.1 = (f32[4,64,512]{2,1,0:T(8,128)S(1)}, f32[4,64,512]{2,1,0:T(8,128)}, u32[]{:S(2)}) copy-start(f32[4,64,512]{2,1,0:T(8,128)} %param.4) | copy-start | bytes 1572868
  28.9 22.9 %collective-permute-start.6 = (f32[2,2,68,512]{3,2,1,0:T(8,128)}, f32[2,2,68,512]{3,2,1,0:T(8,128)}, u32[]{:S(2)}, u32[]{:S(2)}) collective-permute-start(f32[2,2,68,512]{3,2,1,0:T(8,128)} %get-tuple-element.63), channel_id=1, source_target_pairs={{0,4},{4,8},{8,12},{12,16},{16,20},{20,24},{24,28},{1,5},{5,9},{9,... | collective-permute-start | bytes 1671176 | tf_op jit(solution)/shard_map/ppermute | solution.py:39
  32.5 19.2 %collective-permute-start.7 = (f32[2,2,68,512]{3,2,1,0:T(8,128)}, f32[2,2,68,512]{3,2,1,0:T(8,128)}, u32[]{:S(2)}, u32[]{:S(2)}) collective-permute-start(f32[2,2,68,512]{3,2,1,0:T(8,128)} %get-tuple-element.64), channel_id=1, source_target_pairs={{4,0},{8,4},{12,8},{16,12},{20,16},{24,20},{28,24},{5,1},{9,5},{13... | collective-permute-start | bytes 1671176 | tf_op jit(solution)/shard_map/ppermute | solution.py:41
  50.7 1.0 copy-start.15
  56.4 1.0 copy-start.6
  56.5 1.2 copy-start.7
  123.5 0.6 copy-start.8
  123.5 0.9 copy-start.10
  123.5 0.8 copy-start.12
  128.6 0.8 copy-start.9
  128.6 0.9 copy-start.11
  128.7 0.9 copy-start.13
  130.1 2.8 %copy-start.16 = (s32[512]{0:T(512)S(1)}, s32[512]{0:T(512)}, u32[]{:S(2)}) copy-start(s32[512]{0:T(512)} %param.5) | copy-start | bytes 6148
  130.1 3.7 %copy-start.2 = (f32[4,64,512]{2,1,0:T(8,128)S(1)}, f32[4,64,512]{2,1,0:T(8,128)}, u32[]{:S(2)}) copy-start(f32[4,64,512]{2,1,0:T(8,128)} %get-tuple-element.36) | copy-start | bytes 1572868
  132.1 1.6 %copy-start.3 = (f32[4,64,512]{2,1,0:T(8,128)S(1)}, f32[4,64,512]{2,1,0:T(8,128)}, u32[]{:S(2)}) copy-start(f32[4,64,512]{2,1,0:T(8,128)} %get-tuple-element.20) | copy-start | bytes 1572868
  132.1 1.6 %copy-start.4 = (f32[4,64,512]{2,1,0:T(8,128)S(1)}, f32[4,64,512]{2,1,0:T(8,128)}, u32[]{:S(2)}) copy-start(f32[4,64,512]{2,1,0:T(8,128)} %get-tuple-element.30) | copy-start | bytes 1572868
  132.1 1.6 %copy-start.5 = (f32[4,64,512]{2,1,0:T(8,128)S(1)}, f32[4,64,512]{2,1,0:T(8,128)}, u32[]{:S(2)}) copy-start(f32[4,64,512]{2,1,0:T(8,128)} %get-tuple-element.16) | copy-start | bytes 1572868
Sparse Core Ops, SparseCore 0:
  60.5 43.7 all-reduce.96

commit v2 on v1

--- a/solution.py
+++ b/solution.py
@@ -1,7 +1,13 @@
+import functools
+
 import jax
 import jax.numpy as jnp
 from jax import lax
+from jax.experimental import pallas as pl
+from jax.experimental.pallas import tpu as pltpu
 from jax.sharding import PartitionSpec as P
+
+MESH = pl.DeviceIdType.MESH
 
 OUTER = 2
 DEGREE = 3
@@ -29,6 +35,134 @@
 OFFSETS = [(0, 0), (1, 0), (0, 1), (2, 0), (0, 2), (1, 1), (1, -1)]
 
 
+def moved(a, dx, dz):
+    n0, n1 = a.shape
+    if dx:
+        row = lax.broadcasted_iota(jnp.int32, a.shape, 0)
+        a = jnp.where((row + dx >= 0) & (row + dx < n0), pltpu.roll(a, (-dx) % n0, 0), 0.0)
+    if dz:
+        col = lax.broadcasted_iota(jnp.int32, a.shape, 1)
+        a = jnp.where((col + dz >= 0) & (col + dz < n1), pltpu.roll(a, (-dz) % n1, 1), 0.0)
+    return a
+
+
+def cg_body(sn, cn, part, owner, gs, press, crecv, kall, kfull, back, gpad, csend, crecv_sem, ssend, srecv):
+    slab, cross = lax.axis_index("slab"), lax.axis_index("cross")
+    nf, nx, nz = part.shape
+    barrier = pltpu.get_barrier_semaphore()
+    for d in range(1, cn):
+        pl.semaphore_signal(barrier, inc=1, device_id={"cross": lax.rem(cross + d, cn)}, device_id_type=MESH)
+    for d in range(1, sn):
+        pl.semaphore_signal(barrier, inc=1, device_id={"slab": lax.rem(slab + d, sn)}, device_id_type=MESH)
+    pl.semaphore_wait(barrier, cn - 1 + sn - 1)
+    copies = []
+    for d in range(1, cn):
+        copy = pltpu.make_async_remote_copy(
+            src_ref=part, dst_ref=crecv.at[cross], send_sem=csend.at[d - 1], recv_sem=crecv_sem.at[d - 1],
+            device_id={"cross": lax.rem(cross + d, cn)}, device_id_type=MESH,
+        )
+        copy.start()
+        copies.append(copy)
+    crecv[cross] = part[...]
+    for copy in copies:
+        copy.wait()
+    for n in range(nf):
+        total = crecv[0, n]
+        for d in range(1, cn):
+            total = total + crecv[d, n]
+        kall[slab, n] = total
+    copies = []
+    for d in range(1, sn):
+        copy = pltpu.make_async_remote_copy(
+            src_ref=kall.at[slab], dst_ref=kall.at[slab], send_sem=ssend.at[d - 1], recv_sem=srecv.at[d - 1],
+            device_id={"slab": lax.rem(slab + d, sn)}, device_id_type=MESH,
+        )
+        copy.start()
+        copies.append(copy)
+    for copy in copies:
+        copy.wait()
+    for n in range(nf):
+        for s in range(sn):
+            kfull[n, s * nx : (s + 1) * nx, :] = kall[s, n]
+    for n, o in enumerate(OFFSETS[1:]):
+        back[n] = moved(kfull[n + 1], -o[0], -o[1])
+
+    def diverge(cx, cz):
+        return cx - moved(cx, -1, 0) + cz - moved(cz, 0, -1)
+
+    def kapply(q):
+        out = kfull[0] * q
+        for n, o in enumerate(OFFSETS[1:]):
+            out = out + kfull[n + 1] * moved(q, o[0], o[1]) + back[n] * moved(q, -o[0], -o[1])
+        return out
+
+    def grad(q):
+        return q - moved(q, 1, 0), q - moved(q, 0, 1)
+
+    target = diverge(kfull[nf - 2], kfull[nf - 1])
+    pressure = jnp.zeros_like(target)
+    resid = dirn = target
+    rr = jnp.sum(resid * resid)
+    for step in range(OUTER):
+        gx, gz = grad(dirn)
+        image = diverge(kapply(gx), kapply(gz))
+        alpha = rr / jnp.sum(dirn * image)
+        pressure = pressure + alpha * dirn
+        if step + 1 < OUTER:
+            resid = resid - alpha * image
+            fresh = jnp.sum(resid * resid)
+            dirn = resid + (fresh / rr) * dirn
+            rr = fresh
+    zero = jnp.zeros((8, nz), jnp.float32)
+    full = sn * nx
+    for c, q in enumerate(grad(pressure)):
+        for dz in range(-2, 3):
+            gpad[dz + 2, c, 0:8, :] = zero
+            gpad[dz + 2, c, full + 8 : full + 16, :] = zero
+            gpad[dz + 2, c, 8 : full + 8, :] = moved(q, 0, dz)
+    kfull[0] = pressure
+    width = press.shape[1]
+    slot = lax.broadcasted_iota(jnp.int32, (width, nz), 0) + cross * width
+    onehot = (jnp.broadcast_to(owner[...], (width, nz)) == slot).astype(jnp.float32)
+    for s in range(sn):
+
+        @pl.when(slab == s)
+        def _():
+            gs[...] = gpad[:, :, 6 + s * nx : 10 + (s + 1) * nx, :]
+            press[...] = lax.dot_general(
+                kfull[0, s * nx : (s + 1) * nx, :], onehot, (((1,), (1,)), ((), ())),
+                precision=lax.Precision.HIGHEST, preferred_element_type=jnp.float32,
+            )
+
+
+def column_cg(part, owner, sn, cn):
+    nf, nx, nz = part.shape
+    f32 = jnp.float32
+    vmem = pl.BlockSpec(memory_space=pltpu.VMEM)
+    return pl.pallas_call(
+        functools.partial(cg_body, sn, cn),
+        out_shape=(
+            jax.ShapeDtypeStruct((5, 2, nx + 4, nz), f32),
+            jax.ShapeDtypeStruct((nx, nz // cn), f32),
+        ),
+        in_specs=[vmem, vmem],
+        out_specs=(vmem, vmem),
+        scratch_shapes=[
+            pltpu.VMEM((cn, nf, nx, nz), f32),
+            pltpu.VMEM((sn, nf, nx, nz), f32),
+            pltpu.VMEM((nf, sn * nx, nz), f32),
+            pltpu.VMEM((nf - 3, sn * nx, nz), f32),
+            pltpu.VMEM((5, 2, sn * nx + 16, nz), f32),
+            pltpu.SemaphoreType.DMA((cn - 1,)),
+            pltpu.SemaphoreType.DMA((cn - 1,)),
+            pltpu.SemaphoreType.DMA((sn - 1,)),
+            pltpu.SemaphoreType.DMA((sn - 1,)),
+        ],
+        compiler_params=pltpu.CompilerParams(collective_id=0, has_side_effects=True),
+        name="column_cg",
+    )(part, owner)
+
+
 def with_halo(cells, axis, dim, width):
     count = lax.axis_size(axis)
     ends = count - 1
@@ -48,19 +182,6 @@
     if s > 0:
         return jnp.pad(a[..., s:], [(0, 0)] * (a.ndim - 1) + [(0, s)])
     return jnp.pad(a[..., :s], [(0, 0)] * (a.ndim - 1) + [(-s, 0)])
-
-
-def rows(a, s):
-    if s == 0:
-        return a
-    if s > 0:
-        return jnp.pad(a[s:], ((0, s), (0, 0)))
-    return jnp.pad(a[:s], ((-s, 0), (0, 0)))
-
-
-def at(a, dx, dz):
-    a = rows(a, dx)
-    return zs(a, dz) if dz else a
 
 
 def shards(forcing, viscosity, owner_slot):
@@ -130,52 +251,13 @@
     m = {o: d0 * a for o, a in acc.items()}
     m[(0, 0)] = m[(0, 0)] + w0 * d0
 
-    part = jnp.stack([jnp.sum(m[o], axis=1) for o in OFFSETS] + [jnp.sum(free[0], 1), jnp.sum(free[1], 1)], 1)
-    whole = lax.psum(part, "cross")
-    whole = lax.all_gather(whole, "slab", axis=0, tiled=True)
-    K = {o: whole[:, n] for n, o in enumerate(OFFSETS)}
-    cx, cz = whole[:, 7], whole[:, 8]
-
-    def diverge(cx, cz):
-        return cx - rows(cx, -1) + cz - zs(cz, -1)
-
-    def grad(q):
-        return q - rows(q, 1), q - zs(q, 1)
-
-    back = {o: at(a, -o[0], -o[1]) for o, a in K.items()}
-
-    def kapply(q):
-        out = K[(0, 0)] * q
-        for o in OFFSETS[1:]:
-            out = out + K[o] * at(q, o[0], o[1]) + back[o] * at(q, -o[0], -o[1])
-        return out
-
-    target = diverge(cx, cz)
-    pressure = jnp.zeros_like(target)
-    resid = dirn = target
-    rr = jnp.sum(resid * resid)
-    for step in range(OUTER):
-        gx, gz = grad(dirn)
-        image = diverge(kapply(gx), kapply(gz))
-        alpha = rr / jnp.sum(dirn * image)
-        pressure = pressure + alpha * dirn
-        if step + 1 < OUTER:
-            resid = resid - alpha * image
-            fresh = jnp.sum(resid * resid)
-            dirn = resid + (fresh / rr) * dirn
-            rr = fresh
-    g = jnp.pad(jnp.stack(grad(pressure)), ((0, 0), (2, 2), (0, 0)))
-    g = lax.dynamic_slice_in_dim(g, slab * nx, nx + 4, 1)
+    part = jnp.stack([jnp.sum(m[o], axis=1) for o in OFFSETS] + [jnp.sum(free[0], 1), jnp.sum(free[1], 1)], 0)
+    gs, pressure = column_cg(part, owner_slot.reshape(1, nz), slab_n, cross_n)
     velocity = free
     for o, a in m.items():
-        s = g[:, 2 + o[0] : 2 + o[0] + nx]
-        s = zs(s, o[1]) if o[1] else s
+        s = gs[2 + o[1], :, 2 + o[0] : 2 + o[0] + nx]
         velocity = velocity - a[None] * s[:, :, None, :]
-    mine = lax.dynamic_slice_in_dim(pressure, slab * nx, nx, 0)
-    width = nz // cross_n
-    cols = cross * width + jnp.arange(width, dtype=jnp.int32)
-    onehot = (owner_slot[:, None] == cols[None, :]).astype(jnp.float32)
-    return velocity, jnp.dot(mine, onehot, precision=lax.Precision.HIGHEST)
+    return velocity, pressure
 
 
 def solution(mesh):

time: 146 us -> 85.3 us (0.58)
  waiting for transfers between devices: 45 us -> 1.15 us
  Pallas kernels: 0 us -> 27.9 us
  between operations: 18.8 us -> 1.02 us
  blocking collectives: 17.5 us -> 0 us
  local copies, waits for them, and re-layouts: 14.5 us -> 9.55 us
  other arithmetic: 26.1 us -> 23.2 us
    psum x1 -> x0, waiting for transfers between devices: 43.9 us -> none  [shards(): whole = lax.psum(part, 'cross')]
    pallas_call x0 -> x1, Pallas kernels: none -> 27.9 us  [column_cg(): pl.pallas_call(functools.partial(cg_body, sn, cn), out_shape=(jax.ShapeDt...]
    all_gather x1 -> x0, blocking collectives: 17.5 us -> none  [shards(): whole = lax.all_gather(whole, 'slab', axis=0, tiled=True)]
    reduce_sum x3 -> x0, other arithmetic: 2.06 us -> none  [the longest x2 1.45 us: shards(): alpha = rr / jnp.sum(dirn * image)]
    slice x4, local copies, waits for them, and re-layouts: 1.83 us -> 0.2 us  [inner(): return a[..., 1:-1, 1:-1, :]]
    slice x23 -> x5, local copies, waits for them, and re-layouts: 3.62 us -> 2.11 us  [zs(): return jnp.pad(a[..., s:], [(0, 0)] * (a.ndim - 1) + [(0, s)])]
  transfers between devices with their start and end apart: 9 -> 8, of which waited for: 2 -> 1; matrix products, arithmetic and copies ran while one was open for 14% -> 21% of each run, Pallas kernels for 0% -> 0%
where the time goes in v2:
time: 85.3 us; the launch traced here: 84.7 us
  Pallas kernels  27.9 us (33%)
  other arithmetic  23.2 us (27%)
  starting transfers between devices  21.9 us (26%)
  local copies, waits for them, and re-layouts  9.55 us (11%)
  waiting for transfers between devices  1.15 us (1%)
  between operations  1.02 us (1%)
    pallas_call x1, Pallas kernels, column_cg(): pl.pallas_call(functools.partial(cg_body, sn, cn), out_shape=(jax.ShapeDt...  27.9 us
    ppermute x4, starting transfers between devices, with_halo(): lax.ppermute(tail, axis, [(i, i + 1) for i in range(ends)])  15.5 us
    reduce_sum x4, other arithmetic, shards(): jnp.sum(m[o], axis=1)  7.76 us
    ppermute x4, starting transfers between devices, with_halo(): lax.ppermute(head, axis, [(i + 1, i) for i in range(ends)])  6.43 us
    sub x1, other arithmetic, shards(): velocity = velocity - a[None] * s[:, :, None, :]  4.74 us
    add x2, other arithmetic, shards(): free = w0 * inner(inner(y0)) + tapply(w1 * inner(y0) + w2 * t1, faces0, d0)  3.22 us
    slice x4, local copies, waits for them, and re-layouts, with_halo(): lax.slice_in_dim(cells, cells.shape[dim] - width, cells.shape[dim], axis=...  3.13 us
    slice x5, local copies, waits for them, and re-layouts, zs(): return jnp.pad(a[..., s:], [(0, 0)] * (a.ndim - 1) + [(0, s)])  2.11 us
  transfers between devices with their start and end apart: 8, of which 1 were waited for; matrix products, arithmetic and copies ran while one was open for 21% of the time, Pallas kernels for 0%

profile of v2, /device:TPU:9, one launch (start us, length us, event | category | flops | bytes accessed | tf_op | source)
XLA Modules:
  0.0 84.7 jit_solution(15771203570883849645)
XLA Ops:
  0.6 0.9 %fusion.85 = (f32[4,3,512]{2,1,0:T(4,128)S(1)}, f32[4,3,512]{2,1,0:T(4,128)S(1)}) fusion(f32[4,64,512]{2,1,0:T(8,128)} %param.4), kind=kLoop, calls=%fused_computation.151 | loop fusion | bytes 98304 | tf_op jit(solution)/shard_map/slice | solution.py:170
  1.5 3.1 %collective-permute-start = (f32[4,3,512]{2,1,0:T(4,128)S(1)}, f32[4,3,512]{2,1,0:T(4,128)S(1)}, u32[]{:S(2)}, u32[]{:S(2)}) collective-permute-start(f32[4,3,512]{2,1,0:T(4,128)S(1)} %get-tuple-element.80), channel_id=1, source_target_pairs={{0,1},{1,2},{2,3},{4,5},{5,6},{6,7},{8,9},{9,10},{10,11},{12,13},{... | collective-permute-start | bytes 73736 | tf_op jit(solution)/shard_map/ppermute | solution.py:173
  4.6 1.3 %collective-permute-start.1 = (f32[4,3,512]{2,1,0:T(4,128)S(1)}, f32[4,3,512]{2,1,0:T(4,128)S(1)}, u32[]{:S(2)}, u32[]{:S(2)}) collective-permute-start(f32[4,3,512]{2,1,0:T(4,128)S(1)} %get-tuple-element.81), channel_id=1, source_target_pairs={{1,0},{2,1},{3,2},{5,4},{6,5},{7,6},{9,8},{10,9},{11,10},{13,12},{... | collective-permute-start | bytes 73736 | tf_op jit(solution)/shard_map/ppermute | solution.py:175
  5.9 1.0 %fusion.78 = (f32[2,4,2,512]{3,2,1,0:T(2,128)S(1)}, f32[2,4,2,512]{3,2,1,0:T(2,128)S(1)}) fusion(f32[2,4,64,512]{3,2,1,0:T(8,128)} %param.3), kind=kLoop, calls=%fused_computation.144 | loop fusion | bytes 131072 | tf_op jit(solution)/shard_map/slice | solution.py:170
  6.9 4.0 %collective-permute-start.4 = (f32[2,4,2,512]{3,2,1,0:T(2,128)S(1)}, f32[2,4,2,512]{3,2,1,0:T(2,128)S(1)}, u32[]{:S(2)}, u32[]{:S(2)}) collective-permute-start(f32[2,4,2,512]{3,2,1,0:T(2,128)S(1)} %get-tuple-element.66), channel_id=1, source_target_pairs={{0,1},{1,2},{2,3},{4,5},{5,6},{6,7},{8,9},{9,10},{10,11},{12,13},{... | collective-permute-start | bytes 98312 | tf_op jit(solution)/shard_map/ppermute | solution.py:173
  10.9 1.3 %collective-permute-start.5 = (f32[2,4,2,512]{3,2,1,0:T(2,128)S(1)}, f32[2,4,2,512]{3,2,1,0:T(2,128)S(1)}, u32[]{:S(2)}, u32[]{:S(2)}) collective-permute-start(f32[2,4,2,512]{3,2,1,0:T(2,128)S(1)} %get-tuple-element.67), channel_id=1, source_target_pairs={{1,0},{2,1},{3,2},{5,4},{6,5},{7,6},{9,8},{10,9},{11,10},{13,12},{... | collective-permute-start | bytes 98312 | tf_op jit(solution)/shard_map/ppermute | solution.py:175
  12.3 0.0 collective-permute-done
  12.3 0.0 collective-permute-done.1
  12.3 1.1 %pad_maximum_fusion.2 = f32[4,70,512]{2,1,0:T(8,128)S(1)} fusion(f32[4,3,512]{2,1,0:T(4,128)S(1)} %collective-permute-done.1, f32[4,64,512]{2,1,0:T(8,128)} %param.4, f32[4,3,512]{2,1,0:T(4,128)S(1)} %collective-permute-done), kind=kLoop, calls=%fused_computation.52 | loop fusion | flops 286720 | bytes 1146880 | tf_op jit(solution)/shard_map/concatenate | solution.py:171
  13.4 0.0 copy-start
  13.4 0.1 fusion.84
  13.5 4.7 %collective-permute-start.2 = (f32[3,70,512]{2,1,0:T(8,128)S(1)}, f32[3,70,512]{2,1,0:T(8,128)S(1)}, u32[]{:S(2)}, u32[]{:S(2)}) collective-permute-start(f32[3,70,512]{2,1,0:T(8,128)S(1)} %get-tuple-element.78), channel_id=1, source_target_pairs={{0,4},{4,8},{8,12},{12,16},{16,20},{20,24},{24,28},{1,5},{5,9},{9,... | collective-permute-start | bytes 1290248 | tf_op jit(solution)/shard_map/ppermute | solution.py:173
  18.3 1.9 %collective-permute-start.3 = (f32[3,70,512]{2,1,0:T(8,128)S(1)}, f32[3,70,512]{2,1,0:T(8,128)S(1)}, u32[]{:S(2)}, u32[]{:S(2)}) collective-permute-start(f32[3,70,512]{2,1,0:T(8,128)S(1)} %get-tuple-element.79), channel_id=1, source_target_pairs={{4,0},{8,4},{12,8},{16,12},{20,16},{24,20},{28,24},{5,1},{9,5},{13... | collective-permute-start | bytes 1290248 | tf_op jit(solution)/shard_map/ppermute | solution.py:175
  20.2 0.0 collective-permute-done.4
  20.2 0.0 collective-permute-done.5
  20.2 0.0 copy-done
  20.3 0.2 pad_maximum_fusion.1
  20.4 0.0 copy-start.1
  20.4 1.1 %fusion.77 = (f32[2,2,68,512]{3,2,1,0:T(8,128)}, f32[2,2,68,512]{3,2,1,0:T(8,128)}) fusion(f32[2,4,68,512]{3,2,1,0:T(8,128)S(1)} %pad_maximum_fusion.1), kind=kLoop, calls=%fused_computation.143 | loop fusion | bytes 2228224 | tf_op jit(solution)/shard_map/slice | solution.py:170
  21.6 3.6 %collective-permute-start.6 = (f32[2,2,68,512]{3,2,1,0:T(8,128)}, f32[2,2,68,512]{3,2,1,0:T(8,128)}, u32[]{:S(2)}, u32[]{:S(2)}) collective-permute-start(f32[2,2,68,512]{3,2,1,0:T(8,128)} %get-tuple-element.64), channel_id=1, source_target_pairs={{0,4},{4,8},{8,12},{12,16},{16,20},{20,24},{24,28},{1,5},{5,9},{9,... | collective-permute-start | bytes 1671176 | tf_op jit(solution)/shard_map/ppermute | solution.py:173
  25.2 1.9 %collective-permute-start.7 = (f32[2,2,68,512]{3,2,1,0:T(8,128)}, f32[2,2,68,512]{3,2,1,0:T(8,128)}, u32[]{:S(2)}, u32[]{:S(2)}) collective-permute-start(f32[2,2,68,512]{3,2,1,0:T(8,128)} %get-tuple-element.65), channel_id=1, source_target_pairs={{4,0},{8,4},{12,8},{16,12},{20,16},{24,20},{28,24},{5,1},{9,5},{13... | collective-permute-start | bytes 1671176 | tf_op jit(solution)/shard_map/ppermute | solution.py:175
  27.2 0.0 collective-permute-done.2
  27.2 1.1 %collective-permute-done.3 = f32[3,70,512]{2,1,0:T(8,128)S(1)} collective-permute-done((f32[3,70,512]{2,1,0:T(8,128)S(1)}, f32[3,70,512]{2,1,0:T(8,128)S(1)}, u32[]{:S(2)}, u32[]{:S(2)}) %collective-permute-start.3) | collective-permute-done | bytes 430112 | tf_op jit(solution)/shard_map/ppermute | solution.py:175
  28.3 0.0 copy-done.1
  28.3 0.2 pad_maximum_fusion
  28.6 0.5 fusion.75
  29.1 1.4 %divide_select_fusion = (f32[8,68,512]{2,1,0:T(8,128)S(1)}, f32[8,68,512]{2,1,0:T(8,128)S(1)}, f32[8,68,512]{2,1,0:T(8,128)S(1)}, f32[8,68,512]{2,1,0:T(8,128)S(...) fusion(pred[68]{0:T(512)(128)(4,1)S(1)} %get-tuple-element.95, ...), kind=kLoop, calls=%fused_computation.24 | loop fusion | flops 6127616 | bytes 15593360 | tf_op jit(solution)/shard_map/jit(_where)/select_n | solution.py:202
  30.5 0.4 fusion.76
  30.9 1.3 %fusion.24 = (f32[6,66,512]{2,1,0:T(8,128)S(1)}, f32[6,66,512]{2,1,0:T(8,128)S(1)}, f32[6,66,512]{2,1,0:T(8,128)S(1)}, f32[6,66,512]{2,1,0:T(8,128)S(1)}, f32[6,...) fusion(f32[8,68,512]{2,1,0:T(8,128)S(1)} %get-tuple-element.22,, ...), kind=kLoop, calls=%fused_computation.48 | loop fusion | flops 3244032 | bytes 16216992 | tf_op jit(solution)/shard_map/add | solution.py:237
  32.2 0.2 fusion.80
  32.4 0.3 fusion.20
  32.8 0.2 fusion.82
  33.0 1.4 %fusion.65 = (f32[4,512]{1,0:T(4,128)S(1)}, f32[4,64,512]{2,1,0:T(8,128)S(1)}, f32[4,64,512]{2,1,0:T(8,128)S(1)}, f32[4,512]{1,0:T(4,128)S(1)}, f32[4,64,512]{2,1,0:T(8,128)S(1)}, /*index=5*/f32[4,64,512]{2,1,0:T(8,128)}) fusion(f32[6,66,512]{2,1,0:T(8,128)S(1)} %get-tuple-element.59, f32[8,68,512]{2,1,0:T(8,128)S(1)} %get-tuple-element.26, ...), kind=kLoop, calls=%fused_computation.137 | loop fusion | flops 2093056 | bytes 8404992 | tf_op jit(solution)/shard_map/reduce_sum | solution.py:254
  34.5 0.2 fusion.79
  34.7 0.2 fusion.81
  34.9 0.2 fusion.83
  35.2 2.1 %fusion.67 = (f32[4,512]{1,0:T(4,128)S(1)}, f32[4,64,512]{2,1,0:T(8,128)}, f32[4,64,512]{2,1,0:T(8,128)}) fusion(f32[8,68,512]{2,1,0:T(8,128)S(1)} %get-tuple-element.22, f32[4,64,511]{2,1,0:T(8,128)S(1)} %get-tuple-element.73, f32[8,68,512]{2,1,0:T(8,128)S(1)} %get-tuple-element.27, f32[4,64,511]{2,1,0:T(8,128)S(1)} %get-tuple-element.77, ...), kind=kLoop, calls=%fused_computation.138 | loop fusion | flops 2357248 | bytes 8918016 | tf_op jit(solution)/shard_map/reduce_sum | solution.py:254
  37.3 1.9 %fusion.63 = (f32[4,512]{1,0:T(4,128)S(1)}, f32[4,64,512]{2,1,0:T(8,128)}, f32[4,64,512]{2,1,0:T(8,128)}, f32[4,512]{1,0:T(4,128)S(1)}, f32[4,64,512]{2,1,0:T(8,128)}, /*index=5*/f32[4,64,512]{2,1,0:T(8,128)S(1)}) fusion(f32[6,66,512]{2,1,0:T(8,128)S(1)} %get-tuple-element.55, f32[8,68,512]{2,1,0:T(8,128)S(1)} %get-tuple-element.26, ...), kind=kLoop, calls=%fused_computation.136 | loop fusion | flops 2093056 | bytes 8401920 | tf_op jit(solution)/shard_map/reduce_sum | solution.py:254
  39.2 2.3 %fusion.56 = (f32[4,512]{1,0:T(4,128)S(1)}, f32[4,64,512]{2,1,0:T(8,128)}, f32[4,64,512]{2,1,0:T(8,128)}, f32[4,512]{1,0:T(4,128)S(1)}, f32[4,64,512]{2,1,0:T(8,128)}, /*index=5*/f32[4,64,512]{2,1,0:T(8,128)}) fusion(f32[6,66,512]{2,1,0:T(8,128)S(1)} %get-tuple-element.53, f32[8,68,512]{2,1,0:T(8,128)S(1)} %get-tuple-element.24, ...), kind=kLoop, calls=%fused_computation.132 | loop fusion | flops 2093056 | bytes 8401920 | tf_op jit(solution)/shard_map/reduce_sum | solution.py:254
  41.5 0.1 slice.440
  41.6 0.1 slice.442
  41.7 0.1 slice.444
  41.7 0.1 slice.446
  41.8 1.0 %multiply_multiply_fusion.2 = (f32[4,64,512]{2,1,0:T(8,128)}, f32[4,64,512]{2,1,0:T(8,128)S(1)}) fusion(f32[4,64,511]{2,1,0:T(8,128)S(1)} %get-tuple-element.72, f32[8,68,512]{2,1,0:T(8,128)S(1)} %get-tuple-element.28, f32[8,68,512]{2,1,0:T(8,128)S(1)} %get-tuple-element.22), kind=kLoop, calls=%fused_computation.104 | loop fusion | flops 262144 | bytes 2620416 | tf_op jit(solution)/shard_map/mul | solution.py:251
  42.8 0.0 collective-permute-done.6
  42.8 0.0 collective-permute-done.7
  42.8 1.7 %maximum_multiply_fusion = f32[2,8,68,512]{3,2,1,0:T(8,128)S(1)} fusion(f32[2,2,68,512]{3,2,1,0:T(8,128)} %collective-permute-done.7, f32[2,4,2,512]{3,2,1,0:T(2,128)S(1)} %collective-permute-done.5, f32[2,4,64,512]{3,2,1,0:T(8,128)S(1)} %copy-done, f32[2,4,2,512]{3,2,1,0:T(2,128)S(1)} %collective-permute-done.4, f32[2,2,68,512]{3,2,1,0:T(8,128)} %collective-permute-done.6, ...), kind=kLoop, calls=%fused_computation | loop fusion | flops 2785280 | bytes 5570560 | tf_op jit(solution)/shard_map/mul | solution.py:224
  44.5 0.8 fusion.73
  45.3 2.1 %fusion.5 = f32[2,6,66,512]{3,2,1,0:T(8,128)S(1)} fusion(f32[2,8,68,512]{3,2,1,0:T(8,128)S(1)} %maximum_multiply_fusion, f32[2,6,66,511]{3,2,1,0:T(8,128)S(1)} %get-tuple-element.41, f32[2,6,66,511]{3,2,1,0:T(8,128)S(1)} %get-tuple-element.40, f32[6,66,512]{2,1,0:T(8,128)S(1)} %get-tuple-element.54, f32[6,66,512]{2,1,0:T(8,128)S(1)} %get-tuple-element.56, ...), kind=kLoop, calls=%fused_computation.7 | loop fusion | flops 6082560 | bytes 18646848 | tf_op jit(solution)/shard_map/add | solution.py:226
  47.4 0.0 copy-start.3
  47.4 0.5 fusion.74
  47.9 0.6 copy-done.3
  48.5 1.1 %fusion.16 = f32[2,4,64,512]{3,2,1,0:T(8,128)S(1)} fusion(f32[2,6,66,512]{3,2,1,0:T(8,128)S(1)} %fusion.5, f32[2,8,68,512]{3,2,1,0:T(8,128)S(1)} %maximum_multiply_fusion, f32[2,4,64,511]{3,2,1,0:T(8,128)S(1)} %get-tuple-element.43, f32[2,4,64,511]{3,2,1,0:T(8,128)S(1)} %get-tuple-element.42, f32[4,64,512]{2,1,0:T(8,128)S(1)} %get-tuple-element.49, ...), kind=kLoop, calls=%fused_computation.32 | loop fusion | flops 3670016 | bytes 12054528 | tf_op jit(solution)/shard_map/add | solution.py:226
  49.6 0.0 copy-start.2
  49.6 0.1 slice_reduce_fusion
  49.8 0.0 copy-start.4
  49.8 0.6 copy-done.4
  50.4 27.9 %column_cg.1 = (f32[5,2,8,512]{3,2,1,0:T(8,128)}, f32[4,128]{1,0:T(4,128)}) custom-call(f32[9,4,512]{2,1,0:T(4,128)} %copy-done.4, s32[1,512]{1,0:T(1,128)} %bitcast.45), custom_call_target="tpu_custom_call" | custom-call | tf_op jit(solution)/shard_map/column_cg/pallas_call | solution.py:142
  78.3 1.0 %slice_bitcast_fusion.12 = (f32[2,4,512]{2,1,0:T(4,128)S(1)}, f32[2,4,512]{2,1,0:T(4,128)S(1)}, f32[2,4,512]{2,1,0:T(4,128)S(1)}, f32[2,4,512]{2,1,0:T(4,128)S(1...) fusion(f32[5,2,8,512]{3,2,1,0:T(8,128)} %get-tuple-element.4), kind=kLoop, calls=%fused_computation.127 | loop fusion | bytes 425984 | tf_op jit(solution)/shard_map/mul | solution.py:259
  79.3 0.0 copy-done.2
  79.4 0.0 copy-start.5
  79.4 4.7 %multiply_subtract_fusion = f32[2,4,64,512]{3,2,1,0:T(8,128)} fusion(f32[2,4,64,512]{3,2,1,0:T(8,128)S(1)} %fusion.16, f32[2,4,512]{2,1,0:T(4,128)S(1)} %get-tuple-element.83, f32[4,64,512]{2,1,0:T(8,128)} %get-tuple-element.48, f32[2,4,512]{2,1,0:T(4,128)S(1)} %get-tuple-element.84, f32[4,64,512]{2,1,0:T(8,128)} %get-tuple-element.39, ...), kind=kLoop, calls=%fused_computation.39 | loop fusion | flops 6815744 | bytes 9125888 | tf_op jit(solution)/shard_map/sub | solution.py:259
  84.1 0.0 copy-done.5
  84.1 0.6 copy.14
  (11 shorter events, 0.1 us)
Async XLA Ops:
  1.5 10.7 %collective-permute-start = (f32[4,3,512]{2,1,0:T(4,128)S(1)}, f32[4,3,512]{2,1,0:T(4,128)S(1)}, u32[]{:S(2)}, u32[]{:S(2)}) collective-permute-start(f32[4,3,512]{2,1,0:T(4,128)S(1)} %get-tuple-element.80), channel_id=1, source_target_pairs={{0,1},{1,2},{2,3},{4,5},{5,6},{6,7},{8,9},{9,10},{10,11},{12,13},{... | collective-permute-start | bytes 73736 | tf_op jit(solution)/shard_map/ppermute | solution.py:173
  4.6 7.6 %collective-permute-start.1 = (f32[4,3,512]{2,1,0:T(4,128)S(1)}, f32[4,3,512]{2,1,0:T(4,128)S(1)}, u32[]{:S(2)}, u32[]{:S(2)}) collective-permute-start(f32[4,3,512]{2,1,0:T(4,128)S(1)} %get-tuple-element.81), channel_id=1, source_target_pairs={{1,0},{2,1},{3,2},{5,4},{6,5},{7,6},{9,8},{10,9},{11,10},{13,12},{... | collective-permute-start | bytes 73736 | tf_op jit(solution)/shard_map/ppermute | solution.py:175
  6.9 13.3 %collective-permute-start.4 = (f32[2,4,2,512]{3,2,1,0:T(2,128)S(1)}, f32[2,4,2,512]{3,2,1,0:T(2,128)S(1)}, u32[]{:S(2)}, u32[]{:S(2)}) collective-permute-start(f32[2,4,2,512]{3,2,1,0:T(2,128)S(1)} %get-tuple-element.66), channel_id=1, source_target_pairs={{0,1},{1,2},{2,3},{4,5},{5,6},{6,7},{8,9},{9,10},{10,11},{12,13},{... | collective-permute-start | bytes 98312 | tf_op jit(solution)/shard_map/ppermute | solution.py:173
  10.9 9.3 %collective-permute-start.5 = (f32[2,4,2,512]{3,2,1,0:T(2,128)S(1)}, f32[2,4,2,512]{3,2,1,0:T(2,128)S(1)}, u32[]{:S(2)}, u32[]{:S(2)}) collective-permute-start(f32[2,4,2,512]{3,2,1,0:T(2,128)S(1)} %get-tuple-element.67), channel_id=1, source_target_pairs={{1,0},{2,1},{3,2},{5,4},{6,5},{7,6},{9,8},{10,9},{11,10},{13,12},{... | collective-permute-start | bytes 98312 | tf_op jit(solution)/shard_map/ppermute | solution.py:175
  13.4 6.8 %copy-start = (f32[2,4,64,512]{3,2,1,0:T(8,128)S(1)}, f32[2,4,64,512]{3,2,1,0:T(8,128)}, u32[]{:S(2)}) copy-start(f32[2,4,64,512]{3,2,1,0:T(8,128)} %param.3) | copy-start | bytes 3145732
  13.5 13.6 %collective-permute-start.2 = (f32[3,70,512]{2,1,0:T(8,128)S(1)}, f32[3,70,512]{2,1,0:T(8,128)S(1)}, u32[]{:S(2)}, u32[]{:S(2)}) collective-permute-start(f32[3,70,512]{2,1,0:T(8,128)S(1)} %get-tuple-element.78), channel_id=1, source_target_pairs={{0,4},{4,8},{8,12},{12,16},{16,20},{20,24},{24,28},{1,5},{5,9},{9,... | collective-permute-start | bytes 1290248 | tf_op jit(solution)/shard_map/ppermute | solution.py:173
  18.3 10.0 %collective-permute-start.3 = (f32[3,70,512]{2,1,0:T(8,128)S(1)}, f32[3,70,512]{2,1,0:T(8,128)S(1)}, u32[]{:S(2)}, u32[]{:S(2)}) collective-permute-start(f32[3,70,512]{2,1,0:T(8,128)S(1)} %get-tuple-element.79), channel_id=1, source_target_pairs={{4,0},{8,4},{12,8},{16,12},{20,16},{24,20},{28,24},{5,1},{9,5},{13... | collective-permute-start | bytes 1290248 | tf_op jit(solution)/shard_map/ppermute | solution.py:175
  20.4 7.9 %copy-start.1 = (f32[4,64,512]{2,1,0:T(8,128)S(1)}, f32[4,64,512]{2,1,0:T(8,128)}, u32[]{:S(2)}) copy-start(f32[4,64,512]{2,1,0:T(8,128)} %param.4) | copy-start | bytes 1572868
  21.6 21.2 %collective-permute-start.6 = (f32[2,2,68,512]{3,2,1,0:T(8,128)}, f32[2,2,68,512]{3,2,1,0:T(8,128)}, u32[]{:S(2)}, u32[]{:S(2)}) collective-permute-start(f32[2,2,68,512]{3,2,1,0:T(8,128)} %get-tuple-element.64), channel_id=1, source_target_pairs={{0,4},{4,8},{8,12},{12,16},{16,20},{20,24},{24,28},{1,5},{5,9},{9,... | collective-permute-start | bytes 1671176 | tf_op jit(solution)/shard_map/ppermute | solution.py:173
  25.2 17.6 %collective-permute-start.7 = (f32[2,2,68,512]{3,2,1,0:T(8,128)}, f32[2,2,68,512]{3,2,1,0:T(8,128)}, u32[]{:S(2)}, u32[]{:S(2)}) collective-permute-start(f32[2,2,68,512]{3,2,1,0:T(8,128)} %get-tuple-element.65), channel_id=1, source_target_pairs={{4,0},{8,4},{12,8},{16,12},{20,16},{24,20},{28,24},{5,1},{9,5},{13... | collective-permute-start | bytes 1671176 | tf_op jit(solution)/shard_map/ppermute | solution.py:175
  47.4 1.0 %copy-start.3 = (f32[4,64,512]{2,1,0:T(8,128)S(1)}, f32[4,64,512]{2,1,0:T(8,128)}, u32[]{:S(2)}) copy-start(f32[4,64,512]{2,1,0:T(8,128)} %get-tuple-element.47) | copy-start | bytes 1572868
  49.6 29.8 %copy-start.2 = (f32[4,64,512]{2,1,0:T(8,128)S(1)}, f32[4,64,512]{2,1,0:T(8,128)}, u32[]{:S(2)}) copy-start(f32[4,64,512]{2,1,0:T(8,128)} %get-tuple-element.21) | copy-start | bytes 1572868
  49.8 0.6 copy-start.4
  79.4 4.8 %copy-start.5 = (f32[4,128]{1,0:T(4,128)S(1)}, f32[4,128]{1,0:T(4,128)}, u32[]{:S(2)}) copy-start(f32[4,128]{1,0:T(4,128)} %get-tuple-element.100) | copy-start | bytes 6148

commit v3 on v2

--- a/solution.py
+++ b/solution.py
@@ -52,9 +52,15 @@
     barrier = pltpu.get_barrier_semaphore()
     for d in range(1, cn):
         pl.semaphore_signal(barrier, inc=1, device_id={"cross": lax.rem(cross + d, cn)}, device_id_type=MESH)
-    for d in range(1, sn):
-        pl.semaphore_signal(barrier, inc=1, device_id={"slab": lax.rem(slab + d, sn)}, device_id_type=MESH)
-    pl.semaphore_wait(barrier, cn - 1 + sn - 1)
+    zn = sn // 2
+    place, core = slab // 2, lax.rem(slab, 2)
+    for d in range(1, zn):
+        pl.semaphore_signal(
+            barrier, inc=1, device_id={"slab": lax.rem(place + d, zn) * 2 + core}, device_id_type=MESH
+        )
+    partner = place * 2 + 1 - core
+    pl.semaphore_signal(barrier, inc=1, device_id={"slab": partner}, device_id_type=MESH)
+    pl.semaphore_wait(barrier, cn - 1 + zn)
     copies = []
     for d in range(1, cn):
         copy = pltpu.make_async_remote_copy(
@@ -71,16 +77,23 @@
         for d in range(1, cn):
             total = total + crecv[d, n]
         kall[slab, n] = total
-    copies = []
-    for d in range(1, sn):
+    def pass_on(block, target, sem):
         copy = pltpu.make_async_remote_copy(
-            src_ref=kall.at[slab], dst_ref=kall.at[slab], send_sem=ssend.at[d - 1], recv_sem=srecv.at[d - 1],
-            device_id={"slab": lax.rem(slab + d, sn)}, device_id_type=MESH,
+            src_ref=kall.at[block], dst_ref=kall.at[block], send_sem=ssend.at[sem], recv_sem=srecv.at[sem],
+            device_id={"slab": target}, device_id_type=MESH,
         )
         copy.start()
-        copies.append(copy)
-    for copy in copies:
+        return copy
+
+    far = [pass_on(slab, lax.rem(place + d, zn) * 2 + core, d - 1) for d in range(1, zn)]
+    near = [pass_on(slab, partner, zn - 1)]
+    for d in range(1, zn):
+        far[d - 1].wait_recv()
+        near.append(pass_on(lax.rem(place - d + zn, zn) * 2 + core, partner, zn - 1 + d))
+    for copy in near:
         copy.wait()
+    for copy in far:
+        copy.wait_send()
     for n in range(nf):
         for s in range(sn):
             kfull[n, s * nx : (s + 1) * nx, :] = kall[s, n]
@@ -163,19 +176,160 @@
     )(part, owner)
 
 
-def with_halo(cells, axis, dim, width):
-    count = lax.axis_size(axis)
-    ends = count - 1
-    head = lax.slice_in_dim(cells, 0, width, axis=dim)
-    tail = lax.slice_in_dim(cells, cells.shape[dim] - width, cells.shape[dim], axis=dim)
-    return jnp.concatenate(
-        [
-            lax.ppermute(tail, axis, [(i, i + 1) for i in range(ends)]),
-            cells,
-            lax.ppermute(head, axis, [(i + 1, i) for i in range(ends)]),
-        ],
-        axis=dim,
-    )
+def halo_body(sn, cn, visc, forc, ypack, vx, fx, yp, cp, send, recv):
+    slab, cross = lax.axis_index("slab"), lax.axis_index("cross")
+    nx = visc.shape[0]
+    sides = (("slab", slab - 1, slab > 0), ("slab", slab + 1, slab < sn - 1))
+    walls = (("cross", cross - 1, cross > 0), ("cross", cross + 1, cross < cn - 1))
+    barrier = pltpu.get_barrier_semaphore()
+    for axis, peer, there in sides + walls:
+
+        @pl.when(there)
+        def _():
+            pl.semaphore_signal(barrier, inc=1, device_id={axis: peer}, device_id_type=MESH)
+
+    around = [jnp.where(there, 1, 0) for axis, peer, there in sides + walls]
+    pl.semaphore_wait(barrier, around[0] + around[1] + around[2] + around[3])
+
+    def x_copies(s):
+        axis, peer, there = sides[s]
+        v0, f0 = (0, 0) if s == 0 else (nx - 3, nx - 2)
+        pairs = ((visc.at[pl.ds(v0, 3)], vx.at[1 - s]), (forc.at[:, pl.ds(f0, 2)], fx.at[1 - s]))
+        return [
+            pltpu.make_async_remote_copy(
+                src_ref=a, dst_ref=b, send_sem=send.at[2 * s + n], recv_sem=recv.at[2 * (1 - s) + n],
+                device_id={axis: peer}, device_id_type=MESH,
+            )
+            for n, (a, b) in enumerate(pairs)
+        ]
+
+    def y_copy(w):
+        axis, peer, there = walls[w]
+        return pltpu.make_async_remote_copy(
+            src_ref=ypack.at[w], dst_ref=yp.at[1 - w], send_sem=send.at[4 + w], recv_sem=recv.at[4 + 1 - w],
+            device_id={axis: peer}, device_id_type=MESH,
+        )
+
+    def corner_copy(w, s):
+        axis, peer, there = sides[s]
+        return pltpu.make_async_remote_copy(
+            src_ref=yp.at[w], dst_ref=cp.at[1 - s, w], send_sem=send.at[6 + 2 * w + s],
+            recv_sem=recv.at[6 + 2 * w + 1 - s], device_id={axis: peer}, device_id_type=MESH,
+        )
+
+    def y_in(w):
+        return pltpu.make_async_remote_copy(
+            src_ref=ypack.at[w], dst_ref=yp.at[w], send_sem=send.at[4 + w], recv_sem=recv.at[4 + w],
+            device_id={"cross": walls[w][1]}, device_id_type=MESH,
+        )
+
+    def corner_in(w, s):
+        return pltpu.make_async_remote_copy(
+            src_ref=yp.at[w], dst_ref=cp.at[s, w], send_sem=send.at[6 + 2 * w + s],
+            recv_sem=recv.at[6 + 2 * w + s], device_id={"slab": sides[s][1]}, device_id_type=MESH,
+        )
+
+    def x_in(s):
+        pairs = ((visc.at[pl.ds(0, 3)], vx.at[s]), (forc.at[:, pl.ds(0, 2)], fx.at[s]))
+        return [
+            pltpu.make_async_remote_copy(
+                src_ref=a, dst_ref=b, send_sem=send.at[2 * s + n], recv_sem=recv.at[2 * s + n],
+                device_id={"slab": sides[s][1]}, device_id_type=MESH,
+            )
+            for n, (a, b) in enumerate(pairs)
+        ]
+
+    for w in range(2):
+
+        @pl.when(walls[w][2])
+        def _():
+            y_copy(w).start()
+
+    for s in range(2):
+
+        @pl.when(sides[s][2])
+        def _():
+            for copy in x_copies(s):
+                copy.start()
+
+    for w in range(2):
+
+        @pl.when(walls[w][2])
+        def _():
+            y_in(w).wait_recv()
+            for s in range(2):
+
+                @pl.when(sides[s][2])
+                def _():
+                    corner_copy(w, s).start()
+
+    for s in range(2):
+
+        @pl.when(sides[s][2])
+        def _():
+            for copy in x_in(s):
+                copy.wait_recv()
+            for copy in x_copies(s):
+                copy.wait_send()
+
+    for w in range(2):
+
+        @pl.when(walls[w][2])
+        def _():
+            y_copy(w).wait_send()
+            for s in range(2):
+
+                @pl.when(sides[s][2])
+                def _():
+                    corner_in(w, s).wait_recv()
+                    corner_copy(w, s).wait_send()
+
+
+def halos(viscosity, forcing, sn, cn):
+    nx, ny, nz = viscosity.shape
+    f32 = jnp.float32
+
+    def packed(v0, f0):
+        a = viscosity[:, v0 : v0 + 3].reshape(3 * nx, nz)
+        b = forcing[:, :, f0 : f0 + 2].reshape(4 * nx, nz)
+        return jnp.concatenate([a, b], 0)
+
+    ypack = jnp.stack([packed(0, 0), packed(ny - 3, ny - 2)])
+    anywhere = pl.BlockSpec(memory_space=pl.ANY)
+    vx, fx, yp, cp = pl.pallas_call(
+        functools.partial(halo_body, sn, cn),
+        out_shape=(
+            jax.ShapeDtypeStruct((2, 3, ny, nz), f32),
+            jax.ShapeDtypeStruct((2, 2, 2, ny, nz), f32),
+            jax.ShapeDtypeStruct((2, 7 * nx, nz), f32),
+            jax.ShapeDtypeStruct((2, 2, 7 * nx, nz), f32),
+        ),
+        in_specs=[anywhere] * 3,
+        out_specs=(anywhere,) * 4,
+        scratch_shapes=[pltpu.SemaphoreType.DMA((10,)), pltpu.SemaphoreType.DMA((10,))],
+        compiler_params=pltpu.CompilerParams(collective_id=1, has_side_effects=True),
+        name="halos",
+    )(viscosity, forcing, ypack)
+    slab, cross = lax.axis_index("slab"), lax.axis_index("cross")
+    side = (slab > 0, slab < sn - 1)
+    wall = (cross > 0, cross < cn - 1)
+
+    def only(cond, a):
+        return jnp.where(cond, a, 0.0)
+
+    def unpacked(p):
+        return p[: 3 * nx].reshape(nx, 3, nz), p[3 * nx :].reshape(2, nx, 2, nz)
+
+    yv, yf = zip(*[unpacked(only(wall[w], yp[w])) for w in range(2)])
+    vs, fs = [jnp.concatenate([yv[0], viscosity, yv[1]], 1)], [jnp.concatenate([yf[0], forcing, yf[1]], 2)]
+    for s in range(2):
+        cv, cf = zip(*[unpacked(only(side[s] & wall[w], cp[s, w])) for w in range(2)])
+        vcut, fcut = ((nx - 3, nx), (nx - 2, nx)) if s == 0 else ((0, 3), (0, 2))
+        cv = [a[vcut[0] : vcut[1]] for a in cv]
+        cf = [a[:, fcut[0] : fcut[1]] for a in cf]
+        vs.append(jnp.concatenate([cv[0], only(side[s], vx[s]), cv[1]], 1))
+        fs.append(jnp.concatenate([cf[0], only(side[s], fx[s]), cf[1]], 2))
+    return jnp.concatenate([vs[1], vs[0], vs[2]], 0), jnp.concatenate([fs[1], fs[0], fs[2]], 1)
 
 
 def zs(a, s):
@@ -189,8 +343,7 @@
     slab_n, cross_n = lax.axis_size("slab"), lax.axis_size("cross")
     slab, cross = lax.axis_index("slab"), lax.axis_index("cross")
     nx, ny, nz = viscosity.shape
-    v = with_halo(with_halo(viscosity, "cross", 1, 3), "slab", 0, 3)
-    f = with_halo(with_halo(forcing, "cross", 2, 2), "slab", 1, 2)
+    v, f = halos(viscosity, forcing, slab_n, cross_n)
     c = v[1:-1, 1:-1]
     fxp, fxm = 0.5 * (c + v[2:, 1:-1]), 0.5 * (c + v[:-2, 1:-1])
     fyp, fym = 0.5 * (c + v[1:-1, 2:]), 0.5 * (c + v[1:-1, :-2])

time: 85.3 us -> 90.6 us (1.062)
  starting transfers between devices: 21.9 us -> 0 us
  local copies, waits for them, and re-layouts: 9.55 us -> 19.4 us
  other arithmetic: 23.2 us -> 32.1 us
  Pallas kernels: 27.9 us -> 36.5 us
  waiting for transfers between devices: 1.15 us -> 0 us
    ppermute x8 -> x0, starting transfers between devices: 21.9 us -> none  [the longest x4 15.5 us: with_halo(): lax.ppermute(tail, axis, [(i, i + 1) for i in range(ends)])]
    pallas_call x0 -> x1, Pallas kernels: none -> 15.6 us  [halos(): pl.pallas_call(functools.partial(halo_body, sn, cn), out_shape=(jax.Shape...]
    pallas_call x1, Pallas kernels: 27.9 us -> 20.9 us  [column_cg(): pl.pallas_call(functools.partial(cg_body, sn, cn), out_shape=(jax.ShapeDt...]
    slice x4, local copies, waits for them, and re-layouts: 0.2 us -> 4.58 us  [inner(): return a[..., 1:-1, 1:-1, :]]
    select_n x0 -> x4, other arithmetic: none -> 3.47 us  [only(): return jnp.where(cond, a, 0.0)]
    add x1, other arithmetic: 1.34 us -> 3.19 us  [shards(): U[0, 0] = U[0, 0] + w1 * d1]
    unnamed x21 -> x79, local copies, waits for them, and re-layouts: 1.85 us -> 3.65 us
    select_n x1, other arithmetic: 1.39 us -> 2.89 us  [shards(): dinv = jnp.where(inside, 1.0 / jnp.where(inside, diag, 1.0), 0.0)]
  transfers between devices with their start and end apart: 8 -> 0, of which waited for: 1 -> 0; matrix products, arithmetic and copies ran while one was open for 21% -> 0% of each run, Pallas kernels for 0% -> 0%
where the time goes in v3:
time: 90.6 us; the launch traced here: 89.4 us
  Pallas kernels  36.5 us (40%)
  other arithmetic  32.1 us (35%)
  local copies, waits for them, and re-layouts  19.4 us (21%)
  between operations  1.43 us (2%)
    pallas_call x1, Pallas kernels, column_cg(): pl.pallas_call(functools.partial(cg_body, sn, cn), out_shape=(jax.ShapeDt...  20.9 us
    pallas_call x1, Pallas kernels, halos(): pl.pallas_call(functools.partial(halo_body, sn, cn), out_shape=(jax.Shape...  15.6 us
    reduce_sum x4, other arithmetic, shards(): jnp.sum(m[o], axis=1)  8.42 us
    sub x1, other arithmetic, shards(): velocity = velocity - a[None] * s[:, :, None, :]  4.74 us
    slice x4, local copies, waits for them, and re-layouts, inner(): return a[..., 1:-1, 1:-1, :]  4.58 us
    unnamed x79, local copies, waits for them, and re-layouts  3.65 us
    select_n x4, other arithmetic, only(): return jnp.where(cond, a, 0.0)  3.47 us
    add x1, other arithmetic, shards(): U[0, 0] = U[0, 0] + w1 * d1  3.19 us

profile of v3, /device:TPU:9, one launch (start us, length us, event | category | flops | bytes accessed | tf_op | source)
XLA Modules:
  0.0 89.4 jit_solution(8601662463674755127)
XLA Ops:
  0.6 0.9 fusion.83
  1.5 1.0 %fusion.77 = (f32[2,4,2,512]{3,2,1,0:T(2,128)S(1)}, f32[2,4,2,512]{3,2,1,0:T(2,128)S(1)}) fusion(f32[2,4,64,512]{3,2,1,0:T(8,128)} %forc.1), kind=kLoop, calls=%fused_computation.154 | loop fusion | bytes 131072 | tf_op jit(solution)/shard_map/slice | solution.py:294
  2.6 0.7 pad_maximum_fusion.ypack
  3.3 15.6 %halos.1 = (f32[2,3,64,512]{3,2,1,0:T(8,128)}, f32[2,2,2,64,512]{4,3,2,1,0:T(8,128)}, f32[2,28,512]{2,1,0:T(8,128)}, f32[2,2,28,512]{3,2,1,0:T(8,128)}) custom-call(f32[4,64,512]{2,1,0:T(8,128)} %visc.1, f32[2,4,64,512]{3,2,1,0:T(8,128)} %forc.1, f32[2,28,512]{2,1,0:T(8,128)} %pad_maximum_fusion.ypack), custom_call_target="tpu_custom_call" | custom-call | tf_op jit(solution)/shard_map/halos/pallas_call | solution.py:299
  18.9 0.0 copy-start.19
  19.0 0.0 copy-start.11
  19.0 1.1 %slice_select_fusion.5 = (f32[1,1,28,512]{3,2,1,0:T(8,128)S(1)}, f32[1,1,28,512]{3,2,1,0:T(8,128)S(1)}, f32[1,1,28,512]{3,2,1,0:T(8,128)S(1)}, f32[1,1,28,512]{3,2,1,0:T(8,128)S(1)}) fusion(f32[2,2,28,512]{3,2,1,0:T(8,128)} %get-tuple-element.8, pred[]{:T(512)S(6)} %and.27, pred[]{:T(512)S(6)} %and.30, pred[]{:T(512)S(6)} %and.29, pred[]{:T(512)S(6)} %and.28), kind=kLoop, calls=%fused_computation.116 | loop fusion | flops 57344 | bytes 458756 | tf_op jit(solution)/shard_map/jit(_where)/select_n | solution.py:318
  20.1 0.7 slice.421
  20.8 0.6 slice.425
  21.4 0.6 slice.432
  22.0 0.6 slice.436
  22.6 0.0 copy-done.24
  22.7 0.0 copy-done.28
  22.7 0.1 select_bitcast_fusion.3
  22.8 0.6 copy-done.22
  23.5 1.0 %maximum_maximum_fusion = f32[10,70,512]{2,1,0:T(8,128)S(1)} fusion(f32[3,3,512]{2,1,0:T(4,128)} %slice.436, f32[3,64,512]{2,1,0:T(8,128)S(1)} %get-tuple-element.87, f32[3,3,512]{2,1,0:T(4,128)} %slice.432, f32[4,3,512]{2,1,0:T(4,128)S(1)} %reshape.151, f32[4,64,512]{2,1,0:T(8,128)S(1)} %copy-done.11, f32[4,3,512]{2,1,0:T(4,128)S(1)} %reshape.150, ...), kind=kLoop, calls=%fused_computation.14 | loop fusion | flops 2867200 | bytes 2867200 | tf_op jit(solution)/shard_map/concatenate | solution.py:332
  24.5 1.9 %fusion.75 = (f32[8,68,511]{2,1,0:T(8,128)}, f32[8,68,511]{2,1,0:T(8,128)}) fusion(f32[10,70,512]{2,1,0:T(8,128)S(1)} %maximum_maximum_fusion), kind=kLoop, calls=%fused_computation.152 | loop fusion | bytes 4447744 | tf_op jit(solution)/shard_map/slice | solution.py:338
  26.5 2.9 %divide_select_fusion = (f32[8,68,512]{2,1,0:T(8,128)S(1)}, f32[8,68,512]{2,1,0:T(8,128)S(1)}, f32[8,68,512]{2,1,0:T(8,128)S(1)}, f32[8,68,512]{2,1,0:T(8,128)S(...) fusion(pred[68]{0:T(512)(128)(4,1)S(1)} %get-tuple-element.111, ...), kind=kLoop, calls=%fused_computation.23 | loop fusion | flops 6127616 | bytes 15593360 | tf_op jit(solution)/shard_map/jit(_where)/select_n | solution.py:355
  29.4 1.5 %fusion.20 = (f32[6,66,512]{2,1,0:T(8,128)S(1)}, f32[6,66,512]{2,1,0:T(8,128)S(1)}, f32[6,66,512]{2,1,0:T(8,128)}) fusion(f32[8,68,512]{2,1,0:T(8,128)S(1)} %get-tuple-element.30, f32[8,68,512]{2,1,0:T(8,128)S(1)} %get-tuple-element.32), kind=kLoop, calls=%fused_computation.42 | loop fusion | flops 608256 | bytes 4866048 | tf_op jit(solution)/shard_map/mul | solution.py:389
  30.9 0.2 fusion.81
  31.1 0.4 fusion.76
  31.5 3.2 %fusion.24 = (f32[6,66,512]{2,1,0:T(8,128)S(1)}, f32[6,66,512]{2,1,0:T(8,128)}, f32[6,66,512]{2,1,0:T(8,128)}, f32[6,66,512]{2,1,0:T(8,128)S(1)}, f32[6,66,512]{...) fusion(f32[8,68,512]{2,1,0:T(8,128)S(1)} %get-tuple-element.30,, ...), kind=kLoop, calls=%fused_computation.47 | loop fusion | flops 3244032 | bytes 16216992 | tf_op jit(solution)/shard_map/add | solution.py:390
  34.7 0.2 fusion.79
  35.0 2.4 %fusion.56 = (f32[4,512]{1,0:T(4,128)S(1)}, f32[4,64,512]{2,1,0:T(8,128)}, f32[4,64,512]{2,1,0:T(8,128)}, f32[4,512]{1,0:T(4,128)S(1)}, f32[4,64,512]{2,1,0:T(8,128)}, /*index=5*/f32[4,64,512]{2,1,0:T(8,128)}) fusion(f32[6,66,512]{2,1,0:T(8,128)S(1)} %get-tuple-element.61, f32[8,68,512]{2,1,0:T(8,128)S(1)} %get-tuple-element.32, ...), kind=kLoop, calls=%fused_computation.143 | loop fusion | flops 2093056 | bytes 8401920 | tf_op jit(solution)/shard_map/reduce_sum | solution.py:407
  37.3 0.2 fusion.80
  37.6 0.2 fusion.82
  37.8 2.1 %fusion.67 = (f32[4,512]{1,0:T(4,128)S(1)}, f32[4,64,512]{2,1,0:T(8,128)}, f32[4,64,512]{2,1,0:T(8,128)}) fusion(f32[8,68,512]{2,1,0:T(8,128)S(1)} %get-tuple-element.30, f32[4,64,511]{2,1,0:T(8,128)S(1)} %get-tuple-element.81, f32[8,68,512]{2,1,0:T(8,128)S(1)} %get-tuple-element.35, f32[4,64,511]{2,1,0:T(8,128)S(1)} %get-tuple-element.85, ...), kind=kLoop, calls=%fused_computation.149 | loop fusion | flops 2357248 | bytes 8918016 | tf_op jit(solution)/shard_map/reduce_sum | solution.py:407
  39.9 0.0 copy-done.3
  39.9 1.9 %fusion.65 = (f32[4,512]{1,0:T(4,128)S(1)}, f32[4,64,512]{2,1,0:T(8,128)}, f32[4,64,512]{2,1,0:T(8,128)}, f32[4,512]{1,0:T(4,128)S(1)}, f32[4,64,512]{2,1,0:T(8,128)}, /*index=5*/f32[4,64,512]{2,1,0:T(8,128)}) fusion(f32[6,66,512]{2,1,0:T(8,128)S(1)} %get-tuple-element.67, f32[8,68,512]{2,1,0:T(8,128)S(1)} %get-tuple-element.34, ...), kind=kLoop, calls=%fused_computation.148 | loop fusion | flops 2093056 | bytes 8404992 | tf_op jit(solution)/shard_map/reduce_sum | solution.py:407
  41.8 0.2 fusion.78
  42.1 0.0 copy-done
  42.1 0.0 copy-done.1
  42.1 0.0 copy-done.2
  42.1 2.1 %fusion.63 = (f32[4,512]{1,0:T(4,128)S(1)}, f32[4,64,512]{2,1,0:T(8,128)}, f32[4,64,512]{2,1,0:T(8,128)}, f32[4,512]{1,0:T(4,128)S(1)}, f32[4,64,512]{2,1,0:T(8,128)}, /*index=5*/f32[4,64,512]{2,1,0:T(8,128)}) fusion(f32[6,66,512]{2,1,0:T(8,128)S(1)} %get-tuple-element.63, f32[8,68,512]{2,1,0:T(8,128)S(1)} %get-tuple-element.34, ...), kind=kLoop, calls=%fused_computation.147 | loop fusion | flops 2093056 | bytes 8401920 | tf_op jit(solution)/shard_map/reduce_sum | solution.py:407
  44.2 1.2 %multiply_multiply_fusion.2 = (f32[4,64,512]{2,1,0:T(8,128)}, f32[4,64,512]{2,1,0:T(8,128)}) fusion(f32[4,64,511]{2,1,0:T(8,128)S(1)} %get-tuple-element.80, f32[8,68,512]{2,1,0:T(8,128)S(1)} %get-tuple-element.36, f32[8,68,512]{2,1,0:T(8,128)S(1)} %get-tuple-element.30), kind=kLoop, calls=%fused_computation.102 | loop fusion | flops 262144 | bytes 2620416 | tf_op jit(solution)/shard_map/mul | solution.py:404
  45.4 0.0 copy-start.4
  45.5 0.6 reshape.152
  46.1 0.0 copy-done.29
  46.1 0.0 slice-start
  46.3 2.3 %select_bitcast_fusion.1 = (f32[2,2,64,512]{3,2,1,0:T(8,128)}, f32[2,2,64,512]{3,2,1,0:T(8,128)}) fusion(f32[2,2,2,64,512]{4,3,2,1,0:T(8,128)} %get-tuple-element.11, pred[]{:T(512)S(6)} %gt.6, pred[]{:T(512)S(6)} %lt.25), kind=kLoop, calls=%fused_computation.105 | loop fusion | flops 262144 | bytes 2097154 | tf_op jit(solution)/shard_map/jit(_where)/select_n | solution.py:318
  48.6 0.0 copy-done.21
  48.7 1.8 %maximum_multiply_fusion = f32[2,8,68,512]{3,2,1,0:T(8,128)S(1)} fusion(f32[2,2,2,512]{3,2,1,0:T(2,128)S(1)} %slice.557, f32[2,2,64,512]{3,2,1,0:T(8,128)} %get-tuple-element.73, f32[2,2,2,512]{3,2,1,0:T(2,128)S(1)} %slice.555, f32[2,4,2,512]{3,2,1,0:T(2,128)S(1)} %reshape.155, f32[2,4,64,512]{3,2,1,0:T(8,128)S(1)} %copy-done.4, ...), kind=kLoop, calls=%fused_computation | loop fusion | flops 5013504 | bytes 5570560 | tf_op jit(solution)/shard_map/mul | solution.py:377
  50.5 0.0 copy-start.6
  50.6 0.8 fusion.73
  51.4 0.3 copy-done.5
  51.7 0.3 copy-done.6
  51.9 0.3 copy-done.7
  52.2 0.3 copy-done.8
  52.5 0.3 copy-done.9
  52.8 0.3 copy-done.10
  53.0 1.9 %fusion.5 = f32[2,6,66,512]{3,2,1,0:T(8,128)S(1)} fusion(f32[2,8,68,512]{3,2,1,0:T(8,128)S(1)} %maximum_multiply_fusion, f32[2,6,66,511]{3,2,1,0:T(8,128)S(1)} %get-tuple-element.49, f32[2,6,66,511]{3,2,1,0:T(8,128)S(1)} %get-tuple-element.48, f32[6,66,512]{2,1,0:T(8,128)S(1)} %copy-done.8, f32[6,66,512]{2,1,0:T(8,128)S(1)} %copy-done.9, ...), kind=kLoop, calls=%fused_computation.7 | loop fusion | flops 6082560 | bytes 18646848 | tf_op jit(solution)/shard_map/add | solution.py:379
  54.9 0.5 fusion.74
  55.4 1.1 %slice.576 = f32[4,64,512]{2,1,0:T(8,128)S(1)} slice(f32[8,68,512]{2,1,0:T(8,128)} %copy-done.3), slice={[2:6], [2:66], [0:512]} | slice | bytes 1048576 | tf_op jit(solution)/shard_map/slice | solution.py:358
  56.5 1.2 %slice.578 = f32[4,64,512]{2,1,0:T(8,128)S(1)} slice(f32[8,68,512]{2,1,0:T(8,128)} %copy-done.2), slice={[2:6], [2:66], [0:512]} | slice | bytes 1048576 | tf_op jit(solution)/shard_map/slice | solution.py:358
  57.8 1.1 %slice.580 = f32[4,64,512]{2,1,0:T(8,128)S(1)} slice(f32[8,68,512]{2,1,0:T(8,128)} %copy-done.1), slice={[2:6], [2:66], [0:512]} | slice | bytes 1048576 | tf_op jit(solution)/shard_map/slice | solution.py:358
  58.9 1.1 %slice.582 = f32[4,64,512]{2,1,0:T(8,128)S(1)} slice(f32[8,68,512]{2,1,0:T(8,128)} %copy-done), slice={[2:6], [2:66], [0:512]} | slice | bytes 1048576 | tf_op jit(solution)/shard_map/slice | solution.py:358
  60.0 1.1 %fusion.16 = f32[2,4,64,512]{3,2,1,0:T(8,128)S(1)} fusion(f32[2,6,66,512]{3,2,1,0:T(8,128)S(1)} %fusion.5, f32[2,8,68,512]{3,2,1,0:T(8,128)S(1)} %maximum_multiply_fusion, f32[2,4,64,511]{3,2,1,0:T(8,128)S(1)} %get-tuple-element.51, f32[2,4,64,511]{3,2,1,0:T(8,128)S(1)} %get-tuple-element.50, f32[4,64,512]{2,1,0:T(8,128)S(1)} %copy-done.18, ...), kind=kLoop, calls=%fused_computation.31 | loop fusion | flops 3670016 | bytes 12054528 | tf_op jit(solution)/shard_map/add | solution.py:379
  61.2 0.1 slice_reduce_fusion
  61.4 0.0 copy-start.33
  61.4 0.6 copy-done.33
  62.0 20.9 %column_cg.1 = (f32[5,2,8,512]{3,2,1,0:T(8,128)}, f32[4,128]{1,0:T(4,128)}) custom-call(f32[9,4,512]{2,1,0:T(4,128)} %copy-done.33, s32[1,512]{1,0:T(1,128)} %bitcast.65), custom_call_target="tpu_custom_call" | custom-call | tf_op jit(solution)/shard_map/column_cg/pallas_call | solution.py:155
  82.9 1.1 %slice_bitcast_fusion.12 = (f32[2,4,512]{2,1,0:T(4,128)S(1)}, f32[2,4,512]{2,1,0:T(4,128)S(1)}, f32[2,4,512]{2,1,0:T(4,128)S(1)}, f32[2,4,512]{2,1,0:T(4,128)S(1...) fusion(f32[5,2,8,512]{3,2,1,0:T(8,128)} %get-tuple-element.12), kind=kLoop, calls=%fused_computation.138 | loop fusion | bytes 425984 | tf_op jit(solution)/shard_map/mul | solution.py:412
  84.1 4.7 %multiply_subtract_fusion = f32[2,4,64,512]{3,2,1,0:T(8,128)} fusion(f32[2,4,64,512]{3,2,1,0:T(8,128)S(1)} %fusion.16, f32[2,4,512]{2,1,0:T(4,128)S(1)} %get-tuple-element.95, f32[4,64,512]{2,1,0:T(8,128)} %get-tuple-element.56, f32[2,4,512]{2,1,0:T(4,128)S(1)} %get-tuple-element.96, f32[4,64,512]{2,1,0:T(8,128)} %get-tuple-element.47, ...), kind=kLoop, calls=%fused_computation.38 | loop fusion | flops 6815744 | bytes 9125888 | tf_op jit(solution)/shard_map/sub | solution.py:412
  88.8 0.6 copy.14
  (89 shorter events, 0.5 us)
Async XLA Ops:
  18.9 3.7 %copy-start.19 = (f32[2,3,64,512]{3,2,1,0:T(8,128)S(1)}, f32[2,3,64,512]{3,2,1,0:T(8,128)}, u32[]{:S(2)}) copy-start(f32[2,3,64,512]{3,2,1,0:T(8,128)} %get-tuple-element.9) | copy-start | bytes 2359300
  19.0 3.8 %copy-start.32 = (f32[2,28,512]{2,1,0:T(8,128)S(1)}, f32[2,28,512]{2,1,0:T(8,128)}, u32[]{:S(2)}) copy-start(f32[2,28,512]{2,1,0:T(8,128)} %get-tuple-element.10) | copy-start | bytes 344068
  19.0 4.5 %copy-start.11 = (f32[4,64,512]{2,1,0:T(8,128)S(1)}, f32[4,64,512]{2,1,0:T(8,128)}, u32[]{:S(2)}) copy-start(f32[4,64,512]{2,1,0:T(8,128)} %visc.1) | copy-start | bytes 1572868
  20.1 2.6 %copy-start.24 = (f32[1,1,28,512]{3,2,1,0:T(8,128)}, f32[1,1,28,512]{3,2,1,0:T(8,128)S(1)}, u32[]{:S(2)}) copy-start(f32[1,1,28,512]{3,2,1,0:T(8,128)S(1)} %get-tuple-element.91) | copy-start | bytes 172036
  20.1 2.6 %copy-start.26 = (f32[1,1,28,512]{3,2,1,0:T(8,128)}, f32[1,1,28,512]{3,2,1,0:T(8,128)S(1)}, u32[]{:S(2)}) copy-start(f32[1,1,28,512]{3,2,1,0:T(8,128)S(1)} %get-tuple-element.92) | copy-start | bytes 172036
  20.1 2.6 %copy-start.28 = (f32[1,1,28,512]{3,2,1,0:T(8,128)}, f32[1,1,28,512]{3,2,1,0:T(8,128)S(1)}, u32[]{:S(2)}) copy-start(f32[1,1,28,512]{3,2,1,0:T(8,128)S(1)} %get-tuple-element.93) | copy-start | bytes 172036
  20.1 2.6 %copy-start.30 = (f32[1,1,28,512]{3,2,1,0:T(8,128)}, f32[1,1,28,512]{3,2,1,0:T(8,128)S(1)}, u32[]{:S(2)}) copy-start(f32[1,1,28,512]{3,2,1,0:T(8,128)S(1)} %get-tuple-element.90) | copy-start | bytes 172036
  22.8 0.6 copy-start.22
  22.8 1.7 %copy-start.20 = (f32[1,28,512]{2,1,0:T(8,128)}, f32[1,28,512]{2,1,0:T(8,128)S(1)}, u32[]{:S(2)}) copy-start(f32[1,28,512]{2,1,0:T(8,128)S(1)} %get-tuple-element.108) | copy-start | bytes 172036
  29.4 10.5 %copy-start.3 = (f32[8,68,512]{2,1,0:T(8,128)}, f32[8,68,512]{2,1,0:T(8,128)S(1)}, u32[]{:S(2)}) copy-start(f32[8,68,512]{2,1,0:T(8,128)S(1)} %get-tuple-element.31) | copy-start | bytes 3342340
  29.4 12.7 %copy-start = (f32[8,68,512]{2,1,0:T(8,128)}, f32[8,68,512]{2,1,0:T(8,128)S(1)}, u32[]{:S(2)}) copy-start(f32[8,68,512]{2,1,0:T(8,128)S(1)} %get-tuple-element.35) | copy-start | bytes 3342340
  29.4 12.7 %copy-start.1 = (f32[8,68,512]{2,1,0:T(8,128)}, f32[8,68,512]{2,1,0:T(8,128)S(1)}, u32[]{:S(2)}) copy-start(f32[8,68,512]{2,1,0:T(8,128)S(1)} %get-tuple-element.34) | copy-start | bytes 3342340
  29.4 12.7 %copy-start.2 = (f32[8,68,512]{2,1,0:T(8,128)}, f32[8,68,512]{2,1,0:T(8,128)S(1)}, u32[]{:S(2)}) copy-start(f32[8,68,512]{2,1,0:T(8,128)S(1)} %get-tuple-element.33) | copy-start | bytes 3342340
  44.2 1.3 %copy-start.31 = (f32[1,1,28,512]{3,2,1,0:T(8,128)S(1)}, f32[1,1,28,512]{3,2,1,0:T(8,128)}, u32[]{:S(2)}) copy-start(f32[1,1,28,512]{3,2,1,0:T(8,128)} %copy-done.30) | copy-start | bytes 172036
  44.2 1.9 %copy-start.29 = (f32[1,1,28,512]{3,2,1,0:T(8,128)S(1)}, f32[1,1,28,512]{3,2,1,0:T(8,128)}, u32[]{:S(2)}) copy-start(f32[1,1,28,512]{3,2,1,0:T(8,128)} %copy-done.28) | copy-start | bytes 172036
  44.2 1.9 %copy-start.27 = (f32[1,1,28,512]{3,2,1,0:T(8,128)S(1)}, f32[1,1,28,512]{3,2,1,0:T(8,128)}, u32[]{:S(2)}) copy-start(f32[1,1,28,512]{3,2,1,0:T(8,128)} %copy-done.26) | copy-start | bytes 172036
  44.2 2.0 %copy-start.25 = (f32[1,1,28,512]{3,2,1,0:T(8,128)S(1)}, f32[1,1,28,512]{3,2,1,0:T(8,128)}, u32[]{:S(2)}) copy-start(f32[1,1,28,512]{3,2,1,0:T(8,128)} %copy-done.24) | copy-start | bytes 172036
  45.4 3.2 %copy-start.23 = (f32[1,28,512]{2,1,0:T(8,128)S(1)}, f32[1,28,512]{2,1,0:T(8,128)}, u32[]{:S(2)}) copy-start(f32[1,28,512]{2,1,0:T(8,128)} %copy-done.22) | copy-start | bytes 172036
  45.4 3.2 %copy-start.21 = (f32[1,28,512]{2,1,0:T(8,128)S(1)}, f32[1,28,512]{2,1,0:T(8,128)}, u32[]{:S(2)}) copy-start(f32[1,28,512]{2,1,0:T(8,128)} %copy-done.20) | copy-start | bytes 172036
  45.4 3.2 %copy-start.4 = (f32[2,4,64,512]{3,2,1,0:T(8,128)S(1)}, f32[2,4,64,512]{3,2,1,0:T(8,128)}, u32[]{:S(2)}) copy-start(f32[2,4,64,512]{3,2,1,0:T(8,128)} %forc.1) | copy-start | bytes 3145732
  46.1 2.6 %slice-start = ((f32[2,4,2,512]{3,2,1,0:T(2,128)}), f32[2,2,2,512]{3,2,1,0:T(2,128)S(1)}, s32[]{:S(2)}) async-start(f32[2,4,2,512]{3,2,1,0:T(2,128)} %reshape.152), calls=%async_computation | async-start | bytes 32768 | tf_op jit(solution)/shard_map/slice | solution.py:329
  50.5 1.2 %copy-start.5 = (f32[6,66,512]{2,1,0:T(8,128)S(1)}, f32[6,66,512]{2,1,0:T(8,128)}, u32[]{:S(2)}) copy-start(f32[6,66,512]{2,1,0:T(8,128)} %get-tuple-element.69) | copy-start | bytes 2433028
  50.5 1.4 %copy-start.6 = (f32[6,66,512]{2,1,0:T(8,128)S(1)}, f32[6,66,512]{2,1,0:T(8,128)}, u32[]{:S(2)}) copy-start(f32[6,66,512]{2,1,0:T(8,128)} %get-tuple-element.59) | copy-start | bytes 2433028
  50.5 1.7 %copy-start.7 = (f32[6,66,512]{2,1,0:T(8,128)S(1)}, f32[6,66,512]{2,1,0:T(8,128)}, u32[]{:S(2)}) copy-start(f32[6,66,512]{2,1,0:T(8,128)} %get-tuple-element.60) | copy-start | bytes 2433028
  50.5 1.9 %copy-start.8 = (f32[6,66,512]{2,1,0:T(8,128)S(1)}, f32[6,66,512]{2,1,0:T(8,128)}, u32[]{:S(2)}) copy-start(f32[6,66,512]{2,1,0:T(8,128)} %get-tuple-element.62) | copy-start | bytes 2433028
  50.6 2.2 %copy-start.9 = (f32[6,66,512]{2,1,0:T(8,128)S(1)}, f32[6,66,512]{2,1,0:T(8,128)}, u32[]{:S(2)}) copy-start(f32[6,66,512]{2,1,0:T(8,128)} %get-tuple-element.64) | copy-start | bytes 2433028
  50.6 2.5 %copy-start.10 = (f32[6,66,512]{2,1,0:T(8,128)S(1)}, f32[6,66,512]{2,1,0:T(8,128)}, u32[]{:S(2)}) copy-start(f32[6,66,512]{2,1,0:T(8,128)} %get-tuple-element.66) | copy-start | bytes 2433028
  56.5 3.5 %copy-start.16 = (f32[4,64,512]{2,1,0:T(8,128)S(1)}, f32[4,64,512]{2,1,0:T(8,128)}, u32[]{:S(2)}) copy-start(f32[4,64,512]{2,1,0:T(8,128)} %get-tuple-element.55) | copy-start | bytes 1572868
  56.5 3.5 %copy-start.17 = (f32[4,64,512]{2,1,0:T(8,128)S(1)}, f32[4,64,512]{2,1,0:T(8,128)}, u32[]{:S(2)}) copy-start(f32[4,64,512]{2,1,0:T(8,128)} %get-tuple-element.54) | copy-start | bytes 1572868
  56.5 3.5 %copy-start.18 = (f32[4,64,512]{2,1,0:T(8,128)S(1)}, f32[4,64,512]{2,1,0:T(8,128)}, u32[]{:S(2)}) copy-start(f32[4,64,512]{2,1,0:T(8,128)} %get-tuple-element.57) | copy-start | bytes 1572868
  60.0 24.0 %copy-start.15 = (f32[4,64,512]{2,1,0:T(8,128)S(1)}, f32[4,64,512]{2,1,0:T(8,128)}, u32[]{:S(2)}) copy-start(f32[4,64,512]{2,1,0:T(8,128)} %get-tuple-element.45) | copy-start | bytes 1572868
  61.2 22.8 %copy-start.12 = (f32[4,64,512]{2,1,0:T(8,128)S(1)}, f32[4,64,512]{2,1,0:T(8,128)}, u32[]{:S(2)}) copy-start(f32[4,64,512]{2,1,0:T(8,128)} %get-tuple-element.17) | copy-start | bytes 1572868
  61.2 22.8 %copy-start.13 = (f32[4,64,512]{2,1,0:T(8,128)S(1)}, f32[4,64,512]{2,1,0:T(8,128)}, u32[]{:S(2)}) copy-start(f32[4,64,512]{2,1,0:T(8,128)} %get-tuple-element.42) | copy-start | bytes 1572868
  61.2 22.8 %copy-start.14 = (f32[4,64,512]{2,1,0:T(8,128)S(1)}, f32[4,64,512]{2,1,0:T(8,128)}, u32[]{:S(2)}) copy-start(f32[4,64,512]{2,1,0:T(8,128)} %get-tuple-element.44) | copy-start | bytes 1572868
  61.4 0.6 copy-start.33
  84.1 4.8 %copy-start.34 = (f32[4,128]{1,0:T(4,128)S(1)}, f32[4,128]{1,0:T(4,128)}, u32[]{:S(2)}) copy-start(f32[4,128]{1,0:T(4,128)} %get-tuple-element.116) | copy-start | bytes 6148

commit v4 on v3

--- a/solution.py
+++ b/solution.py
@@ -343,7 +343,7 @@
     slab_n, cross_n = lax.axis_size("slab"), lax.axis_size("cross")
     slab, cross = lax.axis_index("slab"), lax.axis_index("cross")
     nx, ny, nz = viscosity.shape
-    v, f = halos(viscosity, forcing, slab_n, cross_n)
+    v, f = lax.optimization_barrier(halos(viscosity, forcing, slab_n, cross_n))
     c = v[1:-1, 1:-1]
     fxp, fxm = 0.5 * (c + v[2:, 1:-1]), 0.5 * (c + v[:-2, 1:-1])
     fyp, fym = 0.5 * (c + v[1:-1, 2:]), 0.5 * (c + v[1:-1, :-2])

time: 90.6 us -> 80.9 us (0.89)
  local copies, waits for them, and re-layouts: 19.4 us -> 13.7 us
  other arithmetic: 32.1 us -> 28.3 us
    slice x4, local copies, waits for them, and re-layouts: 4.58 us -> 0.2 us  [inner(): return a[..., 1:-1, 1:-1, :]]
    concatenate x0 -> x1, other arithmetic: none -> 2.65 us  [halos(): jnp.concatenate([fs[1], fs[0], fs[2]], 1)]
    slice x8, local copies, waits for them, and re-layouts: 2.52 us -> 0.07 us  [halos(): cv = [a[vcut[0]:vcut[1]] for a in cv]]
    slice x5, local copies, waits for them, and re-layouts: 0.01 us -> 1.82 us  [halos(): cf = [a[:, fcut[0]:fcut[1]] for a in cf]]
    add x1, other arithmetic: 3.19 us -> 1.53 us  [shards(): U[0, 0] = U[0, 0] + w1 * d1]
    mul x1, other arithmetic: 1.81 us -> 0.42 us  [shards(): y0 = dinv * f]
    select_n x4, other arithmetic: 3.47 us -> 2.38 us  [only(): return jnp.where(cond, a, 0.0)]
    mul x1, other arithmetic: 1.47 us -> 0.41 us  [shards(): U = {o: w2 * a for o, a in W.items()}]
where the time goes in v4:
time: 80.9 us; the launch traced here: 79.7 us
  Pallas kernels  36.5 us (45%)
  other arithmetic  28.3 us (35%)
  local copies, waits for them, and re-layouts  13.7 us (17%)
  between operations  1.21 us (1%)
    pallas_call x1, Pallas kernels, column_cg(): pl.pallas_call(functools.partial(cg_body, sn, cn), out_shape=(jax.ShapeDt...  20.9 us
    pallas_call x1, Pallas kernels, halos(): pl.pallas_call(functools.partial(halo_body, sn, cn), out_shape=(jax.Shape...  15.6 us
    reduce_sum x4, other arithmetic, shards(): jnp.sum(m[o], axis=1)  8.11 us
    sub x1, other arithmetic, shards(): velocity = velocity - a[None] * s[:, :, None, :]  4.74 us
    add x2, other arithmetic, shards(): free = w0 * inner(inner(y0)) + tapply(w1 * inner(y0) + w2 * t1, faces0, d0)  3.31 us
    slice x4, local copies, waits for them, and re-layouts, zs(): return jnp.pad(a[..., :s], [(0, 0)] * (a.ndim - 1) + [(-s, 0)])  3.22 us
    unnamed x37, local copies, waits for them, and re-layouts  3.01 us
    concatenate x1, other arithmetic, halos(): jnp.concatenate([fs[1], fs[0], fs[2]], 1)  2.65 us

profile of v4, /device:TPU:9, one launch (start us, length us, event | category | flops | bytes accessed | tf_op | source)
XLA Modules:
  0.0 79.7 jit_solution(12253576457718950909)
XLA Ops:
  0.6 0.9 %fusion.75 = (f32[4,3,512]{2,1,0:T(4,128)S(1)}, f32[4,3,512]{2,1,0:T(4,128)S(1)}) fusion(f32[4,64,512]{2,1,0:T(8,128)} %visc.1), kind=kLoop, calls=%fused_computation.157 | loop fusion | bytes 98304 | tf_op jit(solution)/shard_map/slice | solution.py:293
  1.5 1.0 %fusion.69 = (f32[2,4,2,512]{3,2,1,0:T(2,128)S(1)}, f32[2,4,2,512]{3,2,1,0:T(2,128)S(1)}) fusion(f32[2,4,64,512]{3,2,1,0:T(8,128)} %forc.1), kind=kLoop, calls=%fused_computation.151 | loop fusion | bytes 131072 | tf_op jit(solution)/shard_map/slice | solution.py:294
  2.6 0.7 pad_maximum_fusion.ypack
  3.3 15.6 %halos.1 = (f32[2,3,64,512]{3,2,1,0:T(8,128)}, f32[2,2,2,64,512]{4,3,2,1,0:T(8,128)}, f32[2,28,512]{2,1,0:T(8,128)}, f32[2,2,28,512]{3,2,1,0:T(8,128)}) custom-call(f32[4,64,512]{2,1,0:T(8,128)} %visc.1, f32[2,4,64,512]{3,2,1,0:T(8,128)} %forc.1, f32[2,28,512]{2,1,0:T(8,128)} %pad_maximum_fusion.ypack), custom_call_target="tpu_custom_call" | custom-call | tf_op jit(solution)/shard_map/halos/pallas_call | solution.py:299
  18.9 0.0 copy-start.9
  19.0 1.0 %slice_select_fusion.5 = (f32[1,1,28,512]{3,2,1,0:T(8,128)S(1)}, f32[1,1,28,512]{3,2,1,0:T(8,128)S(1)}, f32[1,1,28,512]{3,2,1,0:T(8,128)S(1)}, f32[1,1,28,512]{3,2,1,0:T(8,128)S(1)}) fusion(f32[2,2,28,512]{3,2,1,0:T(8,128)} %get-tuple-element.10, pred[]{:T(512)S(6)} %and.27, pred[]{:T(512)S(6)} %and.30, pred[]{:T(512)S(6)} %and.29, pred[]{:T(512)S(6)} %and.28), kind=kLoop, calls=%fused_computation.113 | loop fusion | flops 57344 | bytes 458756 | tf_op jit(solution)/shard_map/jit(_where)/select_n | solution.py:318
  20.0 0.0 copy-start.10
  20.1 0.0 copy-start.12
  20.1 0.6 slice.544
  20.7 0.0 copy-done.12
  20.8 0.6 slice.548
  21.4 0.6 slice.550
  22.0 0.0 copy-done.9
  22.0 0.1 select_bitcast_fusion.1
  22.2 0.0 copy-done.10
  22.3 0.0 copy-done.1
  22.3 0.0 slice-done
  22.3 2.6 %maximum_maximum_fusion = f32[2,8,68,512]{3,2,1,0:T(8,128)} fusion(f32[2,2,2,512]{3,2,1,0:T(2,128)} %slice.550, f32[2,2,64,512]{3,2,1,0:T(8,128)S(1)} %get-tuple-element.77, f32[2,2,2,512]{3,2,1,0:T(2,128)} %slice.548, f32[2,4,2,512]{3,2,1,0:T(2,128)S(1)} %reshape.155, f32[2,4,64,512]{3,2,1,0:T(8,128)S(1)} %copy-done.1, f32[2,4,2,512]{3,2,1,0:T(2,128)S(1)} %reshape.154, ...), kind=kLoop, calls=%fused_computation | loop fusion | flops 4456448 | bytes 4456448 | tf_op jit(solution)/shard_map/concatenate | solution.py:332
  25.1 1.2 %select_bitcast_fusion.3 = (f32[3,64,512]{2,1,0:T(8,128)S(1)}, f32[3,64,512]{2,1,0:T(8,128)S(1)}) fusion(f32[2,3,64,512]{3,2,1,0:T(8,128)} %get-tuple-element.11, pred[]{:T(512)S(6)} %gt.6, pred[]{:T(512)S(6)} %lt.25), kind=kLoop, calls=%fused_computation.104 | loop fusion | flops 196608 | bytes 1572866 | tf_op jit(solution)/shard_map/jit(_where)/select_n | solution.py:318
  26.4 0.0 copy-done.2
  26.4 0.3 maximum_maximum_fusion.1
  26.6 1.6 %fusion.67 = (f32[8,68,511]{2,1,0:T(8,128)S(1)}, f32[8,68,511]{2,1,0:T(8,128)}) fusion(f32[10,70,512]{2,1,0:T(8,128)S(1)} %maximum_maximum_fusion.1), kind=kLoop, calls=%fused_computation.149 | loop fusion | bytes 4447744 | tf_op jit(solution)/shard_map/slice | solution.py:338
  28.2 2.6 %divide_select_fusion = (f32[8,68,512]{2,1,0:T(8,128)S(1)}, f32[8,68,512]{2,1,0:T(8,128)S(1)}, f32[8,68,512]{2,1,0:T(8,128)S(1)}, f32[8,68,512]{2,1,0:T(8,128)S(...) fusion(pred[68]{0:T(512)(128)(4,1)S(1)} %get-tuple-element.115, ...), kind=kLoop, calls=%fused_computation.16 | loop fusion | flops 6127616 | bytes 15593360 | tf_op jit(solution)/shard_map/jit(_where)/select_n | solution.py:355
  30.9 0.4 fusion.16
  31.3 1.2 %fusion.73 = (f32[4,64,511]{2,1,0:T(8,128)}, f32[4,64,511]{2,1,0:T(8,128)}) fusion(f32[6,66,512]{2,1,0:T(8,128)S(1)} %get-tuple-element.71), kind=kLoop, calls=%fused_computation.155 | loop fusion | bytes 2093056 | tf_op jit(solution)/shard_map/slice | solution.py:338
  32.5 0.4 fusion.68
  32.8 1.5 %fusion.20 = (f32[6,66,512]{2,1,0:T(8,128)S(1)}, f32[6,66,512]{2,1,0:T(8,128)S(1)}, f32[6,66,512]{2,1,0:T(8,128)S(1)}, f32[6,66,512]{2,1,0:T(8,128)S(1)}, f32[6,...) fusion(f32[8,68,512]{2,1,0:T(8,128)S(1)} %get-tuple-element.34,, ...), kind=kLoop, calls=%fused_computation.44 | loop fusion | flops 3244032 | bytes 16216992 | tf_op jit(solution)/shard_map/add | solution.py:390
  34.4 0.0 copy-start.7
  34.4 0.0 copy-start.8
  34.4 0.2 fusion.71
  34.6 0.8 copy-done.7
  35.4 0.2 copy-done.8
  35.6 2.3 %fusion.52 = (f32[4,512]{1,0:T(4,128)S(1)}, f32[4,64,512]{2,1,0:T(8,128)}, f32[4,64,512]{2,1,0:T(8,128)}, f32[4,512]{1,0:T(4,128)S(1)}, f32[4,64,512]{2,1,0:T(8,128)}, /*index=5*/f32[4,64,512]{2,1,0:T(8,128)}) fusion(f32[6,66,512]{2,1,0:T(8,128)S(1)} %get-tuple-element.65, f32[8,68,512]{2,1,0:T(8,128)S(1)} %get-tuple-element.36, ...), kind=kLoop, calls=%fused_computation.140 | loop fusion | flops 2093056 | bytes 8401920 | tf_op jit(solution)/shard_map/reduce_sum | solution.py:407
  37.8 0.2 fusion.72
  38.1 0.2 fusion.74
  38.3 2.1 %fusion.63 = (f32[4,512]{1,0:T(4,128)S(1)}, f32[4,64,512]{2,1,0:T(8,128)}, f32[4,64,512]{2,1,0:T(8,128)}) fusion(f32[8,68,512]{2,1,0:T(8,128)S(1)} %get-tuple-element.34, f32[4,64,511]{2,1,0:T(8,128)S(1)} %get-tuple-element.85, f32[8,68,512]{2,1,0:T(8,128)S(1)} %get-tuple-element.39, f32[4,64,511]{2,1,0:T(8,128)S(1)} %get-tuple-element.89, ...), kind=kLoop, calls=%fused_computation.146 | loop fusion | flops 2357248 | bytes 8918016 | tf_op jit(solution)/shard_map/reduce_sum | solution.py:407
  40.4 1.8 %fusion.61 = (f32[4,512]{1,0:T(4,128)S(1)}, f32[4,64,512]{2,1,0:T(8,128)}, f32[4,64,512]{2,1,0:T(8,128)}, f32[4,512]{1,0:T(4,128)S(1)}, f32[4,64,512]{2,1,0:T(8,128)}, /*index=5*/f32[4,64,512]{2,1,0:T(8,128)S(1)}) fusion(f32[6,66,512]{2,1,0:T(8,128)S(1)} %get-tuple-element.71, f32[8,68,512]{2,1,0:T(8,128)S(1)} %get-tuple-element.38, ...), kind=kLoop, calls=%fused_computation.145 | loop fusion | flops 2093056 | bytes 8404992 | tf_op jit(solution)/shard_map/reduce_sum | solution.py:407
  42.3 0.2 fusion.70
  42.5 1.9 %fusion.59 = (f32[4,512]{1,0:T(4,128)S(1)}, f32[4,64,512]{2,1,0:T(8,128)}, f32[4,64,512]{2,1,0:T(8,128)}, f32[4,512]{1,0:T(4,128)S(1)}, f32[4,64,512]{2,1,0:T(8,128)}, /*index=5*/f32[4,64,512]{2,1,0:T(8,128)S(1)}) fusion(f32[6,66,512]{2,1,0:T(8,128)S(1)} %get-tuple-element.67, f32[8,68,512]{2,1,0:T(8,128)S(1)} %get-tuple-element.38, ...), kind=kLoop, calls=%fused_computation.144 | loop fusion | flops 2093056 | bytes 8401920 | tf_op jit(solution)/shard_map/reduce_sum | solution.py:407
  44.5 1.0 %multiply_multiply_fusion.2 = (f32[4,64,512]{2,1,0:T(8,128)}, f32[4,64,512]{2,1,0:T(8,128)S(1)}) fusion(f32[4,64,511]{2,1,0:T(8,128)S(1)} %get-tuple-element.84, f32[8,68,512]{2,1,0:T(8,128)S(1)} %get-tuple-element.40, f32[8,68,512]{2,1,0:T(8,128)S(1)} %get-tuple-element.34), kind=kLoop, calls=%fused_computation.99 | loop fusion | flops 262144 | bytes 2620416 | tf_op jit(solution)/shard_map/mul | solution.py:404
  45.5 0.8 copy-done
  46.3 0.4 broadcast_multiply_fusion
  46.7 0.8 %fusion.65 = (f32[2,6,66,511]{3,2,1,0:T(8,128)S(1)}, f32[2,6,66,511]{3,2,1,0:T(8,128)S(1)}) fusion(f32[2,8,68,512]{3,2,1,0:T(8,128)S(1)} %broadcast_multiply_fusion), kind=kLoop, calls=%fused_computation.147 | loop fusion | bytes 6475392 | tf_op jit(solution)/shard_map/slice | solution.py:337
  47.5 2.2 %fusion.5 = f32[2,6,66,512]{3,2,1,0:T(8,128)S(1)} fusion(f32[2,8,68,512]{3,2,1,0:T(8,128)S(1)} %broadcast_multiply_fusion, f32[2,6,66,511]{3,2,1,0:T(8,128)S(1)} %get-tuple-element.53, f32[2,6,66,511]{3,2,1,0:T(8,128)S(1)} %get-tuple-element.52, f32[6,66,512]{2,1,0:T(8,128)S(1)} %get-tuple-element.66, f32[6,66,512]{2,1,0:T(8,128)S(1)} %get-tuple-element.68, ...), kind=kLoop, calls=%fused_computation.7 | loop fusion | flops 6082560 | bytes 18646848 | tf_op jit(solution)/shard_map/add | solution.py:379
  49.7 0.4 fusion.66
  50.2 0.1 slice.569
  50.2 0.1 slice.571
  50.3 0.1 slice.573
  50.4 0.1 slice.575
  50.4 0.0 copy-start.6
  50.4 1.1 %fusion.12 = f32[2,4,64,512]{3,2,1,0:T(8,128)S(1)} fusion(f32[2,6,66,512]{3,2,1,0:T(8,128)S(1)} %fusion.5, f32[2,8,68,512]{3,2,1,0:T(8,128)S(1)} %broadcast_multiply_fusion, f32[2,4,64,511]{3,2,1,0:T(8,128)S(1)} %get-tuple-element.55, f32[2,4,64,511]{3,2,1,0:T(8,128)S(1)} %get-tuple-element.54, f32[4,64,512]{2,1,0:T(8,128)S(1)} %get-tuple-element.61, ...), kind=kLoop, calls=%fused_computation.28 | loop fusion | flops 3670016 | bytes 12054528 | tf_op jit(solution)/shard_map/add | solution.py:379
  51.6 0.0 copy-start.3
  51.6 0.0 copy-start.4
  51.6 0.1 slice_reduce_fusion
  51.8 0.6 copy-done.11
  52.4 20.9 %column_cg.1 = (f32[5,2,8,512]{3,2,1,0:T(8,128)}, f32[4,128]{1,0:T(4,128)}) custom-call(f32[9,4,512]{2,1,0:T(4,128)} %copy-done.11, s32[1,512]{1,0:T(1,128)} %bitcast.65), custom_call_target="tpu_custom_call" | custom-call | tf_op jit(solution)/shard_map/column_cg/pallas_call | solution.py:155
  73.3 1.1 %slice_bitcast_fusion.12 = (f32[2,4,512]{2,1,0:T(4,128)S(1)}, f32[2,4,512]{2,1,0:T(4,128)S(1)}, f32[2,4,512]{2,1,0:T(4,128)S(1)}, f32[2,4,512]{2,1,0:T(4,128)S(1...) fusion(f32[5,2,8,512]{3,2,1,0:T(8,128)} %get-tuple-element.16), kind=kLoop, calls=%fused_computation.135 | loop fusion | bytes 425984 | tf_op jit(solution)/shard_map/mul | solution.py:412
  74.4 0.0 copy-done.6
  74.4 0.0 copy-done.3
  74.4 0.0 copy-done.4
  74.4 0.0 copy-done.5
  74.4 0.0 copy-start.13
  74.4 4.7 %multiply_subtract_fusion = f32[2,4,64,512]{3,2,1,0:T(8,128)} fusion(f32[2,4,64,512]{3,2,1,0:T(8,128)S(1)} %fusion.12, f32[2,4,512]{2,1,0:T(4,128)S(1)} %get-tuple-element.99, f32[4,64,512]{2,1,0:T(8,128)} %get-tuple-element.60, f32[2,4,512]{2,1,0:T(4,128)S(1)} %get-tuple-element.100, f32[4,64,512]{2,1,0:T(8,128)} %get-tuple-element.51, ...), kind=kLoop, calls=%fused_computation.35 | loop fusion | flops 6815744 | bytes 9125888 | tf_op jit(solution)/shard_map/sub | solution.py:412
  79.2 0.6 copy.14
  (48 shorter events, 0.5 us)
Async XLA Ops:
  18.9 3.1 %copy-start.9 = (f32[2,2,2,64,512]{4,3,2,1,0:T(8,128)S(1)}, f32[2,2,2,64,512]{4,3,2,1,0:T(8,128)}, u32[]{:S(2)}) copy-start(f32[2,2,2,64,512]{4,3,2,1,0:T(8,128)} %get-tuple-element.13) | copy-start | bytes 3145732
  20.0 2.1 %copy-start.10 = (f32[2,28,512]{2,1,0:T(8,128)S(1)}, f32[2,28,512]{2,1,0:T(8,128)}, u32[]{:S(2)}) copy-start(f32[2,28,512]{2,1,0:T(8,128)} %get-tuple-element.12) | copy-start | bytes 344068
  20.1 0.7 copy-start.12
  20.7 1.5 %copy-start.1 = (f32[2,4,64,512]{3,2,1,0:T(8,128)S(1)}, f32[2,4,64,512]{3,2,1,0:T(8,128)}, u32[]{:S(2)}) copy-start(f32[2,4,64,512]{3,2,1,0:T(8,128)} %forc.1) | copy-start | bytes 3145732
  20.7 1.5 %slice-start = ((f32[2,4,2,512]{3,2,1,0:T(2,128)}), f32[2,2,2,512]{3,2,1,0:T(2,128)S(1)}, s32[]{:S(2)}) async-start(f32[2,4,2,512]{3,2,1,0:T(2,128)} %copy-done.12), calls=%async_computation | async-start | bytes 32768 | tf_op jit(solution)/shard_map/slice | solution.py:329
  24.9 1.4 %copy-start.2 = (f32[4,64,512]{2,1,0:T(8,128)S(1)}, f32[4,64,512]{2,1,0:T(8,128)}, u32[]{:S(2)}) copy-start(f32[4,64,512]{2,1,0:T(8,128)} %visc.1) | copy-start | bytes 1572868
  34.4 1.0 %copy-start.7 = (f32[4,64,511]{2,1,0:T(8,128)S(1)}, f32[4,64,511]{2,1,0:T(8,128)}, u32[]{:S(2)}) copy-start(f32[4,64,511]{2,1,0:T(8,128)} %get-tuple-element.86) | copy-start | bytes 1569796
  34.4 1.2 %copy-start.8 = (f32[4,64,511]{2,1,0:T(8,128)S(1)}, f32[4,64,511]{2,1,0:T(8,128)}, u32[]{:S(2)}) copy-start(f32[4,64,511]{2,1,0:T(8,128)} %get-tuple-element.87) | copy-start | bytes 1569796
  44.4 1.9 %copy-start = (f32[2,8,68,512]{3,2,1,0:T(8,128)S(1)}, f32[2,8,68,512]{3,2,1,0:T(8,128)}, u32[]{:S(2)}) copy-start(f32[2,8,68,512]{3,2,1,0:T(8,128)} %maximum_maximum_fusion) | copy-start | bytes 6684676
  50.4 24.0 %copy-start.6 = (f32[4,64,512]{2,1,0:T(8,128)S(1)}, f32[4,64,512]{2,1,0:T(8,128)}, u32[]{:S(2)}) copy-start(f32[4,64,512]{2,1,0:T(8,128)} %get-tuple-element.49) | copy-start | bytes 1572868
  51.6 22.8 %copy-start.3 = (f32[4,64,512]{2,1,0:T(8,128)S(1)}, f32[4,64,512]{2,1,0:T(8,128)}, u32[]{:S(2)}) copy-start(f32[4,64,512]{2,1,0:T(8,128)} %get-tuple-element.21) | copy-start | bytes 1572868
  51.6 22.8 %copy-start.4 = (f32[4,64,512]{2,1,0:T(8,128)S(1)}, f32[4,64,512]{2,1,0:T(8,128)}, u32[]{:S(2)}) copy-start(f32[4,64,512]{2,1,0:T(8,128)} %get-tuple-element.46) | copy-start | bytes 1572868
  51.6 22.8 %copy-start.5 = (f32[4,64,512]{2,1,0:T(8,128)S(1)}, f32[4,64,512]{2,1,0:T(8,128)}, u32[]{:S(2)}) copy-start(f32[4,64,512]{2,1,0:T(8,128)} %get-tuple-element.48) | copy-start | bytes 1572868
  51.8 0.6 copy-start.11
  74.4 4.8 %copy-start.13 = (f32[4,128]{1,0:T(4,128)S(1)}, f32[4,128]{1,0:T(4,128)}, u32[]{:S(2)}) copy-start(f32[4,128]{1,0:T(4,128)} %get-tuple-element.120) | copy-start | bytes 6148

commit v5 on v4

--- a/solution.py
+++ b/solution.py
@@ -176,6 +176,36 @@
     )(part, owner)
 
 
+def subtract_body(keys, gs, free, *refs):
+    fields, out = refs[:-1], refs[-1]
+    comps, nx = free.shape[0], free.shape[1]
+    for i in range(nx):
+        total = [free[c, i] for c in range(comps)]
+        for (dx, dz), field in zip(keys, fields):
+            a = field[i]
+            for c in range(comps):
+                total[c] = total[c] - a * gs[2 + dz, c, 2 + dx + i : 3 + dx + i, :]
+        for c in range(comps):
+            out[c, i] = total[c]
+
+
+def subtract_gradient(gs, free, m):
+    comps, nx, ny, nz = free.shape
+    step = 16
+    keys = list(m)
+    wide = pl.BlockSpec((comps, nx, step, nz), lambda j: (0, 0, j, 0))
+    one = pl.BlockSpec((nx, step, nz), lambda j: (0, j, 0))
+    whole = pl.BlockSpec(gs.shape, lambda j: (0, 0, 0, 0))
+    return pl.pallas_call(
+        functools.partial(subtract_body, keys),
+        grid=(ny // step,),
+        out_shape=jax.ShapeDtypeStruct(free.shape, jnp.float32),
+        in_specs=[whole, wide] + [one] * len(keys),
+        out_specs=wide,
+        name="subtract_gradient",
+    )(gs, free, *[m[o] for o in keys])
+
+
 def halo_body(sn, cn, visc, forc, ypack, vx, fx, yp, cp, send, recv):
     slab, cross = lax.axis_index("slab"), lax.axis_index("cross")
     nx = visc.shape[0]
@@ -406,10 +436,7 @@
 
     part = jnp.stack([jnp.sum(m[o], axis=1) for o in OFFSETS] + [jnp.sum(free[0], 1), jnp.sum(free[1], 1)], 0)
     gs, pressure = column_cg(part, owner_slot.reshape(1, nz), slab_n, cross_n)
-    velocity = free
-    for o, a in m.items():
-        s = gs[2 + o[1], :, 2 + o[0] : 2 + o[0] + nx]
-        velocity = velocity - a[None] * s[:, :, None, :]
+    velocity = subtract_gradient(gs, free, m)
     return velocity, pressure
 
 

time: 80.9 us -> 78.9 us (0.975)
  Pallas kernels: 36.5 us -> 41.8 us
  other arithmetic: 28.3 us -> 23.4 us
  local copies, waits for them, and re-layouts: 13.7 us -> 11.4 us
    pallas_call x0 -> x1, Pallas kernels: none -> 5.3 us  [subtract_gradient(): pl.pallas_call(functools.partial(subtract_body, keys), grid=(ny // step,)...]
    sub x1 -> x0, other arithmetic: 4.74 us -> none  [shards(): velocity = velocity - a[None] * s[:, :, None, :]]
    slice x0 -> x2, other arithmetic: none -> 1.87 us  [inner(): return a[..., 1:-1, 1:-1, :]]
    add x1 -> x0, other arithmetic: 1.53 us -> none  [shards(): U[0, 0] = U[0, 0] + w1 * d1]
    mul x1 -> x0, local copies, waits for them, and re-layouts: 1.1 us -> none  [shards(): velocity = velocity - a[None] * s[:, :, None, :]]
    slice x4 -> x5, local copies, waits for them, and re-layouts: 3.22 us -> 2.51 us  [zs(): return jnp.pad(a[..., :s], [(0, 0)] * (a.ndim - 1) + [(-s, 0)])]
    unnamed x37 -> x27, local copies, waits for them, and re-layouts: 3.01 us -> 2.73 us
    slice x5 -> x4, local copies, waits for them, and re-layouts: 2.12 us -> 1.89 us  [zs(): return jnp.pad(a[..., s:], [(0, 0)] * (a.ndim - 1) + [(0, s)])]
where the time goes in v5:
time: 78.9 us; the launch traced here: 77.8 us
  Pallas kernels  41.8 us (53%)
  other arithmetic  23.4 us (30%)
  local copies, waits for them, and re-layouts  11.4 us (14%)
  between operations  1.15 us (1%)
    pallas_call x1, Pallas kernels, column_cg(): pl.pallas_call(functools.partial(cg_body, sn, cn), out_shape=(jax.ShapeDt...  20.9 us
    pallas_call x1, Pallas kernels, halos(): pl.pallas_call(functools.partial(halo_body, sn, cn), out_shape=(jax.Shape...  15.6 us
    reduce_sum x4, other arithmetic, shards(): jnp.sum(m[o], axis=1)  8.11 us
    pallas_call x1, Pallas kernels, subtract_gradient(): pl.pallas_call(functools.partial(subtract_body, keys), grid=(ny // step,)...  5.3 us
    add x2, other arithmetic, shards(): free = w0 * inner(inner(y0)) + tapply(w1 * inner(y0) + w2 * t1, faces0, d0)  3.35 us
    unnamed x27, local copies, waits for them, and re-layouts  2.73 us
    select_n x1, other arithmetic, shards(): dinv = jnp.where(inside, 1.0 / jnp.where(inside, diag, 1.0), 0.0)  2.63 us
    concatenate x1, other arithmetic, halos(): jnp.concatenate([fs[1], fs[0], fs[2]], 1)  2.61 us

profile of v5, /device:TPU:9, one launch (start us, length us, event | category | flops | bytes accessed | tf_op | source)
XLA Modules:
  0.0 77.8 jit_solution(14099689371510162591)
XLA Ops:
  0.6 0.9 %fusion.77 = (f32[4,3,512]{2,1,0:T(4,128)S(1)}, f32[4,3,512]{2,1,0:T(4,128)S(1)}) fusion(f32[4,64,512]{2,1,0:T(8,128)} %visc.1), kind=kLoop, calls=%fused_computation.145 | loop fusion | bytes 98304 | tf_op jit(solution)/shard_map/slice | solution.py:323
  1.5 1.0 %fusion.71 = (f32[2,4,2,512]{3,2,1,0:T(2,128)S(1)}, f32[2,4,2,512]{3,2,1,0:T(2,128)S(1)}) fusion(f32[2,4,64,512]{3,2,1,0:T(8,128)} %forc.1), kind=kLoop, calls=%fused_computation.139 | loop fusion | bytes 131072 | tf_op jit(solution)/shard_map/slice | solution.py:324
  2.6 0.7 pad_maximum_fusion.ypack
  3.3 15.6 %halos.1 = (f32[2,3,64,512]{3,2,1,0:T(8,128)}, f32[2,2,2,64,512]{4,3,2,1,0:T(8,128)}, f32[2,28,512]{2,1,0:T(8,128)}, f32[2,2,28,512]{3,2,1,0:T(8,128)}) custom-call(f32[4,64,512]{2,1,0:T(8,128)} %visc.1, f32[2,4,64,512]{3,2,1,0:T(8,128)} %forc.1, f32[2,28,512]{2,1,0:T(8,128)} %pad_maximum_fusion.ypack), custom_call_target="tpu_custom_call" | custom-call | tf_op jit(solution)/shard_map/halos/pallas_call | solution.py:329
  18.9 0.0 copy-start.4
  19.0 1.0 %slice_select_fusion.5 = (f32[1,1,28,512]{3,2,1,0:T(8,128)S(1)}, f32[1,1,28,512]{3,2,1,0:T(8,128)S(1)}, f32[1,1,28,512]{3,2,1,0:T(8,128)S(1)}, f32[1,1,28,512]{3,2,1,0:T(8,128)S(1)}) fusion(f32[2,2,28,512]{3,2,1,0:T(8,128)} %get-tuple-element.10, pred[]{:T(512)S(6)} %and.27, pred[]{:T(512)S(6)} %and.30, pred[]{:T(512)S(6)} %and.29, pred[]{:T(512)S(6)} %and.28), kind=kLoop, calls=%fused_computation.112 | loop fusion | flops 57344 | bytes 458756 | tf_op jit(solution)/shard_map/jit(_where)/select_n | solution.py:348
  20.0 0.0 copy-start.5
  20.1 0.0 copy-start.7
  20.1 0.6 slice.492
  20.7 0.0 copy-done.7
  20.7 0.0 copy-start.2
  20.7 0.0 slice-start
  20.8 0.6 slice.496
  21.4 0.6 slice.498
  22.0 0.0 copy-done.4
  22.0 0.1 select_bitcast_fusion.1
  22.2 0.0 copy-done.5
  22.3 0.0 copy-done.2
  22.3 0.0 slice-done
  22.3 2.6 %maximum_maximum_fusion = f32[2,8,68,512]{3,2,1,0:T(8,128)} fusion(f32[2,2,2,512]{3,2,1,0:T(2,128)} %slice.498, f32[2,2,64,512]{3,2,1,0:T(8,128)S(1)} %get-tuple-element.77, f32[2,2,2,512]{3,2,1,0:T(2,128)} %slice.496, f32[2,4,2,512]{3,2,1,0:T(2,128)S(1)} %reshape.129, f32[2,4,64,512]{3,2,1,0:T(8,128)S(1)} %copy-done.2, f32[2,4,2,512]{3,2,1,0:T(2,128)S(1)} %reshape.128, ...), kind=kLoop, calls=%fused_computation | loop fusion | flops 4456448 | bytes 4456448 | tf_op jit(solution)/shard_map/concatenate | solution.py:362
  24.9 0.0 copy-start.3
  25.0 1.2 %select_bitcast_fusion.3 = (f32[3,64,512]{2,1,0:T(8,128)S(1)}, f32[3,64,512]{2,1,0:T(8,128)S(1)}) fusion(f32[2,3,64,512]{3,2,1,0:T(8,128)} %get-tuple-element.11, pred[]{:T(512)S(6)} %gt.6, pred[]{:T(512)S(6)} %lt.25), kind=kLoop, calls=%fused_computation.103 | loop fusion | flops 196608 | bytes 1572866 | tf_op jit(solution)/shard_map/jit(_where)/select_n | solution.py:348
  26.3 0.0 copy-done.3
  26.3 0.3 maximum_maximum_fusion.1
  26.6 1.6 %fusion.67 = (f32[8,68,511]{2,1,0:T(8,128)S(1)}, f32[8,68,511]{2,1,0:T(8,128)}) fusion(f32[10,70,512]{2,1,0:T(8,128)S(1)} %maximum_maximum_fusion.1), kind=kLoop, calls=%fused_computation.135 | loop fusion | bytes 4447744 | tf_op jit(solution)/shard_map/slice | solution.py:368
  28.2 2.6 %divide_select_fusion = (f32[8,68,512]{2,1,0:T(8,128)S(1)}, f32[8,68,512]{2,1,0:T(8,128)S(1)}, f32[8,68,512]{2,1,0:T(8,128)S(1)}, f32[8,68,512]{2,1,0:T(8,128)S(...) fusion(pred[68]{0:T(512)(128)(4,1)S(1)} %get-tuple-element.100, ...), kind=kLoop, calls=%fused_computation.16 | loop fusion | flops 6127616 | bytes 15593360 | tf_op jit(solution)/shard_map/jit(_where)/select_n | solution.py:385
  30.8 0.4 fusion.70
  31.2 1.4 %fusion.68 = (f32[6,66,512]{2,1,0:T(8,128)S(1)}, f32[6,66,512]{2,1,0:T(8,128)S(1)}, f32[6,66,512]{2,1,0:T(8,128)S(1)}, f32[6,66,512]{2,1,0:T(8,128)S(1)}, f32[6,...) fusion(f32[8,68,512]{2,1,0:T(8,128)S(1)} %get-tuple-element.34,, ...), kind=kLoop, calls=%fused_computation.136 | loop fusion | flops 2433024 | bytes 14594976 | tf_op jit(solution)/shard_map/slice | solution.py:388
  32.6 0.0 copy-start.1
  32.6 1.0 %fusion.25 = (f32[4,64,512]{2,1,0:T(8,128)}, f32[4,64,512]{2,1,0:T(8,128)S(1)}) fusion(f32[6,66,512]{2,1,0:T(8,128)S(1)} %get-tuple-element.67, f32[8,68,512]{2,1,0:T(8,128)S(1)} %get-tuple-element.35, f32[8,68,512]{2,1,0:T(8,128)S(1)} %get-tuple-element.34), kind=kLoop, calls=%fused_computation.54 | loop fusion | flops 262144 | bytes 2621440 | tf_op jit(solution)/shard_map/mul | solution.py:434
  33.6 0.8 %copy-done.1 = f32[2,8,68,512]{3,2,1,0:T(8,128)S(1)} copy-done((f32[2,8,68,512]{3,2,1,0:T(8,128)S(1)}, f32[2,8,68,512]{3,2,1,0:T(8,128)}, u32[]{:S(2)}) %copy-start.1) | copy-done | bytes 2228248
  34.5 0.4 broadcast_multiply_fusion
  34.9 0.8 %fusion.65 = (f32[2,6,66,511]{3,2,1,0:T(8,128)S(1)}, f32[2,6,66,511]{3,2,1,0:T(8,128)S(1)}) fusion(f32[2,8,68,512]{3,2,1,0:T(8,128)S(1)} %broadcast_multiply_fusion), kind=kLoop, calls=%fused_computation.133 | loop fusion | bytes 6475392 | tf_op jit(solution)/shard_map/slice | solution.py:367
  35.7 0.4 fusion.69
  36.1 2.2 %fusion.5 = f32[2,6,66,512]{3,2,1,0:T(8,128)S(1)} fusion(f32[2,8,68,512]{3,2,1,0:T(8,128)S(1)} %broadcast_multiply_fusion, f32[2,6,66,511]{3,2,1,0:T(8,128)S(1)} %get-tuple-element.53, f32[2,6,66,511]{3,2,1,0:T(8,128)S(1)} %get-tuple-element.52, f32[6,66,512]{2,1,0:T(8,128)S(1)} %get-tuple-element.66, f32[6,66,512]{2,1,0:T(8,128)S(1)} %get-tuple-element.64, ...), kind=kLoop, calls=%fused_computation.7 | loop fusion | flops 6082560 | bytes 18646848 | tf_op jit(solution)/shard_map/add | solution.py:409
  38.3 0.5 fusion.66
  38.8 0.2 fusion.74
  39.0 0.2 fusion.76
  39.3 1.9 %fusion.59 = (f32[4,512]{1,0:T(4,128)S(1)}, f32[4,64,512]{2,1,0:T(8,128)}, f32[4,64,512]{2,1,0:T(8,128)}, f32[4,512]{1,0:T(4,128)S(1)}, f32[4,64,512]{2,1,0:T(8,128)}, /*index=5*/f32[4,64,512]{2,1,0:T(8,128)S(1)}) fusion(f32[6,66,512]{2,1,0:T(8,128)S(1)} %get-tuple-element.63, f32[8,68,512]{2,1,0:T(8,128)S(1)} %get-tuple-element.38, ...), kind=kLoop, calls=%fused_computation.130 | loop fusion | flops 2093056 | bytes 8401920 | tf_op jit(solution)/shard_map/reduce_sum | solution.py:437
  41.2 1.8 %fusion.61 = (f32[4,512]{1,0:T(4,128)S(1)}, f32[4,64,512]{2,1,0:T(8,128)}, f32[4,64,512]{2,1,0:T(8,128)}, f32[4,512]{1,0:T(4,128)S(1)}, f32[4,64,512]{2,1,0:T(8,128)}, /*index=5*/f32[4,64,512]{2,1,0:T(8,128)S(1)}) fusion(f32[6,66,512]{2,1,0:T(8,128)S(1)} %get-tuple-element.69, f32[8,68,512]{2,1,0:T(8,128)S(1)} %get-tuple-element.38, ...), kind=kLoop, calls=%fused_computation.131 | loop fusion | flops 2093056 | bytes 8404992 | tf_op jit(solution)/shard_map/reduce_sum | solution.py:437
  43.0 0.1 slice.499
  43.1 0.1 slice.506
  43.2 0.1 slice.516
  43.2 0.1 slice.520
  43.3 1.2 %fusion.12.free = f32[2,4,64,512]{3,2,1,0:T(8,128)S(1)} fusion(f32[2,6,66,512]{3,2,1,0:T(8,128)S(1)} %fusion.5, f32[2,8,68,512]{3,2,1,0:T(8,128)S(1)} %broadcast_multiply_fusion, f32[2,4,64,511]{3,2,1,0:T(8,128)S(1)} %get-tuple-element.55, f32[2,4,64,511]{3,2,1,0:T(8,128)S(1)} %get-tuple-element.54, f32[4,64,512]{2,1,0:T(8,128)S(1)} %slice.516, ...), kind=kLoop, calls=%fused_computation.28 | loop fusion | flops 3670016 | bytes 12054528 | tf_op jit(solution)/shard_map/add | solution.py:409
  44.4 0.0 copy-start
  44.5 0.1 slice_reduce_fusion
  44.6 0.2 fusion.72
  44.8 0.6 copy-done
  45.4 0.2 fusion.73
  45.7 0.2 fusion.75
  45.9 2.2 %fusion.54 = (f32[4,512]{1,0:T(4,128)S(1)}, f32[4,64,512]{2,1,0:T(8,128)}, f32[4,64,512]{2,1,0:T(8,128)}, f32[4,512]{1,0:T(4,128)S(1)}, f32[4,64,512]{2,1,0:T(8,128)}, /*index=5*/f32[4,64,512]{2,1,0:T(8,128)}) fusion(f32[6,66,512]{2,1,0:T(8,128)S(1)} %get-tuple-element.63, f32[8,68,512]{2,1,0:T(8,128)S(1)} %get-tuple-element.36, ...), kind=kLoop, calls=%fused_computation.127 | loop fusion | flops 2093056 | bytes 8400896 | tf_op jit(solution)/shard_map/reduce_sum | solution.py:437
  48.2 2.1 %fusion.63 = (f32[4,512]{1,0:T(4,128)S(1)}, f32[4,64,512]{2,1,0:T(8,128)}, f32[4,64,512]{2,1,0:T(8,128)}) fusion(f32[8,68,512]{2,1,0:T(8,128)S(1)} %get-tuple-element.34, f32[4,64,511]{2,1,0:T(8,128)S(1)} %get-tuple-element.81, f32[8,68,512]{2,1,0:T(8,128)S(1)} %get-tuple-element.39, f32[4,64,511]{2,1,0:T(8,128)S(1)} %get-tuple-element.89, ...), kind=kLoop, calls=%fused_computation.132 | loop fusion | flops 2357248 | bytes 8918016 | tf_op jit(solution)/shard_map/reduce_sum | solution.py:437
  50.4 0.0 copy-start.6
  50.4 0.6 copy-done.6
  51.0 20.9 %column_cg.1 = (f32[5,2,8,512]{3,2,1,0:T(8,128)}, f32[4,128]{1,0:T(4,128)}) custom-call(f32[9,4,512]{2,1,0:T(4,128)} %copy-done.6, s32[1,512]{1,0:T(1,128)} %bitcast.39), custom_call_target="tpu_custom_call" | custom-call | tf_op jit(solution)/shard_map/column_cg/pallas_call | solution.py:155
  71.9 0.0 copy-start.8
  71.9 5.3 %subtract_gradient.1 = f32[2,4,64,512]{3,2,1,0:T(8,128)} custom-call(f32[5,2,8,512]{3,2,1,0:T(8,128)} %get-tuple-element.16.gs, f32[2,4,64,512]{3,2,1,0:T(8,128)} %copy-done, f32[4,64,512]{2,1,0:T(8,128)} %get-tuple-element.33.refs_0_, f32[4,64,512]{2,1,0:T(8,128)} %get-tuple-element.31.refs_1_, f32[4,64,512]{2,1,0:T(8,128)} %get-tuple-element.41.refs_2_, ...), custom_call_target="tpu_custom_call" | custom-call | tf_op jit(solution)/shard_map/subtract_gradient/pallas_call | solution.py:199
  77.2 0.0 copy-done.8
  77.2 0.6 copy.14
  (41 shorter events, 0.5 us)
Async XLA Ops:
  18.9 3.1 %copy-start.4 = (f32[2,2,2,64,512]{4,3,2,1,0:T(8,128)S(1)}, f32[2,2,2,64,512]{4,3,2,1,0:T(8,128)}, u32[]{:S(2)}) copy-start(f32[2,2,2,64,512]{4,3,2,1,0:T(8,128)} %get-tuple-element.13) | copy-start | bytes 3145732
  20.0 2.1 %copy-start.5 = (f32[2,28,512]{2,1,0:T(8,128)S(1)}, f32[2,28,512]{2,1,0:T(8,128)}, u32[]{:S(2)}) copy-start(f32[2,28,512]{2,1,0:T(8,128)} %get-tuple-element.12) | copy-start | bytes 344068
  20.1 0.7 copy-start.7
  20.7 1.5 %copy-start.2 = (f32[2,4,64,512]{3,2,1,0:T(8,128)S(1)}, f32[2,4,64,512]{3,2,1,0:T(8,128)}, u32[]{:S(2)}) copy-start(f32[2,4,64,512]{3,2,1,0:T(8,128)} %forc.1) | copy-start | bytes 3145732
  20.7 1.5 %slice-start = ((f32[2,4,2,512]{3,2,1,0:T(2,128)}), f32[2,2,2,512]{3,2,1,0:T(2,128)S(1)}, s32[]{:S(2)}) async-start(f32[2,4,2,512]{3,2,1,0:T(2,128)} %copy-done.7), calls=%async_computation | async-start | bytes 32768 | tf_op jit(solution)/shard_map/slice | solution.py:359
  24.9 1.4 %copy-start.3 = (f32[4,64,512]{2,1,0:T(8,128)S(1)}, f32[4,64,512]{2,1,0:T(8,128)}, u32[]{:S(2)}) copy-start(f32[4,64,512]{2,1,0:T(8,128)} %visc.1) | copy-start | bytes 1572868
  32.6 1.9 %copy-start.1 = (f32[2,8,68,512]{3,2,1,0:T(8,128)S(1)}, f32[2,8,68,512]{3,2,1,0:T(8,128)}, u32[]{:S(2)}) copy-start(f32[2,8,68,512]{3,2,1,0:T(8,128)} %maximum_maximum_fusion) | copy-start | bytes 6684676
  44.4 1.0 %copy-start = (f32[2,4,64,512]{3,2,1,0:T(8,128)}, f32[2,4,64,512]{3,2,1,0:T(8,128)S(1)}, u32[]{:S(2)}) copy-start(f32[2,4,64,512]{3,2,1,0:T(8,128)S(1)} %fusion.12.free) | copy-start | bytes 3145732
  50.4 0.6 copy-start.6
  71.9 5.3 %copy-start.8 = (f32[4,128]{1,0:T(4,128)S(1)}, f32[4,128]{1,0:T(4,128)}, u32[]{:S(2)}) copy-start(f32[4,128]{1,0:T(4,128)} %get-tuple-element.107) | copy-start | bytes 6148
